TPU v7x, 128 devices: a whole 4x4x4 slice. The times are simulated.
128 devices in a mesh: bins: 64 (over x, y, z), diag: 2 (over core).
Axes of the slice: x: 4, y: 4, z: 4, core: 2. Of those that a mesh axis runs over, the one named last changes fastest.
Arguments:
- held_tiles: float32 [128, 2, 1024, 1024], P('bins', 'diag'), may hold values from 0.01 to 20, as said below
- placed: int32 [128], P('bins'), may hold values from 0 to 1, as said below
- bin_mask: int32 [131072], P('bins'), may hold values 0 or 1
- bias: float32 [131072], P('bins'), may hold values from 0.5 to 2
Outputs:
- balanced: float32 [128, 2, 1024, 1024], P('bins', 'diag')
- bias_out: float32 [131072], P('bins')
Inputs may be any that keep to these rules, and one draw needn't show every extreme that they name: placed[q] equals placed[(q + 64) mod 128]; placed[q] is 1 where q is a multiple of 2. `held_tiles`: entries are positive.
All inputs are finite; a program needn't handle non-finite values. No bound on the sum of `bin_mask` on one device may be relied on, other than what follows from the above.
Results may differ from a plain program's by a relative error of at most 0.00012.
Values sent between devices are 32-bit elements; how exact they have to be, the bound alone decides.
No kernel may reach another device: no remote copies, remote signals or barrier semaphores. Data moves between devices by JAX's collectives and lax.ppermute only.
A program may use at most 128 MiB of HBM per device.

v0:
```python
import jax
import jax.numpy as jnp
from jax import lax
from jax.sharding import PartitionSpec as P

ITERS = 2


def passed_along(value, axis, steps):
    count = lax.axis_size(axis)
    first, last = (max(0, -steps), min(count, count - steps))
    return lax.ppermute(value, axis, [(source, source + steps) for source in range(first, last)])


def partner(value, axis, stride):
    mask = 2**stride
    pairs = [(source, source ^ mask) for source in range(lax.axis_size(axis))]
    return lax.ppermute(value, axis, pairs)


def sent_to_all(shard, axis):
    peers = lax.axis_size(axis)
    return lax.all_to_all(
        jnp.broadcast_to(shard[None], (peers, *shard.shape)), axis, 0, 0, tiled=True
    )


def of_everyone(shard, axis):
    everything = sent_to_all(shard, axis)
    return jnp.sum(everything, axis=0)


def in_one(arrays, axis):
    ends = [0]
    for a in arrays:
        ends.append(ends[-1] + a.size)
    total = of_everyone(jnp.concatenate([a.ravel() for a in arrays]), axis)
    return tuple((total[b:e].reshape(a.shape) for a, b, e in zip(arrays, ends, ends[1:])))


def local(held_tiles, placed, bin_mask, bias):
    rows_dev = held_tiles.shape[0]
    tile_size = held_tiles.shape[2]
    offset_index = lax.axis_index("diag")
    on_diagonal = offset_index == 0
    top_bit = lax.axis_size("bins").bit_length() - 2
    held_local = held_tiles[:, 0]
    placed_flags = (placed == 1)[:, None]
    live_home = bin_mask.astype(jnp.float32).reshape(rows_dev, tile_size)
    first_next = passed_along(live_home[0:1], "bins", -1)
    live_next = jnp.concatenate([live_home[1:], first_next], axis=0)
    lines = jnp.arange(tile_size, dtype=jnp.int32)
    upper_mask = (lines[:, None] <= lines[None, :]).astype(jnp.float32)
    triangle = jnp.where(on_diagonal, upper_mask, 1.0)
    partner_tiles = partner(held_local, "bins", top_bit)
    home_tiles = jnp.where(placed_flags[:, :, None], partner_tiles, held_local)
    live_cols = jnp.where(on_diagonal, live_home, live_next)
    scaled = home_tiles * triangle * live_home[:, :, None] * live_cols[:, None, :]
    bias_now = bias.reshape(rows_dev, tile_size)
    for repeat in range(ITERS):
        row_part = jnp.sum(scaled, axis=2)
        diagonal_terms = jnp.diagonal(scaled, axis1=1, axis2=2)
        col_part = jnp.sum(scaled, axis=1) - jnp.where(on_diagonal, diagonal_terms, 0.0)
        edge_cols = passed_along(col_part[-1:], "bins", 1)
        moved_cols = jnp.concatenate([edge_cols, col_part[:-1]], axis=0)
        contrib = row_part + jnp.where(on_diagonal, col_part, moved_cols)
        sums = of_everyone(contrib, "diag")
        masked_total, live_count = in_one((jnp.sum(sums * live_home), jnp.sum(live_home)), "bins")
        mean_sum = masked_total / live_count
        factor = jnp.where(live_home > 0, sums / mean_sum, 1.0)
        bias_now = bias_now * factor
        inverse = 1.0 / factor
        inverse_first = passed_along(inverse[0:1], "bins", -1)
        inverse_next = jnp.concatenate([inverse[1:], inverse_first], axis=0)
        inverse_cols = jnp.where(on_diagonal, inverse, inverse_next)
        scaled = scaled * inverse[:, :, None] * inverse_cols[:, None, :]
    return (scaled[:, None], bias_now.reshape(rows_dev * tile_size))


def solution(mesh):
    placed = (P("bins", "diag", None, None), P("bins"), P("bins"), P("bins"))
    return jax.shard_map(
        local,
        mesh=mesh,
        in_specs=placed,
        out_specs=(P("bins", "diag", None, None), P("bins")),
        check_vma=False,
    )
```

profile of v0, /device:TPU:0, one launch (start us, length us, event | category | flops | bytes accessed | tf_op | source)
XLA Modules:
  0.0 343.9 jit_solution(13220354077775837842)
XLA Ops:
  0.6 15.4 %copy.55 = f32[2,1,1024,1024]{3,0,2,1:T(2,128)} copy(f32[2,1,1024,1024]{3,2,1,0:T(8,128)} %param.4) | data formatting | bytes 16777216 | tf_op args[0]
  16.0 3.1 collective-permute-start
  19.1 1.3 collective-permute-start.1
  20.4 2.5 convert_select_fusion
  23.2 1.4 collective-permute-done.1
  24.7 175.2 %collective-permute-done = f32[2,1024,1024]{2,0,1:T(2,128)} collective-permute-done((f32[2,1024,1024]{2,0,1:T(2,128)}, f32[2,1024,1024]{2,0,1:T(2,128)}, u32[]{:S(2)}, u32[]{:S(2)}) %collective-permute-start) | collective-permute-done | bytes 8388640 | tf_op jit(solution)/shard_map/ppermute | solution.py:18
  199.9 19.2 %fusion.11 = (f32[2,1024]{1,0:T(2,128)S(1)}, f32[2,1024]{0,1:T(8,128)S(1)}, f32[2,1024,1024]{2,0,1:T(2,128)}) fusion(f32[2,1024]{1,0:T(2,128)S(1)} %maximum_select_fusion, f32[2,1024]{0,1:T(8,128)S(1)} %copy.31, f32[1024,1024]{1,0:T(8,128)} %convert_select_fusion, f32[2,1024,1024]{2,0,1:T(2,128)} %collective-permute-done, f32[2,1,1024,1024]{3,2,1,0:T(8,128)} %param.4, ...), kind=kLoop, calls=%fused_computation.38 | loop fusion | flops 12578816 | bytes 29392898 | tf_op jit(solution)/shard_map/reduce_sum | solution.py:63
  219.1 13.3 %gather_fusion = f32[1024,2]{0,1:T(2,128)S(1)} fusion(f32[2,1024,1024]{2,0,1:T(2,128)} %get-tuple-element.19, s32[1024]{0:T(1024)S(1)} %bitcast.42), kind=kCustom, calls=%fused_computation | custom fusion | bytes 24576 | tf_op jit(solution)/shard_map/jit(diagonal)/gather | solution.py:62
  232.4 4.0 %collective-permute-start.2 = (f32[1,1024]{1,0:T(1,128)S(1)}, f32[1,1024]{1,0:T(1,128)S(1)}, u32[]{:S(2)}, u32[]{:S(2)}) collective-permute-start(f32[1,1024]{1,0:T(1,128)S(1)} %get-tuple-element.26), channel_id=1, source_target_pairs={{0,2},{2,4},{4,6},{6,8},{8,10},{10,12},{12,14},{14,16},{16,18},{18... | collective-permute-start | bytes 12296 | tf_op jit(solution)/shard_map/ppermute | solution.py:12
  237.8 3.7 %all_to_all.22 = f32[2,2,1024]{2,1,0:T(2,128)S(1)} all-to-all(f32[2,2,1024]{2,1,0:T(2,128)S(1)} %broadcast_in_dim.36), channel_id=1, replica_groups=mesh['bins'=64,'diag'=2] {'diag'}, dimensions={0} | all-to-all | bytes 32768 | tf_op jit(solution)/shard_map/all_to_all | solution.py:23
  242.3 1.4 pad_maximum_fusion
  243.7 21.1 %all_to_all.23 = f32[64,1,2]{2,1,0:T(1,128)S(1)} all-to-all(f32[64,1,2]{2,1,0:T(1,128)S(1)} %broadcast_in_dim.37), channel_id=1, replica_groups=mesh['bins'=64,'diag'=2] {'bins'}, dimensions={0} | all-to-all | bytes 1024 | tf_op jit(solution)/shard_map/all_to_all | solution.py:23
  266.8 1.3 collective-permute-start.3
  268.3 4.0 %collective-permute-done.3 = f32[1,1024]{1,0:T(1,128)S(1)} collective-permute-done((f32[1,1024]{1,0:T(1,128)S(1)}, f32[1,1024]{1,0:T(1,128)S(1)}, u32[]{:S(2)}, u32[]{:S(2)}) %collective-permute-start.3) | collective-permute-done | bytes 4128 | tf_op jit(solution)/shard_map/ppermute | solution.py:12
  272.3 9.7 %fusion.10 = (f32[2,1024]{1,0:T(2,128)S(1)}, f32[2,1024]{0,1:T(8,128)S(1)}, f32[2,1024,1024]{2,0,1:T(2,128)}) fusion(f32[2,1024]{1,0:T(2,128)S(1)} %maximum_select_fusion.2, f32[2,1024,1024]{2,0,1:T(2,128)} %get-tuple-element.19, f32[2,1024]{0,1:T(8,128)S(1)} %copy.34), kind=kLoop, calls=%fused_computation.37 | loop fusion | flops 8384512 | bytes 16809984 | tf_op jit(solution)/shard_map/reduce_sum | solution.py:63
  282.0 13.3 %gather_fusion.1 = f32[1024,2]{0,1:T(2,128)S(1)} fusion(f32[2,1024,1024]{2,0,1:T(2,128)} %get-tuple-element.18, s32[1024]{0:T(1024)S(1)} %bitcast.43), kind=kCustom, calls=%fused_computation.1 | custom fusion | bytes 24576 | tf_op jit(solution)/shard_map/jit(diagonal)/gather | solution.py:62
  295.3 2.5 collective-permute-start.4
  299.1 3.7 %all_to_all.24 = f32[2,2,1024]{2,1,0:T(2,128)S(1)} all-to-all(f32[2,2,1024]{2,1,0:T(2,128)S(1)} %broadcast_in_dim.38), channel_id=1, replica_groups=mesh['bins'=64,'diag'=2] {'diag'}, dimensions={0} | all-to-all | bytes 32768 | tf_op jit(solution)/shard_map/all_to_all | solution.py:23
  303.5 1.3 pad_maximum_fusion.1
  304.8 19.9 %all_to_all.25 = f32[64,1,2]{2,1,0:T(1,128)S(1)} all-to-all(f32[64,1,2]{2,1,0:T(1,128)S(1)} %broadcast_in_dim.39), channel_id=1, replica_groups=mesh['bins'=64,'diag'=2] {'bins'}, dimensions={0} | all-to-all | bytes 1024 | tf_op jit(solution)/shard_map/all_to_all | solution.py:23
  326.7 1.5 collective-permute-start.5
  329.0 3.2 collective-permute-done.5
  332.2 5.7 %multiply_bitcast_fusion = f32[2,1,1024,1024]{3,0,2,1:T(2,128)S(1)} fusion(f32[2,1024,1024]{2,0,1:T(2,128)} %get-tuple-element.18, f32[2,1024]{1,0:T(2,128)S(1)} %maximum_select_fusion.4, f32[2,1024]{0,1:T(8,128)S(1)} %copy.37), kind=kLoop, calls=%fused_computation.3 | loop fusion | flops 4194304 | bytes 16793600 | tf_op jit(solution)/shard_map/broadcast_in_dim | solution.py:77
  337.9 6.0 %copy.38 = f32[2,1,1024,1024]{3,2,1,0:T(8,128)} copy(f32[2,1,1024,1024]{3,0,2,1:T(2,128)S(1)} %multiply_bitcast_fusion) | data formatting | bytes 16777216
  (44 shorter events, 6.8 us)
Async XLA Ops:
  0.6 18.5 %copy-start = (s32[2048]{0:T(1024)S(1)}, s32[2048]{0:T(1024)}, u32[]{:S(2)}) copy-start(s32[2048]{0:T(1024)} %param.6) | copy-start | bytes 24580
  0.6 22.3 %copy-start.2 = (s32[2]{0:T(128)S(1)}, s32[2]{0:T(128)}, u32[]{:S(2)}) copy-start(s32[2]{0:T(128)} %param.5) | copy-start | bytes 28
  16.0 183.9 %collective-permute-start = (f32[2,1024,1024]{2,0,1:T(2,128)}, f32[2,1024,1024]{2,0,1:T(2,128)}, u32[]{:S(2)}, u32[]{:S(2)}) collective-permute-start(f32[2,1024,1024]{2,0,1:T(2,128)} %bitcast.41), channel_id=1, source_target_pairs={{0,64},{2,66},{4,68},{6,70},{8,72},{10,74},{12,76},{14,78},{16,80}... | collective-permute-start | bytes 25165832 | tf_op jit(solution)/shard_map/ppermute | solution.py:18
  19.1 5.5 %collective-permute-start.1 = (f32[1,1024]{1,0:T(1,128)S(1)}, f32[1,1024]{1,0:T(1,128)S(1)}, u32[]{:S(2)}, u32[]{:S(2)}) collective-permute-start(f32[1,1024]{1,0:T(1,128)S(1)} %bitcast.49), channel_id=1, source_target_pairs={{2,0},{4,2},{6,4},{8,6},{10,8},{12,10},{14,12},{16,14},{18,16},{20... | collective-permute-start | bytes 12296 | tf_op jit(solution)/shard_map/ppermute | solution.py:12
  232.4 5.4 %collective-permute-start.2 = (f32[1,1024]{1,0:T(1,128)S(1)}, f32[1,1024]{1,0:T(1,128)S(1)}, u32[]{:S(2)}, u32[]{:S(2)}) collective-permute-start(f32[1,1024]{1,0:T(1,128)S(1)} %get-tuple-element.26), channel_id=1, source_target_pairs={{0,2},{2,4},{4,6},{6,8},{8,10},{10,12},{12,14},{14,16},{16,18},{18... | collective-permute-start | bytes 12296 | tf_op jit(solution)/shard_map/ppermute | solution.py:12
  266.8 5.5 %collective-permute-start.3 = (f32[1,1024]{1,0:T(1,128)S(1)}, f32[1,1024]{1,0:T(1,128)S(1)}, u32[]{:S(2)}, u32[]{:S(2)}) collective-permute-start(f32[1,1024]{1,0:T(1,128)S(1)} %get-tuple-element.25), channel_id=1, source_target_pairs={{2,0},{4,2},{6,4},{8,6},{10,8},{12,10},{14,12},{16,14},{18,16},{20... | collective-permute-start | bytes 12296 | tf_op jit(solution)/shard_map/ppermute | solution.py:12
  272.3 55.9 %copy-start.1 = (f32[2048]{0:T(1024)S(1)}, f32[2048]{0:T(1024)}, u32[]{:S(2)}) copy-start(f32[2048]{0:T(1024)} %param.7) | copy-start | bytes 24580
  295.3 3.8 %collective-permute-start.4 = (f32[1,1024]{1,0:T(1,128)S(1)}, f32[1,1024]{1,0:T(1,128)S(1)}, u32[]{:S(2)}, u32[]{:S(2)}) collective-permute-start(f32[1,1024]{1,0:T(1,128)S(1)} %get-tuple-element.22), channel_id=1, source_target_pairs={{0,2},{2,4},{4,6},{6,8},{8,10},{10,12},{12,14},{14,16},{16,18},{18... | collective-permute-start | bytes 12296 | tf_op jit(solution)/shard_map/ppermute | solution.py:12
  326.7 5.5 %collective-permute-start.5 = (f32[1,1024]{1,0:T(1,128)S(1)}, f32[1,1024]{1,0:T(1,128)S(1)}, u32[]{:S(2)}, u32[]{:S(2)}) collective-permute-start(f32[1,1024]{1,0:T(1,128)S(1)} %get-tuple-element.21), channel_id=1, source_target_pairs={{2,0},{4,2},{6,4},{8,6},{10,8},{12,10},{14,12},{16,14},{18,16},{20... | collective-permute-start | bytes 12296 | tf_op jit(solution)/shard_map/ppermute | solution.py:12
where the time goes:
time: 345 us; the launch traced here: 344 us
  waiting for transfers between devices  186 us (54%)
  local copies, waits for them, and re-layouts  50.3 us (15%)
  blocking collectives  48.5 us (14%)
  other arithmetic  42 us (12%)
  starting transfers between devices  13.7 us (4%)
    ppermute x1, waiting for transfers between devices, partner(): return lax.ppermute(value, axis, pairs)  175 us
    all_to_all x4, blocking collectives, sent_to_all(): lax.all_to_all(jnp.broadcast_to(shard[None], (peers, *shard.shape)), axis...  48.5 us
    reduce_sum x2, other arithmetic, local(): jnp.sum(scaled, axis=1) - jnp.where(on_diagonal, diagonal_terms, 0.0)  28.9 us
    gather x2, local copies, waits for them, and re-layouts, local(): diagonal_terms = jnp.diagonal(scaled, axis1=1, axis2=2)  26.6 us
    unnamed x8, local copies, waits for them, and re-layouts  21.4 us
    ppermute x5, waiting for transfers between devices, passed_along(): lax.ppermute(value, axis, [(source, source + steps) for source in range(f...  10.8 us
    ppermute x5, starting transfers between devices, passed_along(): lax.ppermute(value, axis, [(source, source + steps) for source in range(f...  10.6 us
  transfers between devices with their start and end apart: 6, of which 6 were waited for; matrix products, arithmetic and copies ran while one was open for 1% of the time, Pallas kernels for 0%

commit v1 on v0

v1 whole, which is shorter than its diff:
```python
import functools

import jax
import jax.numpy as jnp
from jax import lax
from jax.experimental import pallas as pl
from jax.experimental.pallas import tpu as pltpu
from jax.sharding import PartitionSpec as P

AXES = ("bins", "diag")
F32 = jnp.float32
LANE = 128
VMEM_LIMIT = 48 * 1024 * 1024


def iotas():
    rows = lax.broadcasted_iota(jnp.int32, (LANE, LANE), 0)
    cols = lax.broadcasted_iota(jnp.int32, (LANE, LANE), 1)
    return rows, cols


def as_column(line):
    return jnp.broadcast_to(line, (LANE, LANE)).T


def lanes(k):
    return pl.ds(k * LANE, LANE)


def moves(n_bins):
    half = n_bins // 2

    def send(value, pairs):
        return lax.ppermute(value, AXES, pairs)

    chips = range(n_bins)
    down = [(2 * d, 2 * d + 1) for d in chips]
    up = [(2 * d + 1, 2 * d) for d in chips]
    across = [(2 * d, 2 * ((d + half) % n_bins)) for d in chips]
    tiles = [(2 * d + 1, 2 * ((d + half) % n_bins) + 1) for d in chips]
    relayed = [(2 * d + 1, 2 * ((d + half) % n_bins)) for d in chips]
    before = [(2 * d + 2, 2 * d) for d in range(n_bins - 1)]
    after = [(2 * d, 2 * d + 2) for d in range(n_bins - 1)]
    names = dict(down=down, up=up, across=across, tiles=tiles, relayed=relayed, before=before, after=after)
    out = {name: functools.partial(send, pairs=pairs) for name, pairs in names.items()}

    def total(value):
        step = 1
        while step < n_bins:
            value = value + send(value, [(2 * d, 2 * (d ^ step)) for d in chips])
            step *= 2
        return value

    out["total"] = total
    return out


def pack_place(s):
    t = jnp.where((s >= 1) & (s <= 4), 0, 1)
    k = jnp.where(s == 0, 0, jnp.where(s <= 4, s - 1, s - 4))
    return t, k


def pack_kernel(near_ref, far_ref, most_ref, last_ref, dv_ref):
    s = pl.program_id(0)
    _, k_now = pack_place(s)
    rows, cols = iotas()

    def fill(to_ref, k):
        far = far_ref[0, 0, :, lanes(7 - k)]
        near = near_ref[0, 0, :, lanes(k)]
        to_ref[:, lanes(k)] = jnp.where(cols >= rows, near, far.T)
        dv_ref[0] = jnp.sum(jnp.where(cols == rows, far, 0.0), axis=0, keepdims=True)
        for j in range(k + 1, 8):
            to_ref[:, lanes(j)] = near_ref[0, 0, :, lanes(j)]
        for j in range(k):
            to_ref[:, lanes(j)] = far_ref[0, 0, :, lanes(8 - k + j)]

    @pl.when(s == 0)
    def _():
        fill(last_ref, 0)

    for k in range(4):
        @pl.when((s > 0) & (k_now == k))
        def _():
            fill(most_ref, k)


def pack(held):
    block = (1, 1, LANE, 1024)
    return pl.pallas_call(
        pack_kernel,
        grid=(8,),
        in_specs=[
            pl.BlockSpec(block, lambda s: (pack_place(s)[0], 0, pack_place(s)[1], 0)),
            pl.BlockSpec(block, lambda s: (pack_place(s)[0], 0, 7 - pack_place(s)[1], 0)),
        ],
        out_specs=[
            pl.BlockSpec((LANE, 1024), lambda s: (jnp.maximum(s - 1, 0), 0)),
            pl.BlockSpec((LANE, 1024), lambda s: (0, 0)),
            pl.BlockSpec((1, 1, LANE), lambda s: (s, 0, 0)),
        ],
        out_shape=[
            jax.ShapeDtypeStruct((7 * LANE, 1024), F32),
            jax.ShapeDtypeStruct((LANE, 1024), F32),
            jax.ShapeDtypeStruct((8, 1, LANE), F32),
        ],
        compiler_params=pltpu.CompilerParams(vmem_limit_bytes=VMEM_LIMIT),
        cost_estimate=pl.CostEstimate(flops=1 << 20, bytes_accessed=12 << 20, transcendentals=0),
        name="pack_triangles",
    )(held, held)


ROWS = 256


def sums_kernel(sc_ref, x_ref, a_ref, b_ref, row_ref, col_ref):
    i = pl.program_id(1)
    rows, cols = iotas()
    ahead = cols - rows
    on_diagonal = sc_ref[0] == 1
    least = jnp.where(on_diagonal, 0, -4096)
    least_col = jnp.where(on_diagonal, 1, -4096)

    @pl.when(i == 0)
    def _():
        col_ref[...] = jnp.zeros_like(col_ref)

    for r in range(ROWS // LANE):
        a_line = a_ref[0, :, lanes(r)]
        a_col = as_column(a_line)
        start = i * ROWS + r * LANE
        across = jnp.zeros((LANE, LANE), F32)
        for k in range(8):
            x = x_ref[0, 0, pl.ds(r * LANE, LANE), lanes(k)]
            shift = start - k * LANE
            b_line = b_ref[0, :, lanes(k)]
            across += jnp.where(ahead >= least + shift, x, 0.0) * b_line
            down = jnp.where(ahead >= least_col + shift, x, 0.0) * a_col
            col_ref[0, :, lanes(k)] += jnp.sum(down, axis=0, keepdims=True)
        row_ref[0, :, lanes(r)] = jnp.sum(across.T, axis=0, keepdims=True) * a_line

    @pl.when(i == pl.num_programs(1) - 1)
    def _():
        col_ref[...] *= b_ref[...]


def weighted_sums(scalars, held, row_w, col_w):
    steps = 1024 // ROWS
    shape = jax.ShapeDtypeStruct((2, 1, 1024), F32)
    row_part, col_part = pl.pallas_call(
        sums_kernel,
        grid_spec=pltpu.PrefetchScalarGridSpec(
            num_scalar_prefetch=1,
            grid=(2, steps),
            in_specs=[
                pl.BlockSpec((1, 1, ROWS, 1024), lambda t, i, sc: (t, 0, i, 0)),
                pl.BlockSpec((1, 1, ROWS), lambda t, i, sc: (t, 0, i)),
                pl.BlockSpec((1, 1, 1024), lambda t, i, sc: (t, 0, 0)),
            ],
            out_specs=[
                pl.BlockSpec((1, 1, ROWS), lambda t, i, sc: (t, 0, i)),
                pl.BlockSpec((1, 1, 1024), lambda t, i, sc: (t, 0, 0)),
            ],
        ),
        out_shape=[shape, shape],
        compiler_params=pltpu.CompilerParams(vmem_limit_bytes=VMEM_LIMIT),
        cost_estimate=pl.CostEstimate(flops=8 << 20, bytes_accessed=8 << 20, transcendentals=0),
        name="weighted_sums",
    )(scalars, held, row_w.reshape(2, 1, 1024), col_w.reshape(2, 1, 1024))
    return row_part.reshape(2, 1024), col_part.reshape(2, 1024)


def most_place(i):
    t = jnp.where(i < 8, 0, 1)
    k = jnp.where(i < 8, i // 2, (i - 8) // 2 + 1)
    return t, k, jnp.where(i % 2 == 0, k, 7 - k)


def last_place(i):
    return 1, 0, jnp.where(i == 0, 0, 7)


def balance_kernel(place, sc_ref, got_ref, held_ref, pk_ref, dv_ref, wr_ref, wc_ref, *rest):
    out_ref = rest[-1]
    t, k_now, b = place(pl.program_id(0))
    rows, cols = iotas()
    on_diagonal = sc_ref[0] == 1
    moved = sc_ref[1 + t] == 1
    w_col = as_column(wr_ref[0])

    def put(j, x):
        out_ref[0, 0, :, lanes(j)] = x * w_col * wc_ref[0, :, lanes(j)]

    @pl.when(moved & jnp.logical_not(on_diagonal))
    def _():
        for j in range(8):
            put(j, got_ref[0, 0, :, lanes(j)])

    @pl.when(jnp.logical_not(moved))
    def _():
        least = jnp.where(on_diagonal, 0, -4096) + b * LANE
        for j in range(8):
            put(j, jnp.where(cols - rows >= least - j * LANE, held_ref[0, 0, :, lanes(j)], 0.0))

    for k in range(4):
        @pl.when(moved & on_diagonal & (k_now == k) & (b == k))
        def _():
            for j in range(k):
                out_ref[0, 0, :, lanes(j)] = jnp.zeros((LANE, LANE), F32)
            put(k, jnp.where(cols >= rows, pk_ref[:, lanes(k)], 0.0))
            for j in range(k + 1, 8):
                put(j, pk_ref[:, lanes(j)])

        @pl.when(moved & on_diagonal & (k_now == k) & (b == 7 - k))
        def _():
            for j in range(7 - k):
                out_ref[0, 0, :, lanes(j)] = jnp.zeros((LANE, LANE), F32)
            far = pk_ref[:, lanes(k)].T
            put(7 - k, jnp.where(cols > rows, far, jnp.where(cols == rows, dv_ref[0], 0.0)))
            for j in range(k):
                put(8 - k + j, pk_ref[:, lanes(j)])


def balance(place, steps, packed_row, scalars, got, held, packed, dv, wr, wc, into=None):
    tile = (1, 1, LANE, 1024)

    def got_at(i, sc):
        t, _, b = place(i)
        use = (sc[0] == 0) & (sc[1 + t] == 1)
        return (jnp.where(use, t, 0), 0, jnp.where(use, b, 0), 0)

    def held_at(i, sc):
        t, _, b = place(i)
        use = sc[1 + t] == 0
        return (jnp.where(use, t, 0), 0, jnp.where(use, b, 0), 0)

    def packed_at(i, sc):
        t, k, _ = place(i)
        use = (sc[0] == 1) & (sc[1 + t] == 1)
        return (jnp.where(use, packed_row(t, k), 0), 0)

    def dv_at(i, sc):
        t, k, _ = place(i)
        return (jnp.where(t == 0, 1 + k, jnp.where(k == 0, 0, 4 + k)), 0, 0)

    in_specs = [
        pl.BlockSpec(tile, got_at),
        pl.BlockSpec(tile, held_at),
        pl.BlockSpec((LANE, 1024), packed_at),
        pl.BlockSpec((1, 1, LANE), dv_at),
        pl.BlockSpec((1, 1, LANE), lambda i, sc: (place(i)[0] * 8 + place(i)[2], 0, 0)),
        pl.BlockSpec((1, 1, 1024), lambda i, sc: (place(i)[0], 0, 0)),
    ]
    args = [scalars, got, held, packed, dv, wr, wc]
    aliases = {}
    if into is not None:
        in_specs.append(pl.BlockSpec(memory_space=pl.ANY))
        args.append(into)
        aliases = {len(args) - 1: 0}
    return pl.pallas_call(
        functools.partial(balance_kernel, place),
        grid_spec=pltpu.PrefetchScalarGridSpec(
            num_scalar_prefetch=1,
            grid=(steps,),
            in_specs=in_specs,
            out_specs=pl.BlockSpec(tile, lambda i, sc: (place(i)[0], 0, place(i)[2], 0)),
        ),
        out_shape=jax.ShapeDtypeStruct(held.shape, F32),
        input_output_aliases=aliases,
        compiler_params=pltpu.CompilerParams(vmem_limit_bytes=VMEM_LIMIT),
        cost_estimate=pl.CostEstimate(flops=steps << 18, bytes_accessed=steps << 20, transcendentals=0),
        name="balance_most" if into is None else "balance_last",
    )(*args)


def local(held_tiles, placed, bin_mask, bias):
    move = moves(lax.axis_size("bins"))
    on_diagonal = lax.axis_index("diag") == 0
    live = bin_mask.astype(F32).reshape(2, 1024)
    alive = live > 0
    flags = (placed == 1)[:, None]
    scalars = jnp.concatenate([on_diagonal.astype(jnp.int32)[None], (placed == 1).astype(jnp.int32)])

    got = move["tiles"](held_tiles)
    most, last, dv = pack(held_tiles)
    most = move["relayed"](move["down"](most))
    last = move["relayed"](move["down"](last))

    def as_stored(lines):
        own = jnp.concatenate([lines, move["before"](lines[0:1])], axis=0)
        theirs = move["across"](own)
        rows = jnp.where(flags, theirs[:2], own[:2])
        cols = jnp.where(flags, theirs[1:], own[1:])
        passed = move["down"](jnp.concatenate([rows, cols], axis=0))
        return jnp.where(on_diagonal, rows, passed[:2]), jnp.where(on_diagonal, rows, passed[2:])

    def home_sums(row_w, col_w):
        row_part, col_part = weighted_sums(scalars, held_tiles, row_w, col_w)
        off = move["up"](jnp.concatenate([row_part, col_part], axis=0))
        stored = jnp.concatenate([row_part + col_part + off[:2], off[2:]], axis=0)
        parts = jnp.where(jnp.concatenate([flags, flags], axis=0), move["across"](stored), stored)
        return parts[:2] + jnp.concatenate([move["after"](parts[3:4]), parts[2:3]], axis=0)

    sums_1 = home_sums(*as_stored(live))
    inverse_1 = jnp.where(alive, 1.0 / sums_1, 0.0)
    sums_2 = home_sums(*as_stored(inverse_1))
    inverse = jnp.where(alive, inverse_1 / sums_2, 0.0)
    following = move["before"](inverse[0:1])
    both = [jnp.sum(sums_1 * live), jnp.sum(sums_2 * live), jnp.sum(live)]
    totals = move["total"](jnp.pad(jnp.stack(both)[None], ((0, 0), (0, LANE - 3))))
    mean_1, mean_2 = totals[0, 0] / totals[0, 2], totals[0, 1] / totals[0, 2]
    lines = jnp.concatenate([inverse, following], axis=0)
    weights = jnp.where(lines > 0, lines * (mean_1 * mean_2), 0.0)
    factor = jnp.where(alive, (sums_1 / mean_1) * (sums_2 / mean_2), 1.0)
    result = jnp.concatenate([weights, factor], axis=0)
    result = jnp.where(on_diagonal, result, move["down"](result))
    bias_out = bias.reshape(2, 1024) * result[3:]
    wr = result[:2].reshape(16, 1, LANE)
    wc = jnp.where(on_diagonal, result[:2], result[1:3]).reshape(2, 1, 1024)
    dv = move["across"](dv)

    got, most, wr, wc, dv = lax.optimization_barrier((got, most, wr, wc, dv))
    out = balance(most_place, 14, lambda t, k: k + 3 * t, scalars, got, held_tiles, most, dv, wr, wc)
    out, last = lax.optimization_barrier((out, last))
    out = balance(last_place, 2, lambda t, k: 0, scalars, got, held_tiles, last, dv, wr, wc, into=out)
    return out, bias_out.reshape(2048)


def solution(mesh):
    placed = (P("bins", "diag", None, None), P("bins"), P("bins"), P("bins"))
    return jax.shard_map(
        local,
        mesh=mesh,
        in_specs=placed,
        out_specs=(P("bins", "diag", None, None), P("bins")),
        check_vma=False,
    )
```

time: 345 us -> 180 us (0.52)
  waiting for transfers between devices: 186 us -> 34.5 us
  starting transfers between devices: 13.7 us -> 98.3 us
  local copies, waits for them, and re-layouts: 50.3 us -> 1.41 us
  blocking collectives: 48.5 us -> 0 us
  other arithmetic: 42 us -> 3.96 us
  Pallas kernels: 0 us -> 36.7 us
    ppermute x6 -> x26, waiting for transfers between devices: 186 us -> 34.5 us  [send(): return lax.ppermute(value, AXES, pairs)]
    ppermute x6 -> x26, starting transfers between devices: 13.7 us -> 98.3 us  [send(): return lax.ppermute(value, AXES, pairs)]
    all_to_all x4 -> x0, blocking collectives: 48.5 us -> none  [sent_to_all(): lax.all_to_all(jnp.broadcast_to(shard[None], (peers, *shard.shape)), axis...]
    pallas_call x0 -> x5, Pallas kernels: none -> 36.7 us  [the longest x2 14.8 us: balance(): pl.pallas_call(functools.partial(balance_kernel, place), grid_spec=pltpu....]
    reduce_sum x8 -> x2, other arithmetic: 30.3 us -> 1.28 us  [local(): both = [jnp.sum(sums_1 * live), jnp.sum(sums_2 * live), jnp.sum(live)]]
    gather x2 -> x0, local copies, waits for them, and re-layouts: 26.6 us -> none  [local(): diagonal_terms = jnp.diagonal(scaled, axis1=1, axis2=2)]
    unnamed x8 -> x10, local copies, waits for them, and re-layouts: 21.4 us -> 0.64 us
    broadcast_in_dim x1 -> x3, other arithmetic: 5.73 us -> 2.03 us  [the longest x1 1.95 us: local(): jnp.stack(both)[None]]
  transfers between devices with their start and end apart: 6 -> 26, of which waited for: 6 -> 19; matrix products, arithmetic and copies ran while one was open for 1% -> 3% of each run, Pallas kernels for 0% -> 19%
where the time goes in v1:
time: 180 us; the launch traced here: 179 us
  starting transfers between devices  98.3 us (55%)
  Pallas kernels  36.7 us (20%)
  waiting for transfers between devices  34.5 us (19%)
  other arithmetic  3.96 us (2%)
  between operations  3.77 us (2%)
    ppermute x26, starting transfers between devices, send(): return lax.ppermute(value, AXES, pairs)  98.3 us
    ppermute x26, waiting for transfers between devices, send(): return lax.ppermute(value, AXES, pairs)  34.5 us
    pallas_call x2, Pallas kernels, balance(): pl.pallas_call(functools.partial(balance_kernel, place), grid_spec=pltpu....  14.8 us
    pallas_call x2, Pallas kernels, weighted_sums(): pl.pallas_call(sums_kernel, grid_spec=pltpu.PrefetchScalarGridSpec(num_sc...  14.5 us
    pallas_call x1, Pallas kernels, pack(): pl.pallas_call(pack_kernel, grid=(8,), in_specs=[pl.BlockSpec(block, lamb...  7.32 us
  transfers between devices with their start and end apart: 26, of which 19 were waited for; matrix products, arithmetic and copies ran while one was open for 3% of the time, Pallas kernels for 19%

profile of v1, /device:TPU:0, one launch (start us, length us, event | category | flops | bytes accessed | tf_op | source)
XLA Modules:
  0.0 178.6 jit_solution(12118018455775615394)
XLA Ops:
  0.6 4.1 %collective-permute-start = (f32[2,1,1024,1024]{3,2,1,0:T(8,128)}, f32[2,1,1024,1024]{3,2,1,0:T(8,128)}, u32[]{:S(2)}, u32[]{:S(2)}) collective-permute-start(f32[2,1,1024,1024]{3,2,1,0:T(8,128)} %held_ref.3), channel_id=1, source_target_pairs={{1,65},{3,67},{5,69},{7,71},{9,73},{11,75},{13,77},{15,79},{17,81}... | collective-permute-start | bytes 25165832 | tf_op jit(solution)/shard_map/ppermute | solution.py:34
  4.7 7.3 %pack_triangles.1 = (f32[896,1024]{1,0:T(8,128)}, f32[128,1024]{1,0:T(8,128)S(1)}, f32[8,1,128]{2,1,0:T(1,128)S(1)}) custom-call(f32[2,1,1024,1024]{3,2,1,0:T(8,128)} %held_ref.3, f32[2,1,1024,1024]{3,2,1,0:T(8,128)} %held_ref.3), custom_call_target="tpu_custom_call" | custom-call | flops 1048576 | bytes 12582912 | tf_op jit(solution)/shard_map/pack_triangles/pallas_call | solution.py:91
  12.0 4.3 %collective-permute-start.1 = (f32[896,1024]{1,0:T(8,128)}, f32[896,1024]{1,0:T(8,128)}, u32[]{:S(2)}, u32[]{:S(2)}) collective-permute-start(f32[896,1024]{1,0:T(8,128)} %get-tuple-element.16), channel_id=1, source_target_pairs={{0,1},{2,3},{4,5},{6,7},{8,9},{10,11},{12,13},{14,15},{16,17},{18,... | collective-permute-start | bytes 11010056 | tf_op jit(solution)/shard_map/ppermute | solution.py:34
  17.7 4.2 %collective-permute-done.3 = f32[1,1024]{1,0:T(1,128)S(1)} collective-permute-done((f32[1,1024]{1,0:T(1,128)S(1)}, f32[1,1024]{1,0:T(1,128)S(1)}, u32[]{:S(2)}, u32[]{:S(2)}) %collective-permute-start.3) | collective-permute-done | bytes 4128 | tf_op jit(solution)/shard_map/ppermute | solution.py:34
  21.9 8.2 %collective-permute-start.4 = (f32[3,1024]{1,0:T(4,128)S(1)}, f32[3,1024]{1,0:T(4,128)S(1)}, u32[]{:S(2)}, u32[]{:S(2)}) collective-permute-start(f32[3,1024]{1,0:T(4,128)S(1)} %pad_maximum_fusion.1), channel_id=1, source_target_pairs={{0,64},{2,66},{4,68},{6,70},{8,72},{10,74},{12,76},{14,78},{16,80}... | collective-permute-start | bytes 36872 | tf_op jit(solution)/shard_map/ppermute | solution.py:34
  34.3 7.3 %weighted_sums.2 = (f32[2,1,1024]{2,1,0:T(1,128)S(1)}, f32[2,1,1024]{2,1,0:T(1,128)S(1)}) custom-call(s32[3]{0:T(128)S(1)} %add_convert_fusion.sc_ref, f32[2,1,1024,1024]{3,2,1,0:T(8,128)} %held_ref.3, f32[2,1,1024]{2,1,0:T(1,128)S(1)} %copy.7.a_ref, f32[2,1,1024]{2,1,0:T(1,128)S(1)} %copy.8.b_ref), custom_call_target="tpu_custom_call" | custom-call | flops 8388608 | bytes 8388608 | tf_op jit(solution)/shard_map/weighted_sums/pallas_call | solution.py:151
  44.8 5.4 %collective-permute-start.7 = (f32[4,1024]{1,0:T(4,128)S(1)}, f32[4,1024]{1,0:T(4,128)S(1)}, u32[]{:S(2)}, u32[]{:S(2)}) collective-permute-start(f32[4,1024]{1,0:T(4,128)S(1)} %pad_maximum_fusion.5), channel_id=1, source_target_pairs={{0,64},{2,66},{4,68},{6,70},{8,72},{10,74},{12,76},{14,78},{16,80}... | collective-permute-start | bytes 49160 | tf_op jit(solution)/shard_map/ppermute | solution.py:34
  56.2 4.5 %collective-permute-done.9 = f32[1,1024]{1,0:T(1,128)S(1)} collective-permute-done((f32[1,1024]{1,0:T(1,128)S(1)}, f32[1,1024]{1,0:T(1,128)S(1)}, u32[]{:S(2)}, u32[]{:S(2)}) %collective-permute-start.9) | collective-permute-done | bytes 4128 | tf_op jit(solution)/shard_map/ppermute | solution.py:34
  60.6 13.3 %collective-permute-start.10 = (f32[3,1024]{1,0:T(4,128)S(1)}, f32[3,1024]{1,0:T(4,128)S(1)}, u32[]{:S(2)}, u32[]{:S(2)}) collective-permute-start(f32[3,1024]{1,0:T(4,128)S(1)} %pad_maximum_fusion.2), channel_id=1, source_target_pairs={{0,64},{2,66},{4,68},{6,70},{8,72},{10,74},{12,76},{14,78},{16,80}... | collective-permute-start | bytes 36872 | tf_op jit(solution)/shard_map/ppermute | solution.py:34
  78.2 7.3 %weighted_sums.3 = (f32[2,1,1024]{2,1,0:T(1,128)S(1)}, f32[2,1,1024]{2,1,0:T(1,128)S(1)}) custom-call(s32[3]{0:T(128)S(1)} %add_convert_fusion.sc_ref, f32[2,1,1024,1024]{3,2,1,0:T(8,128)} %held_ref.3, f32[2,1,1024]{2,1,0:T(1,128)S(1)} %copy.9.a_ref, f32[2,1,1024]{2,1,0:T(1,128)S(1)} %copy.10.b_ref), custom_call_target="tpu_custom_call" | custom-call | flops 8388608 | bytes 8388608 | tf_op jit(solution)/shard_map/weighted_sums/pallas_call | solution.py:151
  88.6 5.4 %collective-permute-start.13 = (f32[4,1024]{1,0:T(4,128)S(1)}, f32[4,1024]{1,0:T(4,128)S(1)}, u32[]{:S(2)}, u32[]{:S(2)}) collective-permute-start(f32[4,1024]{1,0:T(4,128)S(1)} %pad_maximum_fusion.8), channel_id=1, source_target_pairs={{0,64},{2,66},{4,68},{6,70},{8,72},{10,74},{12,76},{14,78},{16,80}... | collective-permute-start | bytes 49160 | tf_op jit(solution)/shard_map/ppermute | solution.py:34
  99.8 2.0 %maximum_bitcast_fusion = f32[1,3]{1,0:T(1,128)S(1)} fusion(f32[1]{0:T(128)} %bitcast.10, f32[1]{0:T(128)} %bitcast.9, f32[1]{0:T(128)} %bitcast.8), kind=kLoop, calls=%fused_computation.53 | loop fusion | flops 6 | bytes 24 | tf_op jit(solution)/shard_map/broadcast_in_dim | solution.py:311
  101.7 4.2 %collective-permute-start.16 = (f32[1,128]{1,0:T(1,128)S(1)}, f32[1,128]{1,0:T(1,128)S(1)}, u32[]{:S(2)}, u32[]{:S(2)}) collective-permute-start(f32[1,128]{1,0:T(1,128)S(1)} %pad.4), channel_id=1, source_target_pairs={{0,2},{2,0},{4,6},{6,4},{8,10},{10,8},{12,14},{14,12},{16,18},{18,... | collective-permute-start | bytes 1544 | tf_op jit(solution)/shard_map/ppermute | solution.py:34
  107.4 4.0 %collective-permute-start.17 = (f32[1,128]{1,0:T(1,128)S(1)}, f32[1,128]{1,0:T(1,128)S(1)}, u32[]{:S(2)}, u32[]{:S(2)}) collective-permute-start(f32[1,128]{1,0:T(1,128)S(1)} %pad_add_fusion), channel_id=1, source_target_pairs={{0,4},{2,6},{4,0},{6,2},{8,12},{10,14},{12,8},{14,10},{16,20},{18,... | collective-permute-start | bytes 1544 | tf_op jit(solution)/shard_map/ppermute | solution.py:34
  111.4 3.0 %collective-permute-done.17 = f32[1,128]{1,0:T(1,128)S(1)} collective-permute-done((f32[1,128]{1,0:T(1,128)S(1)}, f32[1,128]{1,0:T(1,128)S(1)}, u32[]{:S(2)}, u32[]{:S(2)}) %collective-permute-start.17) | collective-permute-done | bytes 544 | tf_op jit(solution)/shard_map/ppermute | solution.py:34
  114.4 3.8 %collective-permute-start.18 = (f32[1,128]{1,0:T(1,128)S(1)}, f32[1,128]{1,0:T(1,128)S(1)}, u32[]{:S(2)}, u32[]{:S(2)}) collective-permute-start(f32[1,128]{1,0:T(1,128)S(1)} %add.45), channel_id=1, source_target_pairs={{0,8},{2,10},{4,12},{6,14},{8,0},{10,2},{12,4},{14,6},{16,24},{18,... | collective-permute-start | bytes 1544 | tf_op jit(solution)/shard_map/ppermute | solution.py:34
  119.8 7.2 %collective-permute-start.19 = (f32[1,128]{1,0:T(1,128)S(1)}, f32[1,128]{1,0:T(1,128)S(1)}, u32[]{:S(2)}, u32[]{:S(2)}) collective-permute-start(f32[1,128]{1,0:T(1,128)S(1)} %add.46), channel_id=1, source_target_pairs={{0,16},{2,18},{4,20},{6,22},{8,24},{10,26},{12,28},{14,30},{16,0},... | collective-permute-start | bytes 1544 | tf_op jit(solution)/shard_map/ppermute | solution.py:34
  128.5 9.0 %collective-permute-start.20 = (f32[1,128]{1,0:T(1,128)S(1)}, f32[1,128]{1,0:T(1,128)S(1)}, u32[]{:S(2)}, u32[]{:S(2)}) collective-permute-start(f32[1,128]{1,0:T(1,128)S(1)} %add.47), channel_id=1, source_target_pairs={{0,32},{2,34},{4,36},{6,38},{8,40},{10,42},{12,44},{14,46},{16,48}... | collective-permute-start | bytes 1544 | tf_op jit(solution)/shard_map/ppermute | solution.py:34
  139.0 5.4 %collective-permute-start.21 = (f32[1,128]{1,0:T(1,128)S(1)}, f32[1,128]{1,0:T(1,128)S(1)}, u32[]{:S(2)}, u32[]{:S(2)}) collective-permute-start(f32[1,128]{1,0:T(1,128)S(1)} %add.48), channel_id=1, source_target_pairs={{0,64},{2,66},{4,68},{6,70},{8,72},{10,74},{12,76},{14,78},{16,80}... | collective-permute-start | bytes 1544 | tf_op jit(solution)/shard_map/ppermute | solution.py:34
  151.3 5.5 %collective-permute-start.22 = (f32[5,1024]{1,0:T(8,128)S(1)}, f32[5,1024]{1,0:T(8,128)S(1)}, u32[]{:S(2)}, u32[]{:S(2)}) collective-permute-start(f32[5,1024]{1,0:T(8,128)S(1)} %pad_maximum_fusion), channel_id=1, source_target_pairs={{0,1},{2,3},{4,5},{6,7},{8,9},{10,11},{12,13},{14,15},{16,17},{18,... | collective-permute-start | bytes 61448 | tf_op jit(solution)/shard_map/ppermute | solution.py:34
  156.8 2.6 %collective-permute-start.23 = (f32[8,1,128]{2,1,0:T(1,128)S(1)}, f32[8,1,128]{2,1,0:T(1,128)S(1)}, u32[]{:S(2)}, u32[]{:S(2)}) collective-permute-start(f32[8,1,128]{2,1,0:T(1,128)S(1)} %get-tuple-element.21), channel_id=1, source_target_pairs={{0,64},{2,66},{4,68},{6,70},{8,72},{10,74},{12,76},{14,78},{16,80}... | collective-permute-start | bytes 12296 | tf_op jit(solution)/shard_map/ppermute | solution.py:34
  160.1 3.7 %collective-permute-done.23.dv_ref = f32[8,1,128]{2,1,0:T(1,128)S(1)} collective-permute-done((f32[8,1,128]{2,1,0:T(1,128)S(1)}, f32[8,1,128]{2,1,0:T(1,128)S(1)}, u32[]{:S(2)}, u32[]{:S(2)}) %collective-permute-start.23) | collective-permute-done | bytes 4128 | tf_op jit(solution)/shard_map/ppermute | solution.py:34
  163.8 11.8 %balance_most.1.rest_0_ = f32[2,1,1024,1024]{3,2,1,0:T(8,128)} custom-call(s32[3]{0:T(128)S(1)} %add_convert_fusion.sc_ref, f32[2,1,1024,1024]{3,2,1,0:T(8,128)} %collective-permute-done.got_ref, f32[2,1,1024,1024]{3,2,1,0:T(8,128)} %held_ref.3, f32[896,1024]{1,0:T(8,128)} %collective-permute-done.2.pk_ref, f32[8,1,128]{2,1,0:T(1,128)S(1)} %collective-permute-done.23.dv_ref, ...), custom_call_target="tpu_custom_call" | custom-call | flops 3670016 | bytes 14680064 | tf_op jit(solution)/shard_map/balance_most/pallas_call | solution.py:261
  175.6 3.0 %balance_last.1 = f32[2,1,1024,1024]{3,2,1,0:T(8,128)} custom-call(s32[3]{0:T(128)S(1)} %add_convert_fusion.sc_ref, f32[2,1,1024,1024]{3,2,1,0:T(8,128)} %collective-permute-done.got_ref, f32[2,1,1024,1024]{3,2,1,0:T(8,128)} %held_ref.3, f32[128,1024]{1,0:T(8,128)S(1)} %collective-permute-done.25.pk_ref, ...), custom_call_target="tpu_custom_call", output_to_operand_aliasing={{}: (7, {})} | custom-call | flops 524288 | bytes 2097152 | tf_op jit(solution)/shard_map/balance_last/pallas_call | solution.py:261
  (94 shorter events, 38.5 us)
Async XLA Ops:
  0.6 163.1 %collective-permute-start = (f32[2,1,1024,1024]{3,2,1,0:T(8,128)}, f32[2,1,1024,1024]{3,2,1,0:T(8,128)}, u32[]{:S(2)}, u32[]{:S(2)}) collective-permute-start(f32[2,1,1024,1024]{3,2,1,0:T(8,128)} %held_ref.3), channel_id=1, source_target_pairs={{1,65},{3,67},{5,69},{7,71},{9,73},{11,75},{13,77},{15,79},{17,81}... | collective-permute-start | bytes 25165832 | tf_op jit(solution)/shard_map/ppermute | solution.py:34
  12.0 41.5 %collective-permute-start.1 = (f32[896,1024]{1,0:T(8,128)}, f32[896,1024]{1,0:T(8,128)}, u32[]{:S(2)}, u32[]{:S(2)}) collective-permute-start(f32[896,1024]{1,0:T(8,128)} %get-tuple-element.16), channel_id=1, source_target_pairs={{0,1},{2,3},{4,5},{6,7},{8,9},{10,11},{12,13},{14,15},{16,17},{18,... | collective-permute-start | bytes 11010056 | tf_op jit(solution)/shard_map/ppermute | solution.py:34
  16.4 5.5 %collective-permute-start.3 = (f32[1,1024]{1,0:T(1,128)S(1)}, f32[1,1024]{1,0:T(1,128)S(1)}, u32[]{:S(2)}, u32[]{:S(2)}) collective-permute-start(f32[1,1024]{1,0:T(1,128)S(1)} %bitcast.50), channel_id=1, source_target_pairs={{2,0},{4,2},{6,4},{8,6},{10,8},{12,10},{14,12},{16,14},{18,16},{20... | collective-permute-start | bytes 12296 | tf_op jit(solution)/shard_map/ppermute | solution.py:34
  21.9 10.2 %collective-permute-start.4 = (f32[3,1024]{1,0:T(4,128)S(1)}, f32[3,1024]{1,0:T(4,128)S(1)}, u32[]{:S(2)}, u32[]{:S(2)}) collective-permute-start(f32[3,1024]{1,0:T(4,128)S(1)} %pad_maximum_fusion.1), channel_id=1, source_target_pairs={{0,64},{2,66},{4,68},{6,70},{8,72},{10,74},{12,76},{14,78},{16,80}... | collective-permute-start | bytes 36872 | tf_op jit(solution)/shard_map/ppermute | solution.py:34
  41.6 3.1 %collective-permute-start.6 = (f32[4,1024]{1,0:T(4,128)S(1)}, f32[4,1024]{1,0:T(4,128)S(1)}, u32[]{:S(2)}, u32[]{:S(2)}) collective-permute-start(f32[4,1024]{1,0:T(4,128)S(1)} %pad_maximum_fusion.4), channel_id=1, source_target_pairs={{1,0},{3,2},{5,4},{7,6},{9,8},{11,10},{13,12},{15,14},{17,16},{19,... | collective-permute-start | bytes 49160 | tf_op jit(solution)/shard_map/ppermute | solution.py:34
  44.8 7.4 %collective-permute-start.7 = (f32[4,1024]{1,0:T(4,128)S(1)}, f32[4,1024]{1,0:T(4,128)S(1)}, u32[]{:S(2)}, u32[]{:S(2)}) collective-permute-start(f32[4,1024]{1,0:T(4,128)S(1)} %pad_maximum_fusion.5), channel_id=1, source_target_pairs={{0,64},{2,66},{4,68},{6,70},{8,72},{10,74},{12,76},{14,78},{16,80}... | collective-permute-start | bytes 49160 | tf_op jit(solution)/shard_map/ppermute | solution.py:34
  52.2 2.6 %collective-permute-start.8 = (f32[1,1024]{1,0:T(1,128)S(1)}, f32[1,1024]{1,0:T(1,128)S(1)}, u32[]{:S(2)}, u32[]{:S(2)}) collective-permute-start(f32[1,1024]{1,0:T(1,128)S(1)} %get-tuple-element.51), channel_id=1, source_target_pairs={{0,2},{2,4},{4,6},{6,8},{8,10},{10,12},{12,14},{14,16},{16,18},{18... | collective-permute-start | bytes 12296 | tf_op jit(solution)/shard_map/ppermute | solution.py:34
  53.5 110.3 %collective-permute-start.2 = (f32[896,1024]{1,0:T(8,128)}, f32[896,1024]{1,0:T(8,128)}, u32[]{:S(2)}, u32[]{:S(2)}) collective-permute-start(f32[896,1024]{1,0:T(8,128)} %collective-permute-done.1), channel_id=1, source_target_pairs={{1,64},{3,66},{5,68},{7,70},{9,72},{11,74},{13,76},{15,78},{17,80}... | collective-permute-start | bytes 11010056 | tf_op jit(solution)/shard_map/ppermute | solution.py:34
  54.9 5.8 %collective-permute-start.9 = (f32[1,1024]{1,0:T(1,128)S(1)}, f32[1,1024]{1,0:T(1,128)S(1)}, u32[]{:S(2)}, u32[]{:S(2)}) collective-permute-start(f32[1,1024]{1,0:T(1,128)S(1)} %slice.134), channel_id=1, source_target_pairs={{2,0},{4,2},{6,4},{8,6},{10,8},{12,10},{14,12},{16,14},{18,16},{20... | collective-permute-start | bytes 12296 | tf_op jit(solution)/shard_map/ppermute | solution.py:34
  60.6 15.3 %collective-permute-start.10 = (f32[3,1024]{1,0:T(4,128)S(1)}, f32[3,1024]{1,0:T(4,128)S(1)}, u32[]{:S(2)}, u32[]{:S(2)}) collective-permute-start(f32[3,1024]{1,0:T(4,128)S(1)} %pad_maximum_fusion.2), channel_id=1, source_target_pairs={{0,64},{2,66},{4,68},{6,70},{8,72},{10,74},{12,76},{14,78},{16,80}... | collective-permute-start | bytes 36872 | tf_op jit(solution)/shard_map/ppermute | solution.py:34
  85.5 3.1 %collective-permute-start.12 = (f32[4,1024]{1,0:T(4,128)S(1)}, f32[4,1024]{1,0:T(4,128)S(1)}, u32[]{:S(2)}, u32[]{:S(2)}) collective-permute-start(f32[4,1024]{1,0:T(4,128)S(1)} %pad_maximum_fusion.7), channel_id=1, source_target_pairs={{1,0},{3,2},{5,4},{7,6},{9,8},{11,10},{13,12},{15,14},{17,16},{19,... | collective-permute-start | bytes 49160 | tf_op jit(solution)/shard_map/ppermute | solution.py:34
  88.6 7.4 %collective-permute-start.13 = (f32[4,1024]{1,0:T(4,128)S(1)}, f32[4,1024]{1,0:T(4,128)S(1)}, u32[]{:S(2)}, u32[]{:S(2)}) collective-permute-start(f32[4,1024]{1,0:T(4,128)S(1)} %pad_maximum_fusion.8), channel_id=1, source_target_pairs={{0,64},{2,66},{4,68},{6,70},{8,72},{10,74},{12,76},{14,78},{16,80}... | collective-permute-start | bytes 49160 | tf_op jit(solution)/shard_map/ppermute | solution.py:34
  96.1 3.0 %collective-permute-start.14 = (f32[1,1024]{1,0:T(1,128)S(1)}, f32[1,1024]{1,0:T(1,128)S(1)}, u32[]{:S(2)}, u32[]{:S(2)}) collective-permute-start(f32[1,1024]{1,0:T(1,128)S(1)} %get-tuple-element.47), channel_id=1, source_target_pairs={{0,2},{2,4},{4,6},{6,8},{8,10},{10,12},{12,14},{14,16},{16,18},{18... | collective-permute-start | bytes 12296 | tf_op jit(solution)/shard_map/ppermute | solution.py:34
  101.7 5.7 %collective-permute-start.16 = (f32[1,128]{1,0:T(1,128)S(1)}, f32[1,128]{1,0:T(1,128)S(1)}, u32[]{:S(2)}, u32[]{:S(2)}) collective-permute-start(f32[1,128]{1,0:T(1,128)S(1)} %pad.4), channel_id=1, source_target_pairs={{0,2},{2,0},{4,6},{6,4},{8,10},{10,8},{12,14},{14,12},{16,18},{18,... | collective-permute-start | bytes 1544 | tf_op jit(solution)/shard_map/ppermute | solution.py:34
  105.9 44.0 %collective-permute-start.24 = (f32[128,1024]{1,0:T(8,128)S(1)}, f32[128,1024]{1,0:T(8,128)S(1)}, u32[]{:S(2)}, u32[]{:S(2)}) collective-permute-start(f32[128,1024]{1,0:T(8,128)S(1)} %get-tuple-element.27), channel_id=1, source_target_pairs={{0,1},{2,3},{4,5},{6,7},{8,9},{10,11},{12,13},{14,15},{16,17},{18,... | collective-permute-start | bytes 1572872 | tf_op jit(solution)/shard_map/ppermute | solution.py:34
  107.4 6.9 %collective-permute-start.17 = (f32[1,128]{1,0:T(1,128)S(1)}, f32[1,128]{1,0:T(1,128)S(1)}, u32[]{:S(2)}, u32[]{:S(2)}) collective-permute-start(f32[1,128]{1,0:T(1,128)S(1)} %pad_add_fusion), channel_id=1, source_target_pairs={{0,4},{2,6},{4,0},{6,2},{8,12},{10,14},{12,8},{14,10},{16,20},{18,... | collective-permute-start | bytes 1544 | tf_op jit(solution)/shard_map/ppermute | solution.py:34
  114.4 5.4 %collective-permute-start.18 = (f32[1,128]{1,0:T(1,128)S(1)}, f32[1,128]{1,0:T(1,128)S(1)}, u32[]{:S(2)}, u32[]{:S(2)}) collective-permute-start(f32[1,128]{1,0:T(1,128)S(1)} %add.45), channel_id=1, source_target_pairs={{0,8},{2,10},{4,12},{6,14},{8,0},{10,2},{12,4},{14,6},{16,24},{18,... | collective-permute-start | bytes 1544 | tf_op jit(solution)/shard_map/ppermute | solution.py:34
  119.8 8.7 %collective-permute-start.19 = (f32[1,128]{1,0:T(1,128)S(1)}, f32[1,128]{1,0:T(1,128)S(1)}, u32[]{:S(2)}, u32[]{:S(2)}) collective-permute-start(f32[1,128]{1,0:T(1,128)S(1)} %add.46), channel_id=1, source_target_pairs={{0,16},{2,18},{4,20},{6,22},{8,24},{10,26},{12,28},{14,30},{16,0},... | collective-permute-start | bytes 1544 | tf_op jit(solution)/shard_map/ppermute | solution.py:34
  128.5 10.5 %collective-permute-start.20 = (f32[1,128]{1,0:T(1,128)S(1)}, f32[1,128]{1,0:T(1,128)S(1)}, u32[]{:S(2)}, u32[]{:S(2)}) collective-permute-start(f32[1,128]{1,0:T(1,128)S(1)} %add.47), channel_id=1, source_target_pairs={{0,32},{2,34},{4,36},{6,38},{8,40},{10,42},{12,44},{14,46},{16,48}... | collective-permute-start | bytes 1544 | tf_op jit(solution)/shard_map/ppermute | solution.py:34
  139.0 6.9 %collective-permute-start.21 = (f32[1,128]{1,0:T(1,128)S(1)}, f32[1,128]{1,0:T(1,128)S(1)}, u32[]{:S(2)}, u32[]{:S(2)}) collective-permute-start(f32[1,128]{1,0:T(1,128)S(1)} %add.48), channel_id=1, source_target_pairs={{0,64},{2,66},{4,68},{6,70},{8,72},{10,74},{12,76},{14,78},{16,80}... | collective-permute-start | bytes 1544 | tf_op jit(solution)/shard_map/ppermute | solution.py:34
  144.4 5.5 %collective-permute-start.15 = (f32[1,1024]{1,0:T(1,128)S(1)}, f32[1,1024]{1,0:T(1,128)S(1)}, u32[]{:S(2)}, u32[]{:S(2)}) collective-permute-start(f32[1,1024]{1,0:T(1,128)S(1)} %slice.146), channel_id=1, source_target_pairs={{2,0},{4,2},{6,4},{8,6},{10,8},{12,10},{14,12},{16,14},{18,16},{20... | collective-permute-start | bytes 12296 | tf_op jit(solution)/shard_map/ppermute | solution.py:34
  149.9 25.7 %collective-permute-start.25 = (f32[128,1024]{1,0:T(8,128)S(1)}, f32[128,1024]{1,0:T(8,128)S(1)}, u32[]{:S(2)}, u32[]{:S(2)}) collective-permute-start(f32[128,1024]{1,0:T(8,128)S(1)} %collective-permute-done.24), channel_id=1, source_target_pairs={{1,64},{3,66},{5,68},{7,70},{9,72},{11,74},{13,76},{15,78},{17,80}... | collective-permute-start | bytes 1572872 | tf_op jit(solution)/shard_map/ppermute | solution.py:34
  151.3 8.1 %collective-permute-start.22 = (f32[5,1024]{1,0:T(8,128)S(1)}, f32[5,1024]{1,0:T(8,128)S(1)}, u32[]{:S(2)}, u32[]{:S(2)}) collective-permute-start(f32[5,1024]{1,0:T(8,128)S(1)} %pad_maximum_fusion), channel_id=1, source_target_pairs={{0,1},{2,3},{4,5},{6,7},{8,9},{10,11},{12,13},{14,15},{16,17},{18,... | collective-permute-start | bytes 61448 | tf_op jit(solution)/shard_map/ppermute | solution.py:34
  156.8 7.0 %collective-permute-start.23 = (f32[8,1,128]{2,1,0:T(1,128)S(1)}, f32[8,1,128]{2,1,0:T(1,128)S(1)}, u32[]{:S(2)}, u32[]{:S(2)}) collective-permute-start(f32[8,1,128]{2,1,0:T(1,128)S(1)} %get-tuple-element.21), channel_id=1, source_target_pairs={{0,64},{2,66},{4,68},{6,70},{8,72},{10,74},{12,76},{14,78},{16,80}... | collective-permute-start | bytes 12296 | tf_op jit(solution)/shard_map/ppermute | solution.py:34
  (5 other events, 174.5 us)

commit v2 on v1

v2 whole, which is shorter than its diff:
```python
import functools

import jax
import jax.numpy as jnp
from jax import lax
from jax.experimental import pallas as pl
from jax.experimental.pallas import tpu as pltpu
from jax.sharding import PartitionSpec as P

AXES = ("bins", "diag")
F32 = jnp.float32
LANE = 128
VMEM_LIMIT = 48 * 1024 * 1024


def iotas():
    rows = lax.broadcasted_iota(jnp.int32, (LANE, LANE), 0)
    cols = lax.broadcasted_iota(jnp.int32, (LANE, LANE), 1)
    return rows, cols


def as_column(line):
    return jnp.broadcast_to(line, (LANE, LANE)).T


def lanes(k):
    return pl.ds(k * LANE, LANE)


def moves(n_bins):
    half = n_bins // 2
    chips = range(n_bins)

    def other(d):
        return (d + half) % n_bins

    def move(pairs, source_core, target_core):
        pairs = [(2 * s + source_core, 2 * t + target_core) for s, t in pairs]
        return lambda value: lax.ppermute(value, AXES, pairs)

    plane = max(n_bins // 4, 1)
    planes = [list(range(start, start + plane)) for start in range(0, n_bins, plane)]

    def plane_sum(value):
        spread = jnp.broadcast_to(value, (plane, value.shape[1]))
        seen = lax.all_to_all(spread, "bins", 0, 0, axis_index_groups=planes, tiled=True)
        return jnp.sum(seen, axis=0, keepdims=True)

    same = [(d, d) for d in chips]
    swap = [(d, other(d)) for d in chips]
    both_ways = [(2 * d, 2 * d + 1) for d in chips] + [(2 * d + 1, 2 * d) for d in chips]
    return dict(
        core=lambda value: lax.ppermute(value, AXES, both_ways),
        across=move(swap, 0, 0),
        tiles=move(swap, 1, 1),
        before=move([(d + 1, d) for d in chips[:-1]], 0, 0),
        after=move([(d, d + 1) for d in chips[:-1]], 0, 0),
        ends=move([(half - 1, 0), (half, n_bins - 1)], 0, 0),
        beside=move([(d, d ^ plane) for d in chips], 0, 0),
        plane_sum=plane_sum,
    )


BLOCKS = [(0, 0), (0, 1), (0, 2), (0, 3), (1, 1), (1, 2), (1, 3), (1, 0)]
SENT = (1, 3, 3, 1)


def pack_kernel(held_ref, *refs):
    out_refs, (dv_ref, near_buf, far_buf, in_sem, out_sem) = refs[: len(SENT)], refs[len(SENT) :]
    rows, cols = iotas()
    count = len(BLOCKS)
    targets = [ref.at[pl.ds(j * LANE, LANE), :] for ref, blocks in zip(out_refs, SENT) for j in range(blocks)]

    def source(t, b, start, width):
        return held_ref.at[t, 0, pl.ds(b * LANE, LANE), pl.ds(start * LANE, width * LANE)]

    def near(n, start, width):
        return near_buf.at[n, :, pl.ds(start * LANE, width * LANE)]

    loads = [[] for _ in BLOCKS]
    for n, (t, k) in enumerate(BLOCKS):
        loads[n].append(pltpu.make_async_copy(source(t, 7 - k, 7 - k, 1), far_buf.at[n], in_sem.at[n]))
        loads[n].append(pltpu.make_async_copy(source(t, k, k, 8 - k), near(n, k, 8 - k), in_sem.at[count + n]))
        if k:
            loads[n].append(pltpu.make_async_copy(source(t, 7 - k, 8 - k, k), near(n, 0, k), in_sem.at[2 * count + n]))
        for copy in loads[n]:
            copy.start()
    stores = []
    for n, (t, k) in enumerate(BLOCKS):
        for copy in loads[n]:
            copy.wait()
        far = far_buf[n]
        block = near(n, k, 1)
        block[...] = jnp.where(cols >= rows, block[...], far.T)
        dv_ref[n] = jnp.sum(jnp.where(cols == rows, far, 0.0), axis=0, keepdims=True)
        stores.append(pltpu.make_async_copy(near_buf.at[n], targets[n], out_sem.at[n]))
        stores[-1].start()
    for copy in stores:
        copy.wait()


def pack(held):
    return pl.pallas_call(
        pack_kernel,
        in_specs=[pl.BlockSpec(memory_space=pl.ANY)],
        out_specs=[pl.BlockSpec(memory_space=pltpu.HBM)] * len(SENT) + [pl.BlockSpec(memory_space=pltpu.VMEM)],
        out_shape=[jax.ShapeDtypeStruct((blocks * LANE, 1024), F32) for blocks in SENT]
        + [jax.ShapeDtypeStruct((8, 1, LANE), F32)],
        scratch_shapes=[
            pltpu.VMEM((8, LANE, 1024), F32),
            pltpu.VMEM((8, LANE, LANE), F32),
            pltpu.SemaphoreType.DMA((24,)),
            pltpu.SemaphoreType.DMA((8,)),
        ],
        compiler_params=pltpu.CompilerParams(vmem_limit_bytes=VMEM_LIMIT),
        cost_estimate=pl.CostEstimate(flops=1 << 20, bytes_accessed=8 << 20, transcendentals=0),
        name="pack_triangles",
    )(held)


STREAMS = 4
ROWS = STREAMS * LANE


def sums_kernel(sc_ref, *refs):
    x_refs, (a_ref, b_ref, row_ref, col_ref, acc_ref) = refs[:STREAMS], refs[STREAMS:]
    i = pl.program_id(1)
    rows, cols = iotas()
    ahead = cols - rows

    @pl.when(i == 0)
    def _():
        acc_ref[...] = jnp.zeros_like(acc_ref)

    def add_up(masked):
        for r in range(STREAMS):
            a_line = a_ref[0, :, lanes(r)]
            a_col = as_column(a_line)
            start = i * ROWS + r * LANE
            across = jnp.zeros((LANE, LANE), F32)
            for k in range(8):
                x = x_refs[r][0, 0, :, lanes(k)]
                right = down = x
                if masked:
                    shift = start - k * LANE
                    right, down = jnp.where(ahead >= shift, x, 0.0), jnp.where(ahead > shift, x, 0.0)
                across += right * b_ref[0, :, lanes(k)]
                acc_ref[:, lanes(k)] += jnp.sum((down * a_col).reshape(LANE // 8, 8, LANE), axis=0)
            row_ref[0, :, lanes(r)] = jnp.sum(across.T, axis=0, keepdims=True) * a_line

    @pl.when(sc_ref[0] == 1)
    def _():
        add_up(True)

    @pl.when(sc_ref[0] == 0)
    def _():
        add_up(False)

    @pl.when(i == pl.num_programs(1) - 1)
    def _():
        col_ref[0] = jnp.sum(acc_ref[...], axis=0, keepdims=True) * b_ref[0]


def weighted_sums(scalars, held, row_w, col_w):
    steps = 1024 // ROWS
    shape = jax.ShapeDtypeStruct((2, 1, 1024), F32)

    def stream(r):
        return pl.BlockSpec((1, 1, LANE, 1024), lambda t, i, sc: (t, 0, STREAMS * i + r, 0))

    row_part, col_part = pl.pallas_call(
        sums_kernel,
        grid_spec=pltpu.PrefetchScalarGridSpec(
            num_scalar_prefetch=1,
            grid=(2, steps),
            in_specs=[stream(r) for r in range(STREAMS)]
            + [
                pl.BlockSpec((1, 1, ROWS), lambda t, i, sc: (t, 0, i)),
                pl.BlockSpec((1, 1, 1024), lambda t, i, sc: (t, 0, 0)),
            ],
            out_specs=[
                pl.BlockSpec((1, 1, ROWS), lambda t, i, sc: (t, 0, i)),
                pl.BlockSpec((1, 1, 1024), lambda t, i, sc: (t, 0, 0)),
            ],
            scratch_shapes=[pltpu.VMEM((8, 1024), F32)],
        ),
        out_shape=[shape, shape],
        compiler_params=pltpu.CompilerParams(vmem_limit_bytes=VMEM_LIMIT),
        cost_estimate=pl.CostEstimate(flops=8 << 20, bytes_accessed=8 << 20, transcendentals=0),
        name="weighted_sums",
    )(scalars, *[held] * STREAMS, row_w.reshape(2, 1, 1024), col_w.reshape(2, 1, 1024))
    return row_part.reshape(2, 1024), col_part.reshape(2, 1024)


def ahead_place(i):
    return 0, 0, jnp.where(i == 0, 0, 7)


def first_place(i):
    k = i // 2 + 1
    return 0, k, jnp.where(i % 2 == 0, k, 7 - k)


def mid_place(i):
    k = i // 2 + 1
    return 1, k, jnp.where(i % 2 == 0, k, 7 - k)


def last_place(i):
    return 1, 0, jnp.where(i == 0, 0, 7)


def balance_kernel(place, sc_ref, got_ref, held_ref, pk_ref, dv_ref, wr_ref, wc_ref, *rest):
    out_ref = rest[-1]
    t, k_now, b = place(pl.program_id(0))
    rows, cols = iotas()
    on_diagonal = sc_ref[0] == 1
    moved = sc_ref[1 + t] == 1
    w_col = as_column(wr_ref[0])

    def put(j, x):
        out_ref[0, 0, :, lanes(j)] = x * w_col * wc_ref[0, :, lanes(j)]

    @pl.when(moved & jnp.logical_not(on_diagonal))
    def _():
        for j in range(8):
            put(j, got_ref[0, 0, :, lanes(j)])

    @pl.when(jnp.logical_not(moved))
    def _():
        least = jnp.where(on_diagonal, 0, -4096) + b * LANE
        for j in range(8):
            put(j, jnp.where(cols - rows >= least - j * LANE, held_ref[0, 0, :, lanes(j)], 0.0))

    for k in range(4):
        @pl.when(moved & on_diagonal & (k_now == k) & (b == k))
        def _():
            for j in range(k):
                out_ref[0, 0, :, lanes(j)] = jnp.zeros((LANE, LANE), F32)
            put(k, jnp.where(cols >= rows, pk_ref[:, lanes(k)], 0.0))
            for j in range(k + 1, 8):
                put(j, pk_ref[:, lanes(j)])

        @pl.when(moved & on_diagonal & (k_now == k) & (b == 7 - k))
        def _():
            for j in range(7 - k):
                out_ref[0, 0, :, lanes(j)] = jnp.zeros((LANE, LANE), F32)
            far = pk_ref[:, lanes(k)].T
            put(7 - k, jnp.where(cols > rows, far, jnp.where(cols == rows, dv_ref[0], 0.0)))
            for j in range(k):
                put(8 - k + j, pk_ref[:, lanes(j)])


def balance(name, place, steps, first_k, scalars, got, held, packed, dv, wr, wc, into=None):
    tile = (1, 1, LANE, 1024)

    def got_at(i, sc):
        t, _, b = place(i)
        use = (sc[0] == 0) & (sc[1 + t] == 1)
        return (jnp.where(use, t, 0), 0, jnp.where(use, b, 0), 0)

    def held_at(i, sc):
        t, _, b = place(i)
        use = sc[1 + t] == 0
        return (jnp.where(use, t, 0), 0, jnp.where(use, b, 0), 0)

    def packed_at(i, sc):
        t, k, _ = place(i)
        use = (sc[0] == 1) & (sc[1 + t] == 1)
        return (jnp.where(use, k - first_k, 0), 0)

    def dv_at(i, sc):
        t, k, _ = place(i)
        return (k if t == 0 else jnp.where(k == 0, 7, 3 + k), 0, 0)

    in_specs = [
        pl.BlockSpec(tile, got_at),
        pl.BlockSpec(tile, held_at),
        pl.BlockSpec((LANE, 1024), packed_at),
        pl.BlockSpec((1, 1, LANE), dv_at),
        pl.BlockSpec((1, 1, LANE), lambda i, sc: (place(i)[0] * 8 + place(i)[2], 0, 0)),
        pl.BlockSpec((1, 1, 1024), lambda i, sc: (place(i)[0], 0, 0)),
    ]
    args = [scalars, got, held, packed, dv, wr, wc]
    aliases = {}
    if into is not None:
        in_specs.append(pl.BlockSpec(memory_space=pl.ANY))
        args.append(into)
        aliases = {len(args) - 1: 0}
    return pl.pallas_call(
        functools.partial(balance_kernel, place),
        grid_spec=pltpu.PrefetchScalarGridSpec(
            num_scalar_prefetch=1,
            grid=(steps,),
            in_specs=in_specs,
            out_specs=pl.BlockSpec(tile, lambda i, sc: (place(i)[0], 0, place(i)[2], 0)),
        ),
        out_shape=jax.ShapeDtypeStruct(held.shape, F32),
        input_output_aliases=aliases,
        compiler_params=pltpu.CompilerParams(vmem_limit_bytes=VMEM_LIMIT),
        cost_estimate=pl.CostEstimate(flops=steps << 18, bytes_accessed=steps << 20, transcendentals=0),
        name=name,
    )(*args)


def local(held_tiles, placed, bin_mask, bias):
    move = moves(lax.axis_size("bins"))
    on_diagonal = lax.axis_index("diag") == 0
    live = bin_mask.astype(F32).reshape(2, 1024)
    scalars = jnp.concatenate([on_diagonal.astype(jnp.int32)[None], (placed == 1).astype(jnp.int32)])

    got = move["tiles"](held_tiles)
    ahead, first, mid, last, dv = pack(held_tiles)

    here = lax.axis_index("bins")
    there = here ^ (lax.axis_size("bins") // 2)
    moved = placed[1] == 1

    def stored(lines):
        row_lines = [lines[3:4], jnp.where(moved, lines[4:5], lines[1:2])]
        next_lines = [lines[4:5], jnp.where(moved, lines[5:6], lines[2:3])]
        return jnp.concatenate(row_lines, axis=0), jnp.concatenate(next_lines, axis=0)

    def stored_parts(lines):
        rows, following = stored(lines)
        passed = move["core"](jnp.concatenate([rows, following], axis=0))
        row_w, col_w = jnp.where(on_diagonal, rows, passed[:2]), jnp.where(on_diagonal, rows, passed[2:])
        row_part, col_part = weighted_sums(scalars, held_tiles, row_w, col_w)
        off = move["core"](jnp.concatenate([row_part, col_part], axis=0))
        return row_part + col_part + off[:2], off[2:]

    def home_sums(mine, theirs):
        rows_d = [theirs[0:1], jnp.where(moved, theirs[1:2], mine[1:2])]
        rows_p = [mine[0:1], jnp.where(moved, mine[1:2], theirs[1:2])]
        cols_d = [theirs[2:3], jnp.where(moved, theirs[3:4], mine[3:4])]
        cols_p = [mine[2:3], jnp.where(moved, mine[3:4], theirs[3:4])]
        return rows_d, rows_p, cols_d, cols_p

    def sums_of(parts, which, cols_before, rows_after):
        rows, cols = parts[which], parts[2 + which]
        first = (there if which else here) == 0
        return jnp.concatenate(
            [rows[0] + jnp.where(first, 0.0, cols_before), rows[1] + cols[0], rows_after + cols[1]], axis=0
        )

    def neighbours(parts, count):
        rows_d, rows_p, cols_d, cols_p = parts
        cols_before = move["after"](jnp.concatenate([cols_d[1], cols_p[1]][:count], axis=0))
        rows_after = move["before"](jnp.concatenate([rows_d[0], rows_p[0]][:count], axis=0))
        return cols_before, rows_after

    after_live = move["before"](live[:1])
    live_lines = jnp.concatenate([live, after_live], axis=0)
    live_lines = jnp.concatenate([live_lines, move["across"](live_lines)], axis=0)

    rows, cols = stored_parts(live_lines)
    line_1 = rows[:1] + rows[1:] + cols[:1] + cols[1:]
    mine = jnp.concatenate([rows, cols], axis=0)
    parts = home_sums(mine, move["across"](mine))
    ends = move["ends"](jnp.concatenate([parts[2][1], parts[0][0]], axis=0))
    ends, cols_before, rows_after, ahead = lax.optimization_barrier((ends, *neighbours(parts, 2), ahead))
    ahead = move["across"](ahead)
    cols_before = [cols_before[0:1], jnp.where(here == 0, ends[0:1], cols_before[1:2])]
    rows_after = [rows_after[0:1], jnp.where(there == lax.axis_size("bins") // 2 - 1, ends[1:2], rows_after[1:2])]
    sums_1 = jnp.concatenate([sums_of(parts, 0, cols_before[0], rows_after[0]), sums_of(parts, 1, cols_before[1], rows_after[1])], axis=0)

    rows, cols = stored_parts(jnp.where(live_lines > 0, 1.0 / sums_1, 0.0))
    rows, cols, ahead = lax.optimization_barrier((rows, cols, ahead))
    totals = [line_1, rows[:1] + rows[1:] + cols[:1] + cols[1:], live[:1] + live[1:]]
    mine = jnp.concatenate([rows, cols, *totals, dv.reshape(1, 1024)], axis=0)
    theirs = move["across"](mine)
    parts = home_sums(mine, theirs)
    dv = theirs[7:8].reshape(8, 1, LANE)
    totals = jnp.sum((mine[4:7] + theirs[4:7]).reshape(3, 8, LANE), axis=1).reshape(1, 3 * LANE)
    beside, *around, first, mid, last = lax.optimization_barrier(
        (move["beside"](totals), *neighbours(parts, 1), first, mid, last)
    )
    first, mid, last = move["across"](first), move["across"](mid), move["across"](last)
    totals = move["plane_sum"](totals + beside)
    sums_2 = sums_of(parts, 0, *around)
    totals = jnp.sum(totals.reshape(3, LANE), axis=1)
    scale = (totals[0] / totals[2]) * (totals[1] / totals[2])

    products = sums_1[:3] * sums_2
    weights = jnp.where(live_lines[:3] > 0, scale / products, 0.0)
    factor = jnp.where(live > 0, products[:2] / scale, 1.0)
    result = jnp.concatenate([weights, factor], axis=0)
    result = jnp.where(on_diagonal, result, move["core"](result))
    bias_out = bias.reshape(2, 1024) * result[3:]
    wr = result[:2].reshape(16, 1, LANE)
    wc = jnp.where(on_diagonal, result[:2], result[1:3]).reshape(2, 1, 1024)

    got, ahead, wr, wc, dv = lax.optimization_barrier((got, ahead, wr, wc, dv))
    out = balance("balance_ahead", ahead_place, 2, 0, scalars, got, held_tiles, ahead, dv, wr, wc)
    out, first = lax.optimization_barrier((out, first))
    out = balance("balance_first", first_place, 6, 1, scalars, got, held_tiles, first, dv, wr, wc, into=out)
    out, mid = lax.optimization_barrier((out, mid))
    out = balance("balance_mid", mid_place, 6, 1, scalars, got, held_tiles, mid, dv, wr, wc, into=out)
    out, last = lax.optimization_barrier((out, last))
    out = balance("balance_last", last_place, 2, 0, scalars, got, held_tiles, last, dv, wr, wc, into=out)
    return out, bias_out.reshape(2048)


def solution(mesh):
    placed = (P("bins", "diag", None, None), P("bins"), P("bins"), P("bins"))
    return jax.shard_map(
        local,
        mesh=mesh,
        in_specs=placed,
        out_specs=(P("bins", "diag", None, None), P("bins")),
        check_vma=False,
    )
```

time: 180 us -> 160 us (0.89)
  starting transfers between devices: 98.3 us -> 82 us
  local copies, waits for them, and re-layouts: 1.41 us -> 8.26 us
  Pallas kernels: 36.7 us -> 30.4 us
  waiting for transfers between devices: 34.5 us -> 31.3 us
  other arithmetic: 3.96 us -> 2.09 us
    ppermute x26 -> x20, starting transfers between devices: 98.3 us -> 78.5 us  [the longest x15 78.1 us: move(): return lambda value: lax.ppermute(value, AXES, pairs)]
    ppermute x26 -> x20, waiting for transfers between devices: 34.5 us -> 29.2 us  [the longest x15 24.6 us: move(): return lambda value: lax.ppermute(value, AXES, pairs)]
    unnamed x10 -> x17, local copies, waits for them, and re-layouts: 0.64 us -> 5.56 us
    pallas_call x1, Pallas kernels: 7.32 us -> 2.77 us  [pack(): pl.pallas_call(pack_kernel, in_specs=[pl.BlockSpec(memory_space=pl.ANY)],...]
    all_to_all x0 -> x1, starting transfers between devices: none -> 3.49 us  [plane_sum(): lax.all_to_all(spread, 'bins', 0, 0, axis_index_groups=planes, tiled=True)]
    pallas_call x2, Pallas kernels: 14.5 us -> 11.3 us  [weighted_sums(): pl.pallas_call(sums_kernel, grid_spec=pltpu.PrefetchScalarGridSpec(num_sc...]
    all_to_all x0 -> x1, waiting for transfers between devices: none -> 2.08 us  [plane_sum(): lax.all_to_all(spread, 'bins', 0, 0, axis_index_groups=planes, tiled=True)]
    broadcast_in_dim x3 -> x0, other arithmetic: 2.03 us -> none  [the longest x1 1.95 us: local(): jnp.stack(both)[None]]
  transfers between devices with their start and end apart: 26 -> 21, of which waited for: 19 -> 13; matrix products, arithmetic and copies ran while one was open for 3% -> 3% of each run, Pallas kernels for 19% -> 17%
where the time goes in v2:
time: 160 us; the launch traced here: 158 us
  starting transfers between devices  82 us (51%)
  waiting for transfers between devices  31.3 us (20%)
  Pallas kernels  30.4 us (19%)
  local copies, waits for them, and re-layouts  8.26 us (5%)
  between operations  4.41 us (3%)
  other arithmetic  2.09 us (1%)
    ppermute x15, starting transfers between devices, move(): return lambda value: lax.ppermute(value, AXES, pairs)  78.1 us
    ppermute x15, waiting for transfers between devices, move(): return lambda value: lax.ppermute(value, AXES, pairs)  24.6 us
    pallas_call x4, Pallas kernels, balance(): pl.pallas_call(functools.partial(balance_kernel, place), grid_spec=pltpu....  16.3 us
    pallas_call x2, Pallas kernels, weighted_sums(): pl.pallas_call(sums_kernel, grid_spec=pltpu.PrefetchScalarGridSpec(num_sc...  11.3 us
    unnamed x17, local copies, waits for them, and re-layouts  5.56 us
    ppermute x5, waiting for transfers between devices, moves(): lax.ppermute(value, AXES, both_ways)  4.61 us
    all_to_all x1, starting transfers between devices, plane_sum(): lax.all_to_all(spread, 'bins', 0, 0, axis_index_groups=planes, tiled=True)  3.49 us
  transfers between devices with their start and end apart: 21, of which 13 were waited for; matrix products, arithmetic and copies ran while one was open for 3% of the time, Pallas kernels for 17%

profile of v2, /device:TPU:0, one launch (start us, length us, event | category | flops | bytes accessed | tf_op | source)
XLA Modules:
  0.0 158.4 jit_solution(12317424600871007737)
XLA Ops:
  0.6 3.9 %collective-permute-start = (f32[2,1,1024,1024]{3,2,1,0:T(8,128)}, f32[2,1,1024,1024]{3,2,1,0:T(8,128)}, u32[]{:S(2)}, u32[]{:S(2)}) collective-permute-start(f32[2,1,1024,1024]{3,2,1,0:T(8,128)} %held_ref.9), channel_id=1, source_target_pairs={{1,65},{3,67},{5,69},{7,71},{9,73},{11,75},{13,77},{15,79},{17,81}... | collective-permute-start | bytes 25165832 | tf_op jit(solution)/shard_map/ppermute | solution.py:39
  6.6 4.2 %collective-permute-done.1 = f32[1,1024]{1,0:T(1,128)S(1)} collective-permute-done((f32[1,1024]{1,0:T(1,128)S(1)}, f32[1,1024]{1,0:T(1,128)S(1)}, u32[]{:S(2)}, u32[]{:S(2)}) %collective-permute-start.1) | collective-permute-done | bytes 4128 | tf_op jit(solution)/shard_map/ppermute | solution.py:39
  10.8 9.2 %collective-permute-start.2 = (f32[3,1024]{1,0:T(4,128)S(1)}, f32[3,1024]{1,0:T(4,128)S(1)}, u32[]{:S(2)}, u32[]{:S(2)}) collective-permute-start(f32[3,1024]{1,0:T(4,128)S(1)} %pad_maximum_fusion.1), channel_id=1, source_target_pairs={{0,64},{2,66},{4,68},{6,70},{8,72},{10,74},{12,76},{14,78},{16,80}... | collective-permute-start | bytes 36872 | tf_op jit(solution)/shard_map/ppermute | solution.py:39
  23.9 5.6 %weighted_sums.2 = (f32[2,1,1024]{2,1,0:T(1,128)S(1)}, f32[2,1,1024]{2,1,0:T(1,128)S(1)}) custom-call(s32[3]{0:T(128)S(1)} %add_convert_fusion.sc_ref, f32[2,1,1024,1024]{3,2,1,0:T(8,128)} %held_ref.9, f32[2,1,1024,1024]{3,2,1,0:T(8,128)} %held_ref.9, f32[2,1,1024,1024]{3,2,1,0:T(8,128)} %held_ref.9, f32[2,1,1024,1024]{3,2,1,0:T(8,128)} %held_ref.9, ...), custom_call_target="tpu_custom_call" | custom-call | flops 8388608 | bytes 8388608 | tf_op jit(solution)/shard_map/weighted_sums/pallas_call | solution.py:171
  30.9 4.8 %collective-permute-start.5 = (f32[4,1024]{1,0:T(4,128)S(1)}, f32[4,1024]{1,0:T(4,128)S(1)}, u32[]{:S(2)}, u32[]{:S(2)}) collective-permute-start(f32[4,1024]{1,0:T(4,128)S(1)} %pad_maximum_fusion.4), channel_id=1, source_target_pairs={{0,64},{2,66},{4,68},{6,70},{8,72},{10,74},{12,76},{14,78},{16,80}... | collective-permute-start | bytes 49160 | tf_op jit(solution)/shard_map/ppermute | solution.py:39
  35.7 2.6 %collective-permute-done.5 = f32[4,1024]{1,0:T(4,128)S(1)} collective-permute-done((f32[4,1024]{1,0:T(4,128)S(1)}, f32[4,1024]{1,0:T(4,128)S(1)}, u32[]{:S(2)}, u32[]{:S(2)}) %collective-permute-start.5) | collective-permute-done | bytes 16416 | tf_op jit(solution)/shard_map/ppermute | solution.py:39
  40.9 3.9 %collective-permute-start.7 = (f32[2,1024]{1,0:T(2,128)S(1)}, f32[2,1024]{1,0:T(2,128)S(1)}, u32[]{:S(2)}, u32[]{:S(2)}) collective-permute-start(f32[2,1024]{1,0:T(2,128)S(1)} %get-tuple-element.110), channel_id=1, source_target_pairs={{0,2},{2,4},{4,6},{6,8},{8,10},{10,12},{12,14},{14,16},{16,18},{18... | collective-permute-start | bytes 24584 | tf_op jit(solution)/shard_map/ppermute | solution.py:39
  44.9 2.8 %pack_triangles.1 = (f32[128,1024]{1,0:T(8,128)S(1)}, f32[384,1024]{1,0:T(8,128)S(1)}, f32[384,1024]{1,0:T(8,128)S(1)}, f32[128,1024]{1,0:T(8,128)S(1)}, f32[8,1,128]{2,1,0:T(1,128)S(1)}) custom-call(f32[2,1,1024,1024]{3,2,1,0:T(8,128)} %held_ref.9), custom_call_target="tpu_custom_call" | custom-call | flops 1048576 | bytes 8388608 | tf_op jit(solution)/shard_map/pack_triangles/pallas_call | solution.py:103
  51.3 12.8 %collective-permute-start.11 = (f32[128,1024]{1,0:T(8,128)S(1)}, f32[128,1024]{1,0:T(8,128)S(1)}, u32[]{:S(2)}, u32[]{:S(2)}) collective-permute-start(f32[128,1024]{1,0:T(8,128)S(1)} %get-tuple-element.43), channel_id=1, source_target_pairs={{0,64},{2,66},{4,68},{6,70},{8,72},{10,74},{12,76},{14,78},{16,80}... | collective-permute-start | bytes 1572872 | tf_op jit(solution)/shard_map/ppermute | solution.py:39
  64.2 5.6 %weighted_sums.3 = (f32[2,1,1024]{2,1,0:T(1,128)S(1)}, f32[2,1,1024]{2,1,0:T(1,128)S(1)}) custom-call(s32[3]{0:T(128)S(1)} %add_convert_fusion.sc_ref, f32[2,1,1024,1024]{3,2,1,0:T(8,128)} %held_ref.9, f32[2,1,1024,1024]{3,2,1,0:T(8,128)} %held_ref.9, f32[2,1,1024,1024]{3,2,1,0:T(8,128)} %held_ref.9, f32[2,1,1024,1024]{3,2,1,0:T(8,128)} %held_ref.9, ...), custom_call_target="tpu_custom_call" | custom-call | flops 8388608 | bytes 8388608 | tf_op jit(solution)/shard_map/weighted_sums/pallas_call | solution.py:171
  71.1 5.8 %collective-permute-done.11.pk_ref = f32[128,1024]{1,0:T(8,128)S(1)} collective-permute-done((f32[128,1024]{1,0:T(8,128)S(1)}, f32[128,1024]{1,0:T(8,128)S(1)}, u32[]{:S(2)}, u32[]{:S(2)}) %collective-permute-start.11) | collective-permute-done | bytes 524320 | tf_op jit(solution)/shard_map/ppermute | solution.py:39
  77.8 5.4 %collective-permute-start.12 = (f32[8,1024]{1,0:T(8,128)S(1)}, f32[8,1024]{1,0:T(8,128)S(1)}, u32[]{:S(2)}, u32[]{:S(2)}) collective-permute-start(f32[8,1024]{1,0:T(8,128)S(1)} %concatenate.79), channel_id=1, source_target_pairs={{0,64},{2,66},{4,68},{6,70},{8,72},{10,74},{12,76},{14,78},{16,80}... | collective-permute-start | bytes 98312 | tf_op jit(solution)/shard_map/ppermute | solution.py:39
  83.2 2.3 %collective-permute-done.12 = f32[8,1024]{1,0:T(8,128)S(1)} collective-permute-done((f32[8,1024]{1,0:T(8,128)S(1)}, f32[8,1024]{1,0:T(8,128)S(1)}, u32[]{:S(2)}, u32[]{:S(2)}) %collective-permute-start.12) | collective-permute-done | bytes 32800 | tf_op jit(solution)/shard_map/ppermute | solution.py:39
  86.8 4.5 %collective-permute-start.14 = (f32[1,1024]{1,0:T(1,128)S(1)}, f32[1,1024]{1,0:T(1,128)S(1)}, u32[]{:S(2)}, u32[]{:S(2)}) collective-permute-start(f32[1,1024]{1,0:T(1,128)S(1)} %get-tuple-element.77), channel_id=1, source_target_pairs={{0,2},{2,4},{4,6},{6,8},{8,10},{10,12},{12,14},{14,16},{16,18},{18... | collective-permute-start | bytes 12296 | tf_op jit(solution)/shard_map/ppermute | solution.py:39
  91.4 4.6 %collective-permute-start.13 = (f32[1,384]{1,0:T(1,128)S(1)}, f32[1,384]{1,0:T(1,128)S(1)}, u32[]{:S(2)}, u32[]{:S(2)}) collective-permute-start(f32[1,384]{1,0:T(1,128)S(1)} %bitcast.72), channel_id=1, source_target_pairs={{0,32},{2,34},{4,36},{6,38},{8,40},{10,42},{12,44},{14,46},{16,48}... | collective-permute-start | bytes 4616 | tf_op jit(solution)/shard_map/ppermute | solution.py:39
  97.7 16.4 %collective-permute-start.17 = (f32[384,1024]{1,0:T(8,128)}, f32[384,1024]{1,0:T(8,128)S(1)}, u32[]{:S(2)}, u32[]{:S(2)}) collective-permute-start(f32[384,1024]{1,0:T(8,128)} %copy-done.3), channel_id=1, source_target_pairs={{0,64},{2,66},{4,68},{6,70},{8,72},{10,74},{12,76},{14,78},{16,80}... | collective-permute-start | bytes 4718600 | tf_op jit(solution)/shard_map/ppermute | solution.py:39
  116.6 3.5 %all-to-all-start = ((f32[16,1,384]{2,1,0:T(1,128)}), f32[16,1,384]{2,1,0:T(1,128)S(1)}, u32[]{:S(2)}, u32[]{:S(2)}) async-start(f32[16,1,384]{2,1,0:T(1,128)} %broadcast_in_dim.25), calls=%async_computation | async-start | bytes 49152 | tf_op jit(solution)/shard_map/all_to_all | solution.py:46
  120.1 5.4 %collective-permute-start.19 = (f32[128,1024]{1,0:T(8,128)}, f32[128,1024]{1,0:T(8,128)}, u32[]{:S(2)}, u32[]{:S(2)}) collective-permute-start(f32[128,1024]{1,0:T(8,128)} %copy-done.4), channel_id=1, source_target_pairs={{0,64},{2,66},{4,68},{6,70},{8,72},{10,74},{12,76},{14,78},{16,80}... | collective-permute-start | bytes 1572872 | tf_op jit(solution)/shard_map/ppermute | solution.py:39
  125.6 2.1 %all-to-all-done = f32[16,1,384]{2,1,0:T(1,128)S(1)} async-done(((f32[16,1,384]{2,1,0:T(1,128)}), f32[16,1,384]{2,1,0:T(1,128)S(1)}, u32[]{:S(2)}, u32[]{:S(2)}) %all-to-all-start) | async-done | bytes 24608 | tf_op jit(solution)/shard_map/all_to_all | solution.py:46
  134.2 3.0 %balance_ahead.1.rest_0_ = f32[2,1,1024,1024]{3,2,1,0:T(8,128)} custom-call(s32[3]{0:T(128)S(1)} %add_convert_fusion.sc_ref, f32[2,1,1024,1024]{3,2,1,0:T(8,128)} %collective-permute-done.got_ref, f32[2,1,1024,1024]{3,2,1,0:T(8,128)} %held_ref.9, f32[128,1024]{1,0:T(8,128)S(1)} %copy-done.1, f32[8,1,128]{2,1,0:T(1,128)S(1)} %bitcast.58, ...), custom_call_target="tpu_custom_call" | custom-call | flops 524288 | bytes 2097152 | tf_op jit(solution)/shard_map/balance_ahead/pallas_call | solution.py:290
  137.2 5.1 %balance_first.1.rest_0_ = f32[2,1,1024,1024]{3,2,1,0:T(8,128)} custom-call(s32[3]{0:T(128)S(1)} %add_convert_fusion.sc_ref, f32[2,1,1024,1024]{3,2,1,0:T(8,128)} %collective-permute-done.got_ref, f32[2,1,1024,1024]{3,2,1,0:T(8,128)} %held_ref.9, f32[384,1024]{1,0:T(8,128)S(1)} %collective-permute-done.17.pk_ref, ...), custom_call_target="tpu_custom_call", output_to_operand_aliasing={{}: (7, {})} | custom-call | flops 1572864 | bytes 6291456 | tf_op jit(solution)/shard_map/balance_first/pallas_call | solution.py:290
  142.3 7.2 %collective-permute-done.18.pk_ref = f32[384,1024]{1,0:T(8,128)S(1)} collective-permute-done((f32[384,1024]{1,0:T(8,128)}, f32[384,1024]{1,0:T(8,128)S(1)}, u32[]{:S(2)}, u32[]{:S(2)}) %collective-permute-start.18) | collective-permute-done | bytes 1572896 | tf_op jit(solution)/shard_map/ppermute | solution.py:39
  149.5 5.1 %balance_mid.1.rest_0_ = f32[2,1,1024,1024]{3,2,1,0:T(8,128)} custom-call(s32[3]{0:T(128)S(1)} %add_convert_fusion.sc_ref, f32[2,1,1024,1024]{3,2,1,0:T(8,128)} %collective-permute-done.got_ref, f32[2,1,1024,1024]{3,2,1,0:T(8,128)} %held_ref.9, f32[384,1024]{1,0:T(8,128)S(1)} %collective-permute-done.18.pk_ref, ...), custom_call_target="tpu_custom_call", output_to_operand_aliasing={{}: (7, {})} | custom-call | flops 1572864 | bytes 6291456 | tf_op jit(solution)/shard_map/balance_mid/pallas_call | solution.py:290
  155.2 3.2 %balance_last.1 = f32[2,1,1024,1024]{3,2,1,0:T(8,128)} custom-call(s32[3]{0:T(128)S(1)} %add_convert_fusion.sc_ref, f32[2,1,1024,1024]{3,2,1,0:T(8,128)} %collective-permute-done.got_ref, f32[2,1,1024,1024]{3,2,1,0:T(8,128)} %held_ref.9, f32[128,1024]{1,0:T(8,128)} %collective-permute-done.19.pk_ref, ...), custom_call_target="tpu_custom_call", output_to_operand_aliasing={{}: (7, {})} | custom-call | flops 524288 | bytes 2097152 | tf_op jit(solution)/shard_map/balance_last/pallas_call | solution.py:290
  (89 shorter events, 25.0 us)
Async XLA Ops:
  0.6 132.5 %collective-permute-start = (f32[2,1,1024,1024]{3,2,1,0:T(8,128)}, f32[2,1,1024,1024]{3,2,1,0:T(8,128)}, u32[]{:S(2)}, u32[]{:S(2)}) collective-permute-start(f32[2,1,1024,1024]{3,2,1,0:T(8,128)} %held_ref.9), channel_id=1, source_target_pairs={{1,65},{3,67},{5,69},{7,71},{9,73},{11,75},{13,77},{15,79},{17,81}... | collective-permute-start | bytes 25165832 | tf_op jit(solution)/shard_map/ppermute | solution.py:39
  5.3 5.5 %collective-permute-start.1 = (f32[1,1024]{1,0:T(1,128)S(1)}, f32[1,1024]{1,0:T(1,128)S(1)}, u32[]{:S(2)}, u32[]{:S(2)}) collective-permute-start(f32[1,1024]{1,0:T(1,128)S(1)} %bitcast.71), channel_id=1, source_target_pairs={{2,0},{4,2},{6,4},{8,6},{10,8},{12,10},{14,12},{16,14},{18,16},{20... | collective-permute-start | bytes 12296 | tf_op jit(solution)/shard_map/ppermute | solution.py:39
  10.8 11.8 %collective-permute-start.2 = (f32[3,1024]{1,0:T(4,128)S(1)}, f32[3,1024]{1,0:T(4,128)S(1)}, u32[]{:S(2)}, u32[]{:S(2)}) collective-permute-start(f32[3,1024]{1,0:T(4,128)S(1)} %pad_maximum_fusion.1), channel_id=1, source_target_pairs={{0,64},{2,66},{4,68},{6,70},{8,72},{10,74},{12,76},{14,78},{16,80}... | collective-permute-start | bytes 36872 | tf_op jit(solution)/shard_map/ppermute | solution.py:39
  22.6 1.3 collective-permute-start.3
  29.6 1.3 collective-permute-start.4
  30.9 7.4 %collective-permute-start.5 = (f32[4,1024]{1,0:T(4,128)S(1)}, f32[4,1024]{1,0:T(4,128)S(1)}, u32[]{:S(2)}, u32[]{:S(2)}) collective-permute-start(f32[4,1024]{1,0:T(4,128)S(1)} %pad_maximum_fusion.4), channel_id=1, source_target_pairs={{0,64},{2,66},{4,68},{6,70},{8,72},{10,74},{12,76},{14,78},{16,80}... | collective-permute-start | bytes 49160 | tf_op jit(solution)/shard_map/ppermute | solution.py:39
  38.3 12.4 %collective-permute-start.8 = (f32[2,1024]{1,0:T(2,128)S(1)}, f32[2,1024]{1,0:T(2,128)S(1)}, u32[]{:S(2)}, u32[]{:S(2)}) collective-permute-start(f32[2,1024]{1,0:T(2,128)S(1)} %get-tuple-element.108), channel_id=1, source_target_pairs={{2,0},{4,2},{6,4},{8,6},{10,8},{12,10},{14,12},{16,14},{18,16},{20... | collective-permute-start | bytes 24584 | tf_op jit(solution)/shard_map/ppermute | solution.py:39
  39.6 11.4 %collective-permute-start.6 = (f32[2,1024]{1,0:T(2,128)S(1)}, f32[2,1024]{1,0:T(2,128)S(1)}, u32[]{:S(2)}, u32[]{:S(2)}) collective-permute-start(f32[2,1024]{1,0:T(2,128)S(1)} %get-tuple-element.109), channel_id=1, source_target_pairs={{62,0},{64,126}} | collective-permute-start | bytes 24584 | tf_op jit(solution)/shard_map/ppermute | solution.py:39
  40.9 10.1 %collective-permute-start.7 = (f32[2,1024]{1,0:T(2,128)S(1)}, f32[2,1024]{1,0:T(2,128)S(1)}, u32[]{:S(2)}, u32[]{:S(2)}) collective-permute-start(f32[2,1024]{1,0:T(2,128)S(1)} %get-tuple-element.110), channel_id=1, source_target_pairs={{0,2},{2,4},{4,6},{6,8},{8,10},{10,12},{12,14},{14,16},{16,18},{18... | collective-permute-start | bytes 24584 | tf_op jit(solution)/shard_map/ppermute | solution.py:39
  47.6 1.2 copy-start.2
  48.8 1.1 copy-start.3
  51.2 12.9 %collective-permute-start.9 = (f32[4,1024]{1,0:T(4,128)S(1)}, f32[4,1024]{1,0:T(4,128)S(1)}, u32[]{:S(2)}, u32[]{:S(2)}) collective-permute-start(f32[4,1024]{1,0:T(4,128)S(1)} %pad_maximum_fusion.5), channel_id=1, source_target_pairs={{0,1},{2,3},{4,5},{6,7},{8,9},{10,11},{12,13},{14,15},{16,17},{18,... | collective-permute-start | bytes 49160 | tf_op jit(solution)/shard_map/ppermute | solution.py:53
  51.3 25.6 %collective-permute-start.11 = (f32[128,1024]{1,0:T(8,128)S(1)}, f32[128,1024]{1,0:T(8,128)S(1)}, u32[]{:S(2)}, u32[]{:S(2)}) collective-permute-start(f32[128,1024]{1,0:T(8,128)S(1)} %get-tuple-element.43), channel_id=1, source_target_pairs={{0,64},{2,66},{4,68},{6,70},{8,72},{10,74},{12,76},{14,78},{16,80}... | collective-permute-start | bytes 1572872 | tf_op jit(solution)/shard_map/ppermute | solution.py:39
  64.1 67.2 %copy-start.5 = (f32[2048]{0:T(1024)S(1)}, f32[2048]{0:T(1024)}, u32[]{:S(2)}) copy-start(f32[2048]{0:T(1024)} %param.7) | copy-start | bytes 24580
  69.8 1.3 collective-permute-start.10
  77.8 7.7 %collective-permute-start.12 = (f32[8,1024]{1,0:T(8,128)S(1)}, f32[8,1024]{1,0:T(8,128)S(1)}, u32[]{:S(2)}, u32[]{:S(2)}) collective-permute-start(f32[8,1024]{1,0:T(8,128)S(1)} %concatenate.79), channel_id=1, source_target_pairs={{0,64},{2,66},{4,68},{6,70},{8,72},{10,74},{12,76},{14,78},{16,80}... | collective-permute-start | bytes 98312 | tf_op jit(solution)/shard_map/ppermute | solution.py:39
  85.5 12.2 %collective-permute-start.15 = (f32[1,1024]{1,0:T(1,128)S(1)}, f32[1,1024]{1,0:T(1,128)S(1)}, u32[]{:S(2)}, u32[]{:S(2)}) collective-permute-start(f32[1,1024]{1,0:T(1,128)S(1)} %get-tuple-element.76), channel_id=1, source_target_pairs={{2,0},{4,2},{6,4},{8,6},{10,8},{12,10},{14,12},{16,14},{18,16},{20... | collective-permute-start | bytes 12296 | tf_op jit(solution)/shard_map/ppermute | solution.py:39
  86.8 10.9 %collective-permute-start.14 = (f32[1,1024]{1,0:T(1,128)S(1)}, f32[1,1024]{1,0:T(1,128)S(1)}, u32[]{:S(2)}, u32[]{:S(2)}) collective-permute-start(f32[1,1024]{1,0:T(1,128)S(1)} %get-tuple-element.77), channel_id=1, source_target_pairs={{0,2},{2,4},{4,6},{6,8},{8,10},{10,12},{12,14},{14,16},{16,18},{18... | collective-permute-start | bytes 12296 | tf_op jit(solution)/shard_map/ppermute | solution.py:39
  91.4 6.2 %collective-permute-start.13 = (f32[1,384]{1,0:T(1,128)S(1)}, f32[1,384]{1,0:T(1,128)S(1)}, u32[]{:S(2)}, u32[]{:S(2)}) collective-permute-start(f32[1,384]{1,0:T(1,128)S(1)} %bitcast.72), channel_id=1, source_target_pairs={{0,32},{2,34},{4,36},{6,38},{8,40},{10,42},{12,44},{14,46},{16,48}... | collective-permute-start | bytes 4616 | tf_op jit(solution)/shard_map/ppermute | solution.py:39
  97.7 39.5 %collective-permute-start.17 = (f32[384,1024]{1,0:T(8,128)}, f32[384,1024]{1,0:T(8,128)S(1)}, u32[]{:S(2)}, u32[]{:S(2)}) collective-permute-start(f32[384,1024]{1,0:T(8,128)} %copy-done.3), channel_id=1, source_target_pairs={{0,64},{2,66},{4,68},{6,70},{8,72},{10,74},{12,76},{14,78},{16,80}... | collective-permute-start | bytes 4718600 | tf_op jit(solution)/shard_map/ppermute | solution.py:39
  114.0 35.4 %collective-permute-start.18 = (f32[384,1024]{1,0:T(8,128)}, f32[384,1024]{1,0:T(8,128)S(1)}, u32[]{:S(2)}, u32[]{:S(2)}) collective-permute-start(f32[384,1024]{1,0:T(8,128)} %copy-done.2), channel_id=1, source_target_pairs={{0,64},{2,66},{4,68},{6,70},{8,72},{10,74},{12,76},{14,78},{16,80}... | collective-permute-start | bytes 4718600 | tf_op jit(solution)/shard_map/ppermute | solution.py:39
  116.6 11.0 %all-to-all-start = ((f32[16,1,384]{2,1,0:T(1,128)}), f32[16,1,384]{2,1,0:T(1,128)S(1)}, u32[]{:S(2)}, u32[]{:S(2)}) async-start(f32[16,1,384]{2,1,0:T(1,128)} %broadcast_in_dim.25), calls=%async_computation | async-start | bytes 49152 | tf_op jit(solution)/shard_map/all_to_all | solution.py:46
  120.1 35.1 %collective-permute-start.19 = (f32[128,1024]{1,0:T(8,128)}, f32[128,1024]{1,0:T(8,128)}, u32[]{:S(2)}, u32[]{:S(2)}) collective-permute-start(f32[128,1024]{1,0:T(8,128)} %copy-done.4), channel_id=1, source_target_pairs={{0,64},{2,66},{4,68},{6,70},{8,72},{10,74},{12,76},{14,78},{16,80}... | collective-permute-start | bytes 1572872 | tf_op jit(solution)/shard_map/ppermute | solution.py:39
  131.2 1.3 collective-permute-start.16
  (3 other events, 2.6 us)

commit v3 on v2

--- a/solution.py
+++ b/solution.py
@@ -62,7 +62,7 @@
 
 
 BLOCKS = [(0, 0), (0, 1), (0, 2), (0, 3), (1, 1), (1, 2), (1, 3), (1, 0)]
-SENT = (1, 3, 3, 1)
+SENT = (3, 4, 1)
 
 
 def pack_kernel(held_ref, *refs):
@@ -118,35 +118,33 @@
     )(held)
 
 
-STREAMS = 4
-ROWS = STREAMS * LANE
-
-
-def sums_kernel(sc_ref, *refs):
-    x_refs, (a_ref, b_ref, row_ref, col_ref, acc_ref) = refs[:STREAMS], refs[STREAMS:]
-    i = pl.program_id(1)
+def sums_kernel(sc_ref, held_ref, a_ref, b_ref, row_ref, col_ref, buf, sem):
     rows, cols = iotas()
-    ahead = cols - rows
-
-    @pl.when(i == 0)
-    def _():
-        acc_ref[...] = jnp.zeros_like(acc_ref)
-
-    def add_up(masked):
-        for r in range(STREAMS):
-            a_line = a_ref[0, :, lanes(r)]
-            a_col = as_column(a_line)
-            start = i * ROWS + r * LANE
-            across = jnp.zeros((LANE, LANE), F32)
+
+    def add_up(triangle):
+        copies = []
+        for n in range(16):
+            t, b = n // 8, n % 8
+            near = pl.ds(b * LANE, LANE)
+            kept = pl.ds(b * LANE, (8 - b) * LANE) if triangle else pl.ds(0, 1024)
+            copies.append(pltpu.make_async_copy(held_ref.at[t, 0, near, kept], buf.at[t, near, kept], sem.at[n]))
+            copies[-1].start()
+        for t in range(2):
+            below = [jnp.zeros((8, LANE), F32) for _ in range(8)]
+            for b in range(8):
+                copies[8 * t + b].wait()
+                a_line = a_ref[t, :, lanes(b)]
+                a_col = as_column(a_line)
+                across = jnp.zeros((LANE, LANE), F32)
+                for k in range(b if triangle else 0, 8):
+                    right = down = buf[t, pl.ds(b * LANE, LANE), lanes(k)]
+                    if triangle and k == b:
+                        right, down = jnp.where(cols >= rows, right, 0.0), jnp.where(cols > rows, down, 0.0)
+                    across += right * b_ref[t, :, lanes(k)]
+                    below[k] += jnp.sum((down * a_col).reshape(LANE // 8, 8, LANE), axis=0)
+                row_ref[t, :, lanes(b)] = jnp.sum(across.T, axis=0, keepdims=True) * a_line
             for k in range(8):
-                x = x_refs[r][0, 0, :, lanes(k)]
-                right = down = x
-                if masked:
-                    shift = start - k * LANE
-                    right, down = jnp.where(ahead >= shift, x, 0.0), jnp.where(ahead > shift, x, 0.0)
-                across += right * b_ref[0, :, lanes(k)]
-                acc_ref[:, lanes(k)] += jnp.sum((down * a_col).reshape(LANE // 8, 8, LANE), axis=0)
-            row_ref[0, :, lanes(r)] = jnp.sum(across.T, axis=0, keepdims=True) * a_line
+                col_ref[t, :, lanes(k)] = jnp.sum(below[k], axis=0, keepdims=True) * b_ref[t, :, lanes(k)]
 
     @pl.when(sc_ref[0] == 1)
     def _():
@@ -156,149 +154,124 @@
     def _():
         add_up(False)
 
-    @pl.when(i == pl.num_programs(1) - 1)
-    def _():
-        col_ref[0] = jnp.sum(acc_ref[...], axis=0, keepdims=True) * b_ref[0]
-
 
 def weighted_sums(scalars, held, row_w, col_w):
-    steps = 1024 // ROWS
     shape = jax.ShapeDtypeStruct((2, 1, 1024), F32)
-
-    def stream(r):
-        return pl.BlockSpec((1, 1, LANE, 1024), lambda t, i, sc: (t, 0, STREAMS * i + r, 0))
-
+    here = pl.BlockSpec(memory_space=pltpu.VMEM)
     row_part, col_part = pl.pallas_call(
         sums_kernel,
-        grid_spec=pltpu.PrefetchScalarGridSpec(
-            num_scalar_prefetch=1,
-            grid=(2, steps),
-            in_specs=[stream(r) for r in range(STREAMS)]
-            + [
-                pl.BlockSpec((1, 1, ROWS), lambda t, i, sc: (t, 0, i)),
-                pl.BlockSpec((1, 1, 1024), lambda t, i, sc: (t, 0, 0)),
-            ],
-            out_specs=[
-                pl.BlockSpec((1, 1, ROWS), lambda t, i, sc: (t, 0, i)),
-                pl.BlockSpec((1, 1, 1024), lambda t, i, sc: (t, 0, 0)),
-            ],
-            scratch_shapes=[pltpu.VMEM((8, 1024), F32)],
-        ),
+        in_specs=[pl.BlockSpec(memory_space=pltpu.SMEM), pl.BlockSpec(memory_space=pl.ANY), here, here],
+        out_specs=[here, here],
         out_shape=[shape, shape],
+        scratch_shapes=[pltpu.VMEM((2, 1024, 1024), F32), pltpu.SemaphoreType.DMA((16,))],
         compiler_params=pltpu.CompilerParams(vmem_limit_bytes=VMEM_LIMIT),
         cost_estimate=pl.CostEstimate(flops=8 << 20, bytes_accessed=8 << 20, transcendentals=0),
         name="weighted_sums",
-    )(scalars, *[held] * STREAMS, row_w.reshape(2, 1, 1024), col_w.reshape(2, 1, 1024))
+    )(scalars, held, row_w.reshape(2, 1, 1024), col_w.reshape(2, 1, 1024))
     return row_part.reshape(2, 1024), col_part.reshape(2, 1024)
 
 
-def ahead_place(i):
-    return 0, 0, jnp.where(i == 0, 0, 7)
-
-
-def first_place(i):
-    k = i // 2 + 1
-    return 0, k, jnp.where(i % 2 == 0, k, 7 - k)
-
-
-def mid_place(i):
-    k = i // 2 + 1
-    return 1, k, jnp.where(i % 2 == 0, k, 7 - k)
-
-
-def last_place(i):
-    return 1, 0, jnp.where(i == 0, 0, 7)
-
-
-def balance_kernel(place, sc_ref, got_ref, held_ref, pk_ref, dv_ref, wr_ref, wc_ref, *rest):
-    out_ref = rest[-1]
-    t, k_now, b = place(pl.program_id(0))
+def balance_kernel(t, ks, base, sc_ref, got_ref, held_ref, pk_ref, dv_ref, wr_ref, wc_ref, *rest):
+    out_ref, buf, pk_buf, in_sem, out_sem = rest[-5:]
     rows, cols = iotas()
     on_diagonal = sc_ref[0] == 1
     moved = sc_ref[1 + t] == 1
-    w_col = as_column(wr_ref[0])
-
-    def put(j, x):
-        out_ref[0, 0, :, lanes(j)] = x * w_col * wc_ref[0, :, lanes(j)]
+    blocks = [b for k in ks for b in (k, 7 - k)]
+
+    def place(ref, b):
+        return ref.at[t, 0, pl.ds(b * LANE, LANE), :]
+
+    def put(i, b, w_col, j, x):
+        buf[i, :, lanes(j)] = x * w_col * wc_ref[t, :, lanes(j)]
+
+    def send(i, b):
+        copy = pltpu.make_async_copy(buf.at[i], place(out_ref, b), out_sem.at[i])
+        copy.start()
+        return copy
+
+    def from_rows(ref, masked):
+        loads = [pltpu.make_async_copy(place(ref, b), buf.at[i], in_sem.at[i]) for i, b in enumerate(blocks)]
+        for copy in loads:
+            copy.start()
+        stores = []
+        for i, b in enumerate(blocks):
+            loads[i].wait()
+            w_col = as_column(wr_ref[t * 8 + b])
+            for j in range(8):
+                x = buf[i, :, lanes(j)]
+                put(i, b, w_col, j, jnp.where(cols - rows >= (b - j) * LANE, x, 0.0) if masked else x)
+            stores.append(send(i, b))
+        for copy in stores:
+            copy.wait()
 
     @pl.when(moved & jnp.logical_not(on_diagonal))
     def _():
-        for j in range(8):
-            put(j, got_ref[0, 0, :, lanes(j)])
-
-    @pl.when(jnp.logical_not(moved))
-    def _():
-        least = jnp.where(on_diagonal, 0, -4096) + b * LANE
-        for j in range(8):
-            put(j, jnp.where(cols - rows >= least - j * LANE, held_ref[0, 0, :, lanes(j)], 0.0))
-
-    for k in range(4):
-        @pl.when(moved & on_diagonal & (k_now == k) & (b == k))
-        def _():
+        from_rows(got_ref, False)
+
+    @pl.when(jnp.logical_not(moved) & jnp.logical_not(on_diagonal))
+    def _():
+        from_rows(held_ref, False)
+
+    @pl.when(jnp.logical_not(moved) & on_diagonal)
+    def _():
+        from_rows(held_ref, True)
+
+    @pl.when(moved & on_diagonal)
+    def _():
+        loads = [
+            pltpu.make_async_copy(pk_ref.at[pl.ds((base + n) * LANE, LANE), :], pk_buf.at[n], in_sem.at[n])
+            for n in range(len(ks))
+        ]
+        for copy in loads:
+            copy.start()
+        stores = []
+        for n, k in enumerate(ks):
+            loads[n].wait()
+            near, far = 2 * n, 2 * n + 1
+            w_col = as_column(wr_ref[t * 8 + k])
             for j in range(k):
-                out_ref[0, 0, :, lanes(j)] = jnp.zeros((LANE, LANE), F32)
-            put(k, jnp.where(cols >= rows, pk_ref[:, lanes(k)], 0.0))
+                buf[near, :, lanes(j)] = jnp.zeros((LANE, LANE), F32)
+            put(near, k, w_col, k, jnp.where(cols >= rows, pk_buf[n, :, lanes(k)], 0.0))
             for j in range(k + 1, 8):
-                put(j, pk_ref[:, lanes(j)])
-
-        @pl.when(moved & on_diagonal & (k_now == k) & (b == 7 - k))
-        def _():
+                put(near, k, w_col, j, pk_buf[n, :, lanes(j)])
+            stores.append(send(near, k))
+            w_col = as_column(wr_ref[t * 8 + 7 - k])
             for j in range(7 - k):
-                out_ref[0, 0, :, lanes(j)] = jnp.zeros((LANE, LANE), F32)
-            far = pk_ref[:, lanes(k)].T
-            put(7 - k, jnp.where(cols > rows, far, jnp.where(cols == rows, dv_ref[0], 0.0)))
+                buf[far, :, lanes(j)] = jnp.zeros((LANE, LANE), F32)
+            diagonal = dv_ref[BLOCKS.index((t, k))]
+            block = jnp.where(cols > rows, pk_buf[n, :, lanes(k)].T, jnp.where(cols == rows, diagonal, 0.0))
+            put(far, 7 - k, w_col, 7 - k, block)
             for j in range(k):
-                put(8 - k + j, pk_ref[:, lanes(j)])
-
-
-def balance(name, place, steps, first_k, scalars, got, held, packed, dv, wr, wc, into=None):
-    tile = (1, 1, LANE, 1024)
-
-    def got_at(i, sc):
-        t, _, b = place(i)
-        use = (sc[0] == 0) & (sc[1 + t] == 1)
-        return (jnp.where(use, t, 0), 0, jnp.where(use, b, 0), 0)
-
-    def held_at(i, sc):
-        t, _, b = place(i)
-        use = sc[1 + t] == 0
-        return (jnp.where(use, t, 0), 0, jnp.where(use, b, 0), 0)
-
-    def packed_at(i, sc):
-        t, k, _ = place(i)
-        use = (sc[0] == 1) & (sc[1 + t] == 1)
-        return (jnp.where(use, k - first_k, 0), 0)
-
-    def dv_at(i, sc):
-        t, k, _ = place(i)
-        return (k if t == 0 else jnp.where(k == 0, 7, 3 + k), 0, 0)
-
-    in_specs = [
-        pl.BlockSpec(tile, got_at),
-        pl.BlockSpec(tile, held_at),
-        pl.BlockSpec((LANE, 1024), packed_at),
-        pl.BlockSpec((1, 1, LANE), dv_at),
-        pl.BlockSpec((1, 1, LANE), lambda i, sc: (place(i)[0] * 8 + place(i)[2], 0, 0)),
-        pl.BlockSpec((1, 1, 1024), lambda i, sc: (place(i)[0], 0, 0)),
-    ]
+                put(far, 7 - k, w_col, 8 - k + j, pk_buf[n, :, lanes(j)])
+            stores.append(send(far, 7 - k))
+        for copy in stores:
+            copy.wait()
+
+
+def balance(name, t, ks, scalars, got, held, packed, dv, wr, wc, into=None, base=0):
+    here, anywhere = pl.BlockSpec(memory_space=pltpu.VMEM), pl.BlockSpec(memory_space=pl.ANY)
     args = [scalars, got, held, packed, dv, wr, wc]
+    in_specs = [pl.BlockSpec(memory_space=pltpu.SMEM), anywhere, anywhere, anywhere, here, here, here]
     aliases = {}
     if into is not None:
-        in_specs.append(pl.BlockSpec(memory_space=pl.ANY))
+        aliases = {len(args): 0}
+        in_specs.append(anywhere)
         args.append(into)
-        aliases = {len(args) - 1: 0}
+    count = 2 * len(ks)
     return pl.pallas_call(
-        functools.partial(balance_kernel, place),
-        grid_spec=pltpu.PrefetchScalarGridSpec(
-            num_scalar_prefetch=1,
-            grid=(steps,),
-            in_specs=in_specs,
-            out_specs=pl.BlockSpec(tile, lambda i, sc: (place(i)[0], 0, place(i)[2], 0)),
-        ),
+        functools.partial(balance_kernel, t, ks, base),
+        in_specs=in_specs,
+        out_specs=anywhere,
         out_shape=jax.ShapeDtypeStruct(held.shape, F32),
+        scratch_shapes=[
+            pltpu.VMEM((count, LANE, 1024), F32),
+            pltpu.VMEM((len(ks), LANE, 1024), F32),
+            pltpu.SemaphoreType.DMA((count,)),
+            pltpu.SemaphoreType.DMA((count,)),
+        ],
         input_output_aliases=aliases,
         compiler_params=pltpu.CompilerParams(vmem_limit_bytes=VMEM_LIMIT),
-        cost_estimate=pl.CostEstimate(flops=steps << 18, bytes_accessed=steps << 20, transcendentals=0),
+        cost_estimate=pl.CostEstimate(flops=count << 18, bytes_accessed=count << 20, transcendentals=0),
         name=name,
     )(*args)
 
@@ -310,7 +283,7 @@
     scalars = jnp.concatenate([on_diagonal.astype(jnp.int32)[None], (placed == 1).astype(jnp.int32)])
 
     got = move["tiles"](held_tiles)
-    ahead, first, mid, last, dv = pack(held_tiles)
+    ahead, most, last, dv = pack(held_tiles)
 
     here = lax.axis_index("bins")
     there = here ^ (lax.axis_size("bins") // 2)
@@ -352,30 +325,31 @@
     after_live = move["before"](live[:1])
     live_lines = jnp.concatenate([live, after_live], axis=0)
     live_lines = jnp.concatenate([live_lines, move["across"](live_lines)], axis=0)
+    live_lines, ahead = lax.optimization_barrier((live_lines, ahead))
+    ahead = move["across"](ahead)
 
     rows, cols = stored_parts(live_lines)
+    rows, cols, ahead = lax.optimization_barrier((rows, cols, ahead))
     line_1 = rows[:1] + rows[1:] + cols[:1] + cols[1:]
     mine = jnp.concatenate([rows, cols], axis=0)
     parts = home_sums(mine, move["across"](mine))
     ends = move["ends"](jnp.concatenate([parts[2][1], parts[0][0]], axis=0))
-    ends, cols_before, rows_after, ahead = lax.optimization_barrier((ends, *neighbours(parts, 2), ahead))
-    ahead = move["across"](ahead)
+    ends, cols_before, rows_after = lax.optimization_barrier((ends, *neighbours(parts, 2)))
     cols_before = [cols_before[0:1], jnp.where(here == 0, ends[0:1], cols_before[1:2])]
     rows_after = [rows_after[0:1], jnp.where(there == lax.axis_size("bins") // 2 - 1, ends[1:2], rows_after[1:2])]
     sums_1 = jnp.concatenate([sums_of(parts, 0, cols_before[0], rows_after[0]), sums_of(parts, 1, cols_before[1], rows_after[1])], axis=0)
 
     rows, cols = stored_parts(jnp.where(live_lines > 0, 1.0 / sums_1, 0.0))
-    rows, cols, ahead = lax.optimization_barrier((rows, cols, ahead))
     totals = [line_1, rows[:1] + rows[1:] + cols[:1] + cols[1:], live[:1] + live[1:]]
     mine = jnp.concatenate([rows, cols, *totals, dv.reshape(1, 1024)], axis=0)
     theirs = move["across"](mine)
     parts = home_sums(mine, theirs)
     dv = theirs[7:8].reshape(8, 1, LANE)
     totals = jnp.sum((mine[4:7] + theirs[4:7]).reshape(3, 8, LANE), axis=1).reshape(1, 3 * LANE)
-    beside, *around, first, mid, last = lax.optimization_barrier(
-        (move["beside"](totals), *neighbours(parts, 1), first, mid, last)
+    beside, *around, most, last = lax.optimization_barrier(
+        (move["beside"](totals), *neighbours(parts, 1), most, last)
     )
-    first, mid, last = move["across"](first), move["across"](mid), move["across"](last)
+    most, last = move["across"](most), move["across"](last)
     totals = move["plane_sum"](totals + beside)
     sums_2 = sums_of(parts, 0, *around)
     totals = jnp.sum(totals.reshape(3, LANE), axis=1)
@@ -391,13 +365,12 @@
     wc = jnp.where(on_diagonal, result[:2], result[1:3]).reshape(2, 1, 1024)
 
     got, ahead, wr, wc, dv = lax.optimization_barrier((got, ahead, wr, wc, dv))
-    out = balance("balance_ahead", ahead_place, 2, 0, scalars, got, held_tiles, ahead, dv, wr, wc)
-    out, first = lax.optimization_barrier((out, first))
-    out = balance("balance_first", first_place, 6, 1, scalars, got, held_tiles, first, dv, wr, wc, into=out)
-    out, mid = lax.optimization_barrier((out, mid))
-    out = balance("balance_mid", mid_place, 6, 1, scalars, got, held_tiles, mid, dv, wr, wc, into=out)
+    out = balance("balance_ahead", 0, (0, 1, 2), scalars, got, held_tiles, ahead, dv, wr, wc)
+    out, most = lax.optimization_barrier((out, most))
+    out = balance("balance_most", 0, (3,), scalars, got, held_tiles, most, dv, wr, wc, into=out)
+    out = balance("balance_rest", 1, (1, 2, 3), scalars, got, held_tiles, most, dv, wr, wc, into=out, base=1)
     out, last = lax.optimization_barrier((out, last))
-    out = balance("balance_last", last_place, 2, 0, scalars, got, held_tiles, last, dv, wr, wc, into=out)
+    out = balance("balance_last", 1, (0,), scalars, got, held_tiles, last, dv, wr, wc, into=out)
     return out, bias_out.reshape(2048)
 
 

time: 160 us -> 156 us (0.975)
  waiting for transfers between devices: 31.3 us -> 60.7 us
  starting transfers between devices: 82 us -> 63.7 us
  Pallas kernels: 30.4 us -> 18.7 us
  local copies, waits for them, and re-layouts: 8.26 us -> 6.26 us
    ppermute x15 -> x14, waiting for transfers between devices: 24.6 us -> 52.4 us  [move(): return lambda value: lax.ppermute(value, AXES, pairs)]
    ppermute x15 -> x14, starting transfers between devices: 78.1 us -> 58.3 us  [move(): return lambda value: lax.ppermute(value, AXES, pairs)]
    pallas_call x6, Pallas kernels: 27.6 us -> 15.9 us  [the longest x4 8.69 us: balance(): pl.pallas_call(functools.partial(balance_kernel, t, ks, base), in_specs=i...]
  transfers between devices with their start and end apart: 21 -> 20, of which waited for: 13 -> 14; matrix products, arithmetic and copies ran while one was open for 3% -> 3% of each run, Pallas kernels for 17% -> 11%
where the time goes in v3:
time: 156 us; the launch traced here: 155 us
  starting transfers between devices  63.7 us (41%)
  waiting for transfers between devices  60.7 us (39%)
  Pallas kernels  18.7 us (12%)
  local copies, waits for them, and re-layouts  6.26 us (4%)
  between operations  4.45 us (3%)
    ppermute x14, starting transfers between devices, move(): return lambda value: lax.ppermute(value, AXES, pairs)  58.3 us
    ppermute x14, waiting for transfers between devices, move(): return lambda value: lax.ppermute(value, AXES, pairs)  52.4 us
    pallas_call x4, Pallas kernels, balance(): pl.pallas_call(functools.partial(balance_kernel, t, ks, base), in_specs=i...  8.69 us
    pallas_call x2, Pallas kernels, weighted_sums(): pl.pallas_call(sums_kernel, in_specs=[pl.BlockSpec(memory_space=pltpu.SME...  7.23 us
    ppermute x5, waiting for transfers between devices, moves(): lax.ppermute(value, AXES, both_ways)  5.11 us
    unnamed x17, local copies, waits for them, and re-layouts  4.21 us
    all_to_all x1, starting transfers between devices, plane_sum(): lax.all_to_all(spread, 'bins', 0, 0, axis_index_groups=planes, tiled=True)  3.48 us
    all_to_all x1, waiting for transfers between devices, plane_sum(): lax.all_to_all(spread, 'bins', 0, 0, axis_index_groups=planes, tiled=True)  3.25 us
  transfers between devices with their start and end apart: 20, of which 14 were waited for; matrix products, arithmetic and copies ran while one was open for 3% of the time, Pallas kernels for 11%

profile of v3, /device:TPU:0, one launch (start us, length us, event | category | flops | bytes accessed | tf_op | source)
XLA Modules:
  0.0 155.3 jit_solution(1279009421927090061)
XLA Ops:
  0.6 3.9 %collective-permute-start = (f32[2,1,1024,1024]{3,2,1,0:T(8,128)}, f32[2,1,1024,1024]{3,2,1,0:T(8,128)}, u32[]{:S(2)}, u32[]{:S(2)}) collective-permute-start(f32[2,1,1024,1024]{3,2,1,0:T(8,128)} %held_ref.13), channel_id=1, source_target_pairs={{1,65},{3,67},{5,69},{7,71},{9,73},{11,75},{13,77},{15,79},{17,81}... | collective-permute-start | bytes 25165832 | tf_op jit(solution)/shard_map/ppermute | solution.py:39
  6.6 4.2 %collective-permute-done.1 = f32[1,1024]{1,0:T(1,128)S(1)} collective-permute-done((f32[1,1024]{1,0:T(1,128)S(1)}, f32[1,1024]{1,0:T(1,128)S(1)}, u32[]{:S(2)}, u32[]{:S(2)}) %collective-permute-start.1) | collective-permute-done | bytes 4128 | tf_op jit(solution)/shard_map/ppermute | solution.py:39
  10.8 9.2 %collective-permute-start.2 = (f32[3,1024]{1,0:T(4,128)S(1)}, f32[3,1024]{1,0:T(4,128)S(1)}, u32[]{:S(2)}, u32[]{:S(2)}) collective-permute-start(f32[3,1024]{1,0:T(4,128)S(1)} %pad_maximum_fusion.2), channel_id=1, source_target_pairs={{0,64},{2,66},{4,68},{6,70},{8,72},{10,74},{12,76},{14,78},{16,80}... | collective-permute-start | bytes 36872 | tf_op jit(solution)/shard_map/ppermute | solution.py:39
  20.0 2.8 %pack_triangles.1 = (f32[384,1024]{1,0:T(8,128)S(1)}, f32[512,1024]{1,0:T(8,128)S(1)}, f32[128,1024]{1,0:T(8,128)S(1)}, f32[8,1,128]{2,1,0:T(1,128)S(1)}) custom-call(f32[2,1,1024,1024]{3,2,1,0:T(8,128)} %held_ref.13), custom_call_target="tpu_custom_call" | custom-call | flops 1048576 | bytes 8388608 | tf_op jit(solution)/shard_map/pack_triangles/pallas_call | solution.py:103
  25.0 2.4 %collective-permute-start.5 = (f32[384,1024]{1,0:T(8,128)S(1)}, f32[384,1024]{1,0:T(8,128)S(1)}, u32[]{:S(2)}, u32[]{:S(2)}) collective-permute-start(f32[384,1024]{1,0:T(8,128)S(1)} %get-tuple-element.36), channel_id=1, source_target_pairs={{0,64},{2,66},{4,68},{6,70},{8,72},{10,74},{12,76},{14,78},{16,80}... | collective-permute-start | bytes 4718600 | tf_op jit(solution)/shard_map/ppermute | solution.py:39
  30.0 3.6 %weighted_sums.2 = (f32[2,1,1024]{2,1,0:T(1,128)S(1)}, f32[2,1,1024]{2,1,0:T(1,128)S(1)}) custom-call(s32[3]{0:T(128)S(1)} %add_convert_fusion.sc_ref, f32[2,1,1024,1024]{3,2,1,0:T(8,128)} %held_ref.13, f32[2,1,1024]{2,1,0:T(1,128)S(1)} %copy.33.a_ref, f32[2,1,1024]{2,1,0:T(1,128)S(1)} %copy.34.b_ref), custom_call_target="tpu_custom_call" | custom-call | flops 8388608 | bytes 8388608 | tf_op jit(solution)/shard_map/weighted_sums/pallas_call | solution.py:161
  35.4 30.3 %collective-permute-done.5.pk_ref = f32[384,1024]{1,0:T(8,128)S(1)} collective-permute-done((f32[384,1024]{1,0:T(8,128)S(1)}, f32[384,1024]{1,0:T(8,128)S(1)}, u32[]{:S(2)}, u32[]{:S(2)}) %collective-permute-start.5) | collective-permute-done | bytes 1572896 | tf_op jit(solution)/shard_map/ppermute | solution.py:39
  65.7 2.4 %collective-permute-start.6 = (f32[4,1024]{1,0:T(4,128)S(1)}, f32[4,1024]{1,0:T(4,128)S(1)}, u32[]{:S(2)}, u32[]{:S(2)}) collective-permute-start(f32[4,1024]{1,0:T(4,128)S(1)} %pad_maximum_fusion.5), channel_id=1, source_target_pairs={{0,64},{2,66},{4,68},{6,70},{8,72},{10,74},{12,76},{14,78},{16,80}... | collective-permute-start | bytes 49160 | tf_op jit(solution)/shard_map/ppermute | solution.py:39
  68.1 5.0 %collective-permute-done.6 = f32[4,1024]{1,0:T(4,128)S(1)} collective-permute-done((f32[4,1024]{1,0:T(4,128)S(1)}, f32[4,1024]{1,0:T(4,128)S(1)}, u32[]{:S(2)}, u32[]{:S(2)}) %collective-permute-start.6) | collective-permute-done | bytes 16416 | tf_op jit(solution)/shard_map/ppermute | solution.py:39
  75.8 3.9 %collective-permute-start.8 = (f32[2,1024]{1,0:T(2,128)S(1)}, f32[2,1024]{1,0:T(2,128)S(1)}, u32[]{:S(2)}, u32[]{:S(2)}) collective-permute-start(f32[2,1024]{1,0:T(2,128)S(1)} %get-tuple-element.103), channel_id=1, source_target_pairs={{0,2},{2,4},{4,6},{6,8},{8,10},{10,12},{12,14},{14,16},{16,18},{18... | collective-permute-start | bytes 24584 | tf_op jit(solution)/shard_map/ppermute | solution.py:39
  79.7 4.7 %collective-permute-done.7 = f32[2,1024]{1,0:T(2,128)S(1)} collective-permute-done((f32[2,1024]{1,0:T(2,128)S(1)}, f32[2,1024]{1,0:T(2,128)S(1)}, u32[]{:S(2)}, u32[]{:S(2)}) %collective-permute-start.7) | collective-permute-done | bytes 8224 | tf_op jit(solution)/shard_map/ppermute | solution.py:39
  85.9 3.6 %weighted_sums.3 = (f32[2,1,1024]{2,1,0:T(1,128)S(1)}, f32[2,1,1024]{2,1,0:T(1,128)S(1)}) custom-call(s32[3]{0:T(128)S(1)} %add_convert_fusion.sc_ref, f32[2,1,1024,1024]{3,2,1,0:T(8,128)} %held_ref.13, f32[2,1,1024]{2,1,0:T(1,128)S(1)} %copy.35.a_ref, f32[2,1,1024]{2,1,0:T(1,128)S(1)} %copy.36.b_ref), custom_call_target="tpu_custom_call" | custom-call | flops 8388608 | bytes 8388608 | tf_op jit(solution)/shard_map/weighted_sums/pallas_call | solution.py:161
  91.3 12.8 %collective-permute-start.12 = (f32[8,1024]{1,0:T(8,128)S(1)}, f32[8,1024]{1,0:T(8,128)S(1)}, u32[]{:S(2)}, u32[]{:S(2)}) collective-permute-start(f32[8,1024]{1,0:T(8,128)S(1)} %concatenate.79), channel_id=1, source_target_pairs={{0,64},{2,66},{4,68},{6,70},{8,72},{10,74},{12,76},{14,78},{16,80}... | collective-permute-start | bytes 98312 | tf_op jit(solution)/shard_map/ppermute | solution.py:39
  104.1 2.3 %collective-permute-done.12 = f32[8,1024]{1,0:T(8,128)S(1)} collective-permute-done((f32[8,1024]{1,0:T(8,128)S(1)}, f32[8,1024]{1,0:T(8,128)S(1)}, u32[]{:S(2)}, u32[]{:S(2)}) %collective-permute-start.12) | collective-permute-done | bytes 32800 | tf_op jit(solution)/shard_map/ppermute | solution.py:39
  107.7 4.5 %collective-permute-start.14 = (f32[1,1024]{1,0:T(1,128)S(1)}, f32[1,1024]{1,0:T(1,128)S(1)}, u32[]{:S(2)}, u32[]{:S(2)}) collective-permute-start(f32[1,1024]{1,0:T(1,128)S(1)} %get-tuple-element.71), channel_id=1, source_target_pairs={{0,2},{2,4},{4,6},{6,8},{8,10},{10,12},{12,14},{14,16},{16,18},{18... | collective-permute-start | bytes 12296 | tf_op jit(solution)/shard_map/ppermute | solution.py:39
  112.3 3.9 %collective-permute-start.13 = (f32[1,384]{1,0:T(1,128)S(1)}, f32[1,384]{1,0:T(1,128)S(1)}, u32[]{:S(2)}, u32[]{:S(2)}) collective-permute-start(f32[1,384]{1,0:T(1,128)S(1)} %bitcast.70), channel_id=1, source_target_pairs={{0,32},{2,34},{4,36},{6,38},{8,40},{10,42},{12,44},{14,46},{16,48}... | collective-permute-start | bytes 4616 | tf_op jit(solution)/shard_map/ppermute | solution.py:39
  117.8 5.8 %collective-permute-start.17 = (f32[512,1024]{1,0:T(8,128)}, f32[512,1024]{1,0:T(8,128)S(1)}, u32[]{:S(2)}, u32[]{:S(2)}) collective-permute-start(f32[512,1024]{1,0:T(8,128)} %copy-done.2), channel_id=1, source_target_pairs={{0,64},{2,66},{4,68},{6,70},{8,72},{10,74},{12,76},{14,78},{16,80}... | collective-permute-start | bytes 6291464 | tf_op jit(solution)/shard_map/ppermute | solution.py:39
  124.2 3.5 %all-to-all-start = ((f32[16,1,384]{2,1,0:T(1,128)}), f32[16,1,384]{2,1,0:T(1,128)S(1)}, u32[]{:S(2)}, u32[]{:S(2)}) async-start(f32[16,1,384]{2,1,0:T(1,128)} %broadcast_in_dim.25), calls=%async_computation | async-start | bytes 49152 | tf_op jit(solution)/shard_map/all_to_all | solution.py:46
  127.7 4.3 %collective-permute-start.18 = (f32[128,1024]{1,0:T(8,128)}, f32[128,1024]{1,0:T(8,128)S(1)}, u32[]{:S(2)}, u32[]{:S(2)}) collective-permute-start(f32[128,1024]{1,0:T(8,128)} %copy-done.3), channel_id=1, source_target_pairs={{0,64},{2,66},{4,68},{6,70},{8,72},{10,74},{12,76},{14,78},{16,80}... | collective-permute-start | bytes 1572872 | tf_op jit(solution)/shard_map/ppermute | solution.py:39
  132.0 3.3 %all-to-all-done = f32[16,1,384]{2,1,0:T(1,128)S(1)} async-done(((f32[16,1,384]{2,1,0:T(1,128)}), f32[16,1,384]{2,1,0:T(1,128)S(1)}, u32[]{:S(2)}, u32[]{:S(2)}) %all-to-all-start) | async-done | bytes 24608 | tf_op jit(solution)/shard_map/all_to_all | solution.py:46
  142.0 2.5 %balance_ahead.1.rest_0_ = f32[2,1,1024,1024]{3,2,1,0:T(8,128)} custom-call(s32[3]{0:T(128)S(1)} %add_convert_fusion.sc_ref, f32[2,1,1024,1024]{3,2,1,0:T(8,128)} %collective-permute-done.got_ref, f32[2,1,1024,1024]{3,2,1,0:T(8,128)} %held_ref.13, f32[384,1024]{1,0:T(8,128)S(1)} %copy-done.1, f32[8,1,128]{2,1,0:T(1,128)S(1)} %bitcast.57, ...), custom_call_target="tpu_custom_call" | custom-call | flops 1572864 | bytes 6291456 | tf_op jit(solution)/shard_map/balance_ahead/pallas_call | solution.py:261
  144.6 3.2 %collective-permute-done.17.pk_ref = f32[512,1024]{1,0:T(8,128)S(1)} collective-permute-done((f32[512,1024]{1,0:T(8,128)}, f32[512,1024]{1,0:T(8,128)S(1)}, u32[]{:S(2)}, u32[]{:S(2)}) %collective-permute-start.17) | collective-permute-done | bytes 2097184 | tf_op jit(solution)/shard_map/ppermute | solution.py:39
  147.8 1.9 %balance_most.1.rest_0_ = f32[2,1,1024,1024]{3,2,1,0:T(8,128)} custom-call(s32[3]{0:T(128)S(1)} %add_convert_fusion.sc_ref, f32[2,1,1024,1024]{3,2,1,0:T(8,128)} %collective-permute-done.got_ref, f32[2,1,1024,1024]{3,2,1,0:T(8,128)} %held_ref.13, f32[512,1024]{1,0:T(8,128)S(1)} %collective-permute-done.17.pk_ref, ...), custom_call_target="tpu_custom_call", output_to_operand_aliasing={{}: (7, {})} | custom-call | flops 524288 | bytes 2097152 | tf_op jit(solution)/shard_map/balance_most/pallas_call | solution.py:261
  149.7 2.5 %balance_rest.1.rest_0_ = f32[2,1,1024,1024]{3,2,1,0:T(8,128)} custom-call(s32[3]{0:T(128)S(1)} %add_convert_fusion.sc_ref, f32[2,1,1024,1024]{3,2,1,0:T(8,128)} %collective-permute-done.got_ref, f32[2,1,1024,1024]{3,2,1,0:T(8,128)} %held_ref.13, f32[512,1024]{1,0:T(8,128)S(1)} %collective-permute-done.17.pk_ref, ...), custom_call_target="tpu_custom_call", output_to_operand_aliasing={{}: (7, {})} | custom-call | flops 1572864 | bytes 6291456 | tf_op jit(solution)/shard_map/balance_rest/pallas_call | solution.py:261
  (88 shorter events, 24.3 us)
Async XLA Ops:
  0.6 26.8 %copy-start.5 = (s32[2]{0:T(128)S(1)}, s32[2]{0:T(128)}, u32[]{:S(2)}) copy-start(s32[2]{0:T(128)} %param.5) | copy-start | bytes 28
  0.6 140.0 %collective-permute-start = (f32[2,1,1024,1024]{3,2,1,0:T(8,128)}, f32[2,1,1024,1024]{3,2,1,0:T(8,128)}, u32[]{:S(2)}, u32[]{:S(2)}) collective-permute-start(f32[2,1,1024,1024]{3,2,1,0:T(8,128)} %held_ref.13), channel_id=1, source_target_pairs={{1,65},{3,67},{5,69},{7,71},{9,73},{11,75},{13,77},{15,79},{17,81}... | collective-permute-start | bytes 25165832 | tf_op jit(solution)/shard_map/ppermute | solution.py:39
  5.3 5.5 %collective-permute-start.1 = (f32[1,1024]{1,0:T(1,128)S(1)}, f32[1,1024]{1,0:T(1,128)S(1)}, u32[]{:S(2)}, u32[]{:S(2)}) collective-permute-start(f32[1,1024]{1,0:T(1,128)S(1)} %bitcast.69), channel_id=1, source_target_pairs={{2,0},{4,2},{6,4},{8,6},{10,8},{12,10},{14,12},{16,14},{18,16},{20... | collective-permute-start | bytes 12296 | tf_op jit(solution)/shard_map/ppermute | solution.py:39
  10.8 14.2 %collective-permute-start.2 = (f32[3,1024]{1,0:T(4,128)S(1)}, f32[3,1024]{1,0:T(4,128)S(1)}, u32[]{:S(2)}, u32[]{:S(2)}) collective-permute-start(f32[3,1024]{1,0:T(4,128)S(1)} %pad_maximum_fusion.2), channel_id=1, source_target_pairs={{0,64},{2,66},{4,68},{6,70},{8,72},{10,74},{12,76},{14,78},{16,80}... | collective-permute-start | bytes 36872 | tf_op jit(solution)/shard_map/ppermute | solution.py:39
  25.0 40.7 %collective-permute-start.5 = (f32[384,1024]{1,0:T(8,128)S(1)}, f32[384,1024]{1,0:T(8,128)S(1)}, u32[]{:S(2)}, u32[]{:S(2)}) collective-permute-start(f32[384,1024]{1,0:T(8,128)S(1)} %get-tuple-element.36), channel_id=1, source_target_pairs={{0,64},{2,66},{4,68},{6,70},{8,72},{10,74},{12,76},{14,78},{16,80}... | collective-permute-start | bytes 4718600 | tf_op jit(solution)/shard_map/ppermute | solution.py:39
  28.7 1.3 collective-permute-start.3
  30.0 108.7 %copy-start.4 = (f32[2048]{0:T(1024)S(1)}, f32[2048]{0:T(1024)}, u32[]{:S(2)}) copy-start(f32[2048]{0:T(1024)} %param.7) | copy-start | bytes 24580
  33.7 1.7 %collective-permute-start.4 = (f32[4,1024]{1,0:T(4,128)S(1)}, f32[4,1024]{1,0:T(4,128)S(1)}, u32[]{:S(2)}, u32[]{:S(2)}) collective-permute-start(f32[4,1024]{1,0:T(4,128)S(1)} %pad_maximum_fusion.4), channel_id=1, source_target_pairs={{0,1},{2,3},{4,5},{6,7},{8,9},{10,11},{12,13},{14,15},{16,17},{18,... | collective-permute-start | bytes 49160 | tf_op jit(solution)/shard_map/ppermute | solution.py:53
  65.7 52.1 %copy-start = (f32[384,1024]{1,0:T(8,128)}, f32[384,1024]{1,0:T(8,128)S(1)}, u32[]{:S(2)}) copy-start(f32[384,1024]{1,0:T(8,128)S(1)} %collective-permute-done.5.pk_ref) | copy-start | bytes 4718596
  65.7 7.4 %collective-permute-start.6 = (f32[4,1024]{1,0:T(4,128)S(1)}, f32[4,1024]{1,0:T(4,128)S(1)}, u32[]{:S(2)}, u32[]{:S(2)}) collective-permute-start(f32[4,1024]{1,0:T(4,128)S(1)} %pad_maximum_fusion.5), channel_id=1, source_target_pairs={{0,64},{2,66},{4,68},{6,70},{8,72},{10,74},{12,76},{14,78},{16,80}... | collective-permute-start | bytes 49160 | tf_op jit(solution)/shard_map/ppermute | solution.py:39
  73.2 6.5 %collective-permute-start.9 = (f32[2,1024]{1,0:T(2,128)S(1)}, f32[2,1024]{1,0:T(2,128)S(1)}, u32[]{:S(2)}, u32[]{:S(2)}) collective-permute-start(f32[2,1024]{1,0:T(2,128)S(1)} %get-tuple-element.101), channel_id=1, source_target_pairs={{2,0},{4,2},{6,4},{8,6},{10,8},{12,10},{14,12},{16,14},{18,16},{20... | collective-permute-start | bytes 24584 | tf_op jit(solution)/shard_map/ppermute | solution.py:39
  74.5 9.9 %collective-permute-start.7 = (f32[2,1024]{1,0:T(2,128)S(1)}, f32[2,1024]{1,0:T(2,128)S(1)}, u32[]{:S(2)}, u32[]{:S(2)}) collective-permute-start(f32[2,1024]{1,0:T(2,128)S(1)} %get-tuple-element.102), channel_id=1, source_target_pairs={{62,0},{64,126}} | collective-permute-start | bytes 24584 | tf_op jit(solution)/shard_map/ppermute | solution.py:39
  75.8 8.6 %collective-permute-start.8 = (f32[2,1024]{1,0:T(2,128)S(1)}, f32[2,1024]{1,0:T(2,128)S(1)}, u32[]{:S(2)}, u32[]{:S(2)}) collective-permute-start(f32[2,1024]{1,0:T(2,128)S(1)} %get-tuple-element.103), channel_id=1, source_target_pairs={{0,2},{2,4},{4,6},{6,8},{8,10},{10,12},{12,14},{14,16},{16,18},{18... | collective-permute-start | bytes 24584 | tf_op jit(solution)/shard_map/ppermute | solution.py:39
  84.5 1.3 collective-permute-start.10
  89.5 1.7 %collective-permute-start.11 = (f32[4,1024]{1,0:T(4,128)S(1)}, f32[4,1024]{1,0:T(4,128)S(1)}, u32[]{:S(2)}, u32[]{:S(2)}) collective-permute-start(f32[4,1024]{1,0:T(4,128)S(1)} %pad_maximum_fusion.7), channel_id=1, source_target_pairs={{0,1},{2,3},{4,5},{6,7},{8,9},{10,11},{12,13},{14,15},{16,17},{18,... | collective-permute-start | bytes 49160 | tf_op jit(solution)/shard_map/ppermute | solution.py:53
  91.3 15.1 %collective-permute-start.12 = (f32[8,1024]{1,0:T(8,128)S(1)}, f32[8,1024]{1,0:T(8,128)S(1)}, u32[]{:S(2)}, u32[]{:S(2)}) collective-permute-start(f32[8,1024]{1,0:T(8,128)S(1)} %concatenate.79), channel_id=1, source_target_pairs={{0,64},{2,66},{4,68},{6,70},{8,72},{10,74},{12,76},{14,78},{16,80}... | collective-permute-start | bytes 98312 | tf_op jit(solution)/shard_map/ppermute | solution.py:39
  106.4 11.4 %collective-permute-start.15 = (f32[1,1024]{1,0:T(1,128)S(1)}, f32[1,1024]{1,0:T(1,128)S(1)}, u32[]{:S(2)}, u32[]{:S(2)}) collective-permute-start(f32[1,1024]{1,0:T(1,128)S(1)} %get-tuple-element.70), channel_id=1, source_target_pairs={{2,0},{4,2},{6,4},{8,6},{10,8},{12,10},{14,12},{16,14},{18,16},{20... | collective-permute-start | bytes 12296 | tf_op jit(solution)/shard_map/ppermute | solution.py:39
  107.7 10.1 %collective-permute-start.14 = (f32[1,1024]{1,0:T(1,128)S(1)}, f32[1,1024]{1,0:T(1,128)S(1)}, u32[]{:S(2)}, u32[]{:S(2)}) collective-permute-start(f32[1,1024]{1,0:T(1,128)S(1)} %get-tuple-element.71), channel_id=1, source_target_pairs={{0,2},{2,4},{4,6},{6,8},{8,10},{10,12},{12,14},{14,16},{16,18},{18... | collective-permute-start | bytes 12296 | tf_op jit(solution)/shard_map/ppermute | solution.py:39
  112.3 5.5 %collective-permute-start.13 = (f32[1,384]{1,0:T(1,128)S(1)}, f32[1,384]{1,0:T(1,128)S(1)}, u32[]{:S(2)}, u32[]{:S(2)}) collective-permute-start(f32[1,384]{1,0:T(1,128)S(1)} %bitcast.70), channel_id=1, source_target_pairs={{0,32},{2,34},{4,36},{6,38},{8,40},{10,42},{12,44},{14,46},{16,48}... | collective-permute-start | bytes 4616 | tf_op jit(solution)/shard_map/ppermute | solution.py:39
  117.8 30.0 %collective-permute-start.17 = (f32[512,1024]{1,0:T(8,128)}, f32[512,1024]{1,0:T(8,128)S(1)}, u32[]{:S(2)}, u32[]{:S(2)}) collective-permute-start(f32[512,1024]{1,0:T(8,128)} %copy-done.2), channel_id=1, source_target_pairs={{0,64},{2,66},{4,68},{6,70},{8,72},{10,74},{12,76},{14,78},{16,80}... | collective-permute-start | bytes 6291464 | tf_op jit(solution)/shard_map/ppermute | solution.py:39
  124.2 11.0 %all-to-all-start = ((f32[16,1,384]{2,1,0:T(1,128)}), f32[16,1,384]{2,1,0:T(1,128)S(1)}, u32[]{:S(2)}, u32[]{:S(2)}) async-start(f32[16,1,384]{2,1,0:T(1,128)} %broadcast_in_dim.25), calls=%async_computation | async-start | bytes 49152 | tf_op jit(solution)/shard_map/all_to_all | solution.py:46
  127.7 25.7 %collective-permute-start.18 = (f32[128,1024]{1,0:T(8,128)}, f32[128,1024]{1,0:T(8,128)S(1)}, u32[]{:S(2)}, u32[]{:S(2)}) collective-permute-start(f32[128,1024]{1,0:T(8,128)} %copy-done.3), channel_id=1, source_target_pairs={{0,64},{2,66},{4,68},{6,70},{8,72},{10,74},{12,76},{14,78},{16,80}... | collective-permute-start | bytes 1572872 | tf_op jit(solution)/shard_map/ppermute | solution.py:39
  138.7 1.3 collective-permute-start.16
  140.6 1.4 copy-start.1
  (2 other events, 2.2 us)

commit v4 on v3

--- a/solution.py
+++ b/solution.py
@@ -62,7 +62,7 @@
 
 
 BLOCKS = [(0, 0), (0, 1), (0, 2), (0, 3), (1, 1), (1, 2), (1, 3), (1, 0)]
-SENT = (3, 4, 1)
+SENT = (2, 5, 1)
 
 
 def pack_kernel(held_ref, *refs):
@@ -365,10 +365,10 @@
     wc = jnp.where(on_diagonal, result[:2], result[1:3]).reshape(2, 1, 1024)
 
     got, ahead, wr, wc, dv = lax.optimization_barrier((got, ahead, wr, wc, dv))
-    out = balance("balance_ahead", 0, (0, 1, 2), scalars, got, held_tiles, ahead, dv, wr, wc)
+    out = balance("balance_ahead", 0, (0, 1), scalars, got, held_tiles, ahead, dv, wr, wc)
     out, most = lax.optimization_barrier((out, most))
-    out = balance("balance_most", 0, (3,), scalars, got, held_tiles, most, dv, wr, wc, into=out)
-    out = balance("balance_rest", 1, (1, 2, 3), scalars, got, held_tiles, most, dv, wr, wc, into=out, base=1)
+    out = balance("balance_most", 0, (2, 3), scalars, got, held_tiles, most, dv, wr, wc, into=out)
+    out = balance("balance_rest", 1, (1, 2, 3), scalars, got, held_tiles, most, dv, wr, wc, into=out, base=2)
     out, last = lax.optimization_barrier((out, last))
     out = balance("balance_last", 1, (0,), scalars, got, held_tiles, last, dv, wr, wc, into=out)
     return out, bias_out.reshape(2048)

time: 156 us -> 154 us (0.987)
  waiting for transfers between devices: 60.7 us -> 57.4 us
    ppermute x14, waiting for transfers between devices: 52.4 us -> 49.1 us  [move(): return lambda value: lax.ppermute(value, AXES, pairs)]
    unnamed x17 -> x15, local copies, waits for them, and re-layouts: 4.21 us -> 4.38 us
  transfers between devices with their start and end apart: 20 -> 20, of which waited for: 14 -> 14; matrix products, arithmetic and copies ran while one was open for 3% -> 4% of each run, Pallas kernels for 11% -> 11%
where the time goes in v4:
time: 154 us; the launch traced here: 153 us
  starting transfers between devices  62.8 us (41%)
  waiting for transfers between devices  57.4 us (37%)
  Pallas kernels  18.7 us (12%)
  local copies, waits for them, and re-layouts  7.1 us (5%)
  between operations  4.47 us (3%)
  other arithmetic  2.09 us (1%)
    ppermute x14, starting transfers between devices, move(): return lambda value: lax.ppermute(value, AXES, pairs)  57.4 us
    ppermute x14, waiting for transfers between devices, move(): return lambda value: lax.ppermute(value, AXES, pairs)  49.1 us
    pallas_call x4, Pallas kernels, balance(): pl.pallas_call(functools.partial(balance_kernel, t, ks, base), in_specs=i...  8.69 us
    pallas_call x2, Pallas kernels, weighted_sums(): pl.pallas_call(sums_kernel, in_specs=[pl.BlockSpec(memory_space=pltpu.SME...  7.23 us
    ppermute x5, waiting for transfers between devices, moves(): lax.ppermute(value, AXES, both_ways)  5.11 us
    unnamed x15, local copies, waits for them, and re-layouts  4.38 us
    all_to_all x1, starting transfers between devices, plane_sum(): lax.all_to_all(spread, 'bins', 0, 0, axis_index_groups=planes, tiled=True)  3.5 us
    all_to_all x1, waiting for transfers between devices, plane_sum(): lax.all_to_all(spread, 'bins', 0, 0, axis_index_groups=planes, tiled=True)  3.2 us
  transfers between devices with their start and end apart: 20, of which 14 were waited for; matrix products, arithmetic and copies ran while one was open for 4% of the time, Pallas kernels for 11%

profile of v4, /device:TPU:0, one launch (start us, length us, event | category | flops | bytes accessed | tf_op | source)
XLA Modules:
  0.0 152.5 jit_solution(15784213132610940242)
XLA Ops:
  0.6 3.9 %collective-permute-start = (f32[2,1,1024,1024]{3,2,1,0:T(8,128)}, f32[2,1,1024,1024]{3,2,1,0:T(8,128)}, u32[]{:S(2)}, u32[]{:S(2)}) collective-permute-start(f32[2,1,1024,1024]{3,2,1,0:T(8,128)} %held_ref.13), channel_id=1, source_target_pairs={{1,65},{3,67},{5,69},{7,71},{9,73},{11,75},{13,77},{15,79},{17,81}... | collective-permute-start | bytes 25165832 | tf_op jit(solution)/shard_map/ppermute | solution.py:39
  6.6 4.2 %collective-permute-done.1 = f32[1,1024]{1,0:T(1,128)S(1)} collective-permute-done((f32[1,1024]{1,0:T(1,128)S(1)}, f32[1,1024]{1,0:T(1,128)S(1)}, u32[]{:S(2)}, u32[]{:S(2)}) %collective-permute-start.1) | collective-permute-done | bytes 4128 | tf_op jit(solution)/shard_map/ppermute | solution.py:39
  10.8 9.2 %collective-permute-start.2 = (f32[3,1024]{1,0:T(4,128)S(1)}, f32[3,1024]{1,0:T(4,128)S(1)}, u32[]{:S(2)}, u32[]{:S(2)}) collective-permute-start(f32[3,1024]{1,0:T(4,128)S(1)} %pad_maximum_fusion.2), channel_id=1, source_target_pairs={{0,64},{2,66},{4,68},{6,70},{8,72},{10,74},{12,76},{14,78},{16,80}... | collective-permute-start | bytes 36872 | tf_op jit(solution)/shard_map/ppermute | solution.py:39
  22.5 2.8 %pack_triangles.1 = (f32[256,1024]{1,0:T(8,128)S(1)}, f32[640,1024]{1,0:T(8,128)S(1)}, f32[128,1024]{1,0:T(8,128)S(1)}, f32[8,1,128]{2,1,0:T(1,128)S(1)}) custom-call(f32[2,1,1024,1024]{3,2,1,0:T(8,128)} %held_ref.13), custom_call_target="tpu_custom_call" | custom-call | flops 1048576 | bytes 8388608 | tf_op jit(solution)/shard_map/pack_triangles/pallas_call | solution.py:103
  26.9 1.9 %collective-permute-start.5 = (f32[256,1024]{1,0:T(8,128)S(1)}, f32[256,1024]{1,0:T(8,128)S(1)}, u32[]{:S(2)}, u32[]{:S(2)}) collective-permute-start(f32[256,1024]{1,0:T(8,128)S(1)} %get-tuple-element.36), channel_id=1, source_target_pairs={{0,64},{2,66},{4,68},{6,70},{8,72},{10,74},{12,76},{14,78},{16,80}... | collective-permute-start | bytes 3145736 | tf_op jit(solution)/shard_map/ppermute | solution.py:39
  30.2 3.6 %weighted_sums.2 = (f32[2,1,1024]{2,1,0:T(1,128)S(1)}, f32[2,1,1024]{2,1,0:T(1,128)S(1)}) custom-call(s32[3]{0:T(128)S(1)} %add_convert_fusion.sc_ref, f32[2,1,1024,1024]{3,2,1,0:T(8,128)} %held_ref.13, f32[2,1,1024]{2,1,0:T(1,128)S(1)} %copy.33.a_ref, f32[2,1,1024]{2,1,0:T(1,128)S(1)} %copy.34.b_ref), custom_call_target="tpu_custom_call" | custom-call | flops 8388608 | bytes 8388608 | tf_op jit(solution)/shard_map/weighted_sums/pallas_call | solution.py:161
  35.6 20.8 %collective-permute-done.5.pk_ref = f32[256,1024]{1,0:T(8,128)S(1)} collective-permute-done((f32[256,1024]{1,0:T(8,128)S(1)}, f32[256,1024]{1,0:T(8,128)S(1)}, u32[]{:S(2)}, u32[]{:S(2)}) %collective-permute-start.5) | collective-permute-done | bytes 1048608 | tf_op jit(solution)/shard_map/ppermute | solution.py:39
  57.4 1.9 %collective-permute-start.6 = (f32[4,1024]{1,0:T(4,128)S(1)}, f32[4,1024]{1,0:T(4,128)S(1)}, u32[]{:S(2)}, u32[]{:S(2)}) collective-permute-start(f32[4,1024]{1,0:T(4,128)S(1)} %pad_maximum_fusion.5), channel_id=1, source_target_pairs={{0,64},{2,66},{4,68},{6,70},{8,72},{10,74},{12,76},{14,78},{16,80}... | collective-permute-start | bytes 49160 | tf_op jit(solution)/shard_map/ppermute | solution.py:39
  59.3 5.4 %collective-permute-done.6 = f32[4,1024]{1,0:T(4,128)S(1)} collective-permute-done((f32[4,1024]{1,0:T(4,128)S(1)}, f32[4,1024]{1,0:T(4,128)S(1)}, u32[]{:S(2)}, u32[]{:S(2)}) %collective-permute-start.6) | collective-permute-done | bytes 16416 | tf_op jit(solution)/shard_map/ppermute | solution.py:39
  67.4 3.9 %collective-permute-start.8 = (f32[2,1024]{1,0:T(2,128)S(1)}, f32[2,1024]{1,0:T(2,128)S(1)}, u32[]{:S(2)}, u32[]{:S(2)}) collective-permute-start(f32[2,1024]{1,0:T(2,128)S(1)} %get-tuple-element.103), channel_id=1, source_target_pairs={{0,2},{2,4},{4,6},{6,8},{8,10},{10,12},{12,14},{14,16},{16,18},{18... | collective-permute-start | bytes 24584 | tf_op jit(solution)/shard_map/ppermute | solution.py:39
  71.4 4.7 %collective-permute-done.7 = f32[2,1024]{1,0:T(2,128)S(1)} collective-permute-done((f32[2,1024]{1,0:T(2,128)S(1)}, f32[2,1024]{1,0:T(2,128)S(1)}, u32[]{:S(2)}, u32[]{:S(2)}) %collective-permute-start.7) | collective-permute-done | bytes 8224 | tf_op jit(solution)/shard_map/ppermute | solution.py:39
  77.5 3.6 %weighted_sums.3 = (f32[2,1,1024]{2,1,0:T(1,128)S(1)}, f32[2,1,1024]{2,1,0:T(1,128)S(1)}) custom-call(s32[3]{0:T(128)S(1)} %add_convert_fusion.sc_ref, f32[2,1,1024,1024]{3,2,1,0:T(8,128)} %held_ref.13, f32[2,1,1024]{2,1,0:T(1,128)S(1)} %copy.35.a_ref, f32[2,1,1024]{2,1,0:T(1,128)S(1)} %copy.36.b_ref), custom_call_target="tpu_custom_call" | custom-call | flops 8388608 | bytes 8388608 | tf_op jit(solution)/shard_map/weighted_sums/pallas_call | solution.py:161
  82.9 12.8 %collective-permute-start.12 = (f32[8,1024]{1,0:T(8,128)S(1)}, f32[8,1024]{1,0:T(8,128)S(1)}, u32[]{:S(2)}, u32[]{:S(2)}) collective-permute-start(f32[8,1024]{1,0:T(8,128)S(1)} %concatenate.79), channel_id=1, source_target_pairs={{0,64},{2,66},{4,68},{6,70},{8,72},{10,74},{12,76},{14,78},{16,80}... | collective-permute-start | bytes 98312 | tf_op jit(solution)/shard_map/ppermute | solution.py:39
  95.7 2.3 %collective-permute-done.12 = f32[8,1024]{1,0:T(8,128)S(1)} collective-permute-done((f32[8,1024]{1,0:T(8,128)S(1)}, f32[8,1024]{1,0:T(8,128)S(1)}, u32[]{:S(2)}, u32[]{:S(2)}) %collective-permute-start.12) | collective-permute-done | bytes 32800 | tf_op jit(solution)/shard_map/ppermute | solution.py:39
  99.3 4.5 %collective-permute-start.14 = (f32[1,1024]{1,0:T(1,128)S(1)}, f32[1,1024]{1,0:T(1,128)S(1)}, u32[]{:S(2)}, u32[]{:S(2)}) collective-permute-start(f32[1,1024]{1,0:T(1,128)S(1)} %get-tuple-element.71), channel_id=1, source_target_pairs={{0,2},{2,4},{4,6},{6,8},{8,10},{10,12},{12,14},{14,16},{16,18},{18... | collective-permute-start | bytes 12296 | tf_op jit(solution)/shard_map/ppermute | solution.py:39
  104.0 3.9 %collective-permute-start.13 = (f32[1,384]{1,0:T(1,128)S(1)}, f32[1,384]{1,0:T(1,128)S(1)}, u32[]{:S(2)}, u32[]{:S(2)}) collective-permute-start(f32[1,384]{1,0:T(1,128)S(1)} %bitcast.70), channel_id=1, source_target_pairs={{0,32},{2,34},{4,36},{6,38},{8,40},{10,42},{12,44},{14,46},{16,48}... | collective-permute-start | bytes 4616 | tf_op jit(solution)/shard_map/ppermute | solution.py:39
  109.4 5.8 %collective-permute-start.17 = (f32[640,1024]{1,0:T(8,128)}, f32[640,1024]{1,0:T(8,128)S(1)}, u32[]{:S(2)}, u32[]{:S(2)}) collective-permute-start(f32[640,1024]{1,0:T(8,128)} %copy-done.2), channel_id=1, source_target_pairs={{0,64},{2,66},{4,68},{6,70},{8,72},{10,74},{12,76},{14,78},{16,80}... | collective-permute-start | bytes 7864328 | tf_op jit(solution)/shard_map/ppermute | solution.py:39
  115.9 3.5 %all-to-all-start = ((f32[16,1,384]{2,1,0:T(1,128)}), f32[16,1,384]{2,1,0:T(1,128)S(1)}, u32[]{:S(2)}, u32[]{:S(2)}) async-start(f32[16,1,384]{2,1,0:T(1,128)} %broadcast_in_dim.25), calls=%async_computation | async-start | bytes 49152 | tf_op jit(solution)/shard_map/all_to_all | solution.py:46
  119.4 4.3 %collective-permute-start.18 = (f32[128,1024]{1,0:T(8,128)}, f32[128,1024]{1,0:T(8,128)S(1)}, u32[]{:S(2)}, u32[]{:S(2)}) collective-permute-start(f32[128,1024]{1,0:T(8,128)} %copy-done.3), channel_id=1, source_target_pairs={{0,64},{2,66},{4,68},{6,70},{8,72},{10,74},{12,76},{14,78},{16,80}... | collective-permute-start | bytes 1572872 | tf_op jit(solution)/shard_map/ppermute | solution.py:39
  123.7 3.2 %all-to-all-done = f32[16,1,384]{2,1,0:T(1,128)S(1)} async-done(((f32[16,1,384]{2,1,0:T(1,128)}), f32[16,1,384]{2,1,0:T(1,128)S(1)}, u32[]{:S(2)}, u32[]{:S(2)}) %all-to-all-start) | async-done | bytes 24608 | tf_op jit(solution)/shard_map/all_to_all | solution.py:46
  133.6 2.1 %balance_ahead.1.rest_0_ = f32[2,1,1024,1024]{3,2,1,0:T(8,128)} custom-call(s32[3]{0:T(128)S(1)} %add_convert_fusion.sc_ref, f32[2,1,1024,1024]{3,2,1,0:T(8,128)} %collective-permute-done.got_ref, f32[2,1,1024,1024]{3,2,1,0:T(8,128)} %held_ref.13, f32[256,1024]{1,0:T(8,128)S(1)} %copy-done.1, f32[8,1,128]{2,1,0:T(1,128)S(1)} %bitcast.57, ...), custom_call_target="tpu_custom_call" | custom-call | flops 1048576 | bytes 4194304 | tf_op jit(solution)/shard_map/balance_ahead/pallas_call | solution.py:261
  135.7 9.3 %collective-permute-done.17.pk_ref = f32[640,1024]{1,0:T(8,128)S(1)} collective-permute-done((f32[640,1024]{1,0:T(8,128)}, f32[640,1024]{1,0:T(8,128)S(1)}, u32[]{:S(2)}, u32[]{:S(2)}) %collective-permute-start.17) | collective-permute-done | bytes 2621472 | tf_op jit(solution)/shard_map/ppermute | solution.py:39
  145.1 2.3 %balance_most.1.rest_0_ = f32[2,1,1024,1024]{3,2,1,0:T(8,128)} custom-call(s32[3]{0:T(128)S(1)} %add_convert_fusion.sc_ref, f32[2,1,1024,1024]{3,2,1,0:T(8,128)} %collective-permute-done.got_ref, f32[2,1,1024,1024]{3,2,1,0:T(8,128)} %held_ref.13, f32[640,1024]{1,0:T(8,128)S(1)} %collective-permute-done.17.pk_ref, ...), custom_call_target="tpu_custom_call", output_to_operand_aliasing={{}: (7, {})} | custom-call | flops 1048576 | bytes 4194304 | tf_op jit(solution)/shard_map/balance_most/pallas_call | solution.py:261
  147.4 2.5 %balance_rest.1.rest_0_ = f32[2,1,1024,1024]{3,2,1,0:T(8,128)} custom-call(s32[3]{0:T(128)S(1)} %add_convert_fusion.sc_ref, f32[2,1,1024,1024]{3,2,1,0:T(8,128)} %collective-permute-done.got_ref, f32[2,1,1024,1024]{3,2,1,0:T(8,128)} %held_ref.13, f32[640,1024]{1,0:T(8,128)S(1)} %collective-permute-done.17.pk_ref, ...), custom_call_target="tpu_custom_call", output_to_operand_aliasing={{}: (7, {})} | custom-call | flops 1572864 | bytes 6291456 | tf_op jit(solution)/shard_map/balance_rest/pallas_call | solution.py:261
  (86 shorter events, 25.4 us)
Async XLA Ops:
  0.6 131.7 %collective-permute-start = (f32[2,1,1024,1024]{3,2,1,0:T(8,128)}, f32[2,1,1024,1024]{3,2,1,0:T(8,128)}, u32[]{:S(2)}, u32[]{:S(2)}) collective-permute-start(f32[2,1,1024,1024]{3,2,1,0:T(8,128)} %held_ref.13), channel_id=1, source_target_pairs={{1,65},{3,67},{5,69},{7,71},{9,73},{11,75},{13,77},{15,79},{17,81}... | collective-permute-start | bytes 25165832 | tf_op jit(solution)/shard_map/ppermute | solution.py:39
  5.3 5.5 %collective-permute-start.1 = (f32[1,1024]{1,0:T(1,128)S(1)}, f32[1,1024]{1,0:T(1,128)S(1)}, u32[]{:S(2)}, u32[]{:S(2)}) collective-permute-start(f32[1,1024]{1,0:T(1,128)S(1)} %bitcast.69), channel_id=1, source_target_pairs={{2,0},{4,2},{6,4},{8,6},{10,8},{12,10},{14,12},{16,14},{18,16},{20... | collective-permute-start | bytes 12296 | tf_op jit(solution)/shard_map/ppermute | solution.py:39
  10.8 16.1 %collective-permute-start.2 = (f32[3,1024]{1,0:T(4,128)S(1)}, f32[3,1024]{1,0:T(4,128)S(1)}, u32[]{:S(2)}, u32[]{:S(2)}) collective-permute-start(f32[3,1024]{1,0:T(4,128)S(1)} %pad_maximum_fusion.2), channel_id=1, source_target_pairs={{0,64},{2,66},{4,68},{6,70},{8,72},{10,74},{12,76},{14,78},{16,80}... | collective-permute-start | bytes 36872 | tf_op jit(solution)/shard_map/ppermute | solution.py:39
  25.3 1.6 %copy-start.2 = (f32[640,1024]{1,0:T(8,128)}, f32[640,1024]{1,0:T(8,128)S(1)}, u32[]{:S(2)}) copy-start(f32[640,1024]{1,0:T(8,128)S(1)} %get-tuple-element.56) | copy-start | bytes 7864324
  26.9 29.5 %copy-start.3 = (f32[128,1024]{1,0:T(8,128)}, f32[128,1024]{1,0:T(8,128)S(1)}, u32[]{:S(2)}) copy-start(f32[128,1024]{1,0:T(8,128)S(1)} %get-tuple-element.59) | copy-start | bytes 1572868
  26.9 29.5 %collective-permute-start.5 = (f32[256,1024]{1,0:T(8,128)S(1)}, f32[256,1024]{1,0:T(8,128)S(1)}, u32[]{:S(2)}, u32[]{:S(2)}) collective-permute-start(f32[256,1024]{1,0:T(8,128)S(1)} %get-tuple-element.36), channel_id=1, source_target_pairs={{0,64},{2,66},{4,68},{6,70},{8,72},{10,74},{12,76},{14,78},{16,80}... | collective-permute-start | bytes 3145736 | tf_op jit(solution)/shard_map/ppermute | solution.py:39
  28.9 1.3 collective-permute-start.3
  30.2 100.3 %copy-start.4 = (f32[2048]{0:T(1024)S(1)}, f32[2048]{0:T(1024)}, u32[]{:S(2)}) copy-start(f32[2048]{0:T(1024)} %param.7) | copy-start | bytes 24580
  33.9 1.7 %collective-permute-start.4 = (f32[4,1024]{1,0:T(4,128)S(1)}, f32[4,1024]{1,0:T(4,128)S(1)}, u32[]{:S(2)}, u32[]{:S(2)}) collective-permute-start(f32[4,1024]{1,0:T(4,128)S(1)} %pad_maximum_fusion.4), channel_id=1, source_target_pairs={{0,1},{2,3},{4,5},{6,7},{8,9},{10,11},{12,13},{14,15},{16,17},{18,... | collective-permute-start | bytes 49160 | tf_op jit(solution)/shard_map/ppermute | solution.py:53
  57.4 7.4 %collective-permute-start.6 = (f32[4,1024]{1,0:T(4,128)S(1)}, f32[4,1024]{1,0:T(4,128)S(1)}, u32[]{:S(2)}, u32[]{:S(2)}) collective-permute-start(f32[4,1024]{1,0:T(4,128)S(1)} %pad_maximum_fusion.5), channel_id=1, source_target_pairs={{0,64},{2,66},{4,68},{6,70},{8,72},{10,74},{12,76},{14,78},{16,80}... | collective-permute-start | bytes 49160 | tf_op jit(solution)/shard_map/ppermute | solution.py:39
  64.8 6.5 %collective-permute-start.9 = (f32[2,1024]{1,0:T(2,128)S(1)}, f32[2,1024]{1,0:T(2,128)S(1)}, u32[]{:S(2)}, u32[]{:S(2)}) collective-permute-start(f32[2,1024]{1,0:T(2,128)S(1)} %get-tuple-element.101), channel_id=1, source_target_pairs={{2,0},{4,2},{6,4},{8,6},{10,8},{12,10},{14,12},{16,14},{18,16},{20... | collective-permute-start | bytes 24584 | tf_op jit(solution)/shard_map/ppermute | solution.py:39
  66.1 9.9 %collective-permute-start.7 = (f32[2,1024]{1,0:T(2,128)S(1)}, f32[2,1024]{1,0:T(2,128)S(1)}, u32[]{:S(2)}, u32[]{:S(2)}) collective-permute-start(f32[2,1024]{1,0:T(2,128)S(1)} %get-tuple-element.102), channel_id=1, source_target_pairs={{62,0},{64,126}} | collective-permute-start | bytes 24584 | tf_op jit(solution)/shard_map/ppermute | solution.py:39
  67.4 8.6 %collective-permute-start.8 = (f32[2,1024]{1,0:T(2,128)S(1)}, f32[2,1024]{1,0:T(2,128)S(1)}, u32[]{:S(2)}, u32[]{:S(2)}) collective-permute-start(f32[2,1024]{1,0:T(2,128)S(1)} %get-tuple-element.103), channel_id=1, source_target_pairs={{0,2},{2,4},{4,6},{6,8},{8,10},{10,12},{12,14},{14,16},{16,18},{18... | collective-permute-start | bytes 24584 | tf_op jit(solution)/shard_map/ppermute | solution.py:39
  76.2 1.3 collective-permute-start.10
  81.2 1.7 %collective-permute-start.11 = (f32[4,1024]{1,0:T(4,128)S(1)}, f32[4,1024]{1,0:T(4,128)S(1)}, u32[]{:S(2)}, u32[]{:S(2)}) collective-permute-start(f32[4,1024]{1,0:T(4,128)S(1)} %pad_maximum_fusion.7), channel_id=1, source_target_pairs={{0,1},{2,3},{4,5},{6,7},{8,9},{10,11},{12,13},{14,15},{16,17},{18,... | collective-permute-start | bytes 49160 | tf_op jit(solution)/shard_map/ppermute | solution.py:53
  82.9 15.1 %collective-permute-start.12 = (f32[8,1024]{1,0:T(8,128)S(1)}, f32[8,1024]{1,0:T(8,128)S(1)}, u32[]{:S(2)}, u32[]{:S(2)}) collective-permute-start(f32[8,1024]{1,0:T(8,128)S(1)} %concatenate.79), channel_id=1, source_target_pairs={{0,64},{2,66},{4,68},{6,70},{8,72},{10,74},{12,76},{14,78},{16,80}... | collective-permute-start | bytes 98312 | tf_op jit(solution)/shard_map/ppermute | solution.py:39
  98.0 11.4 %collective-permute-start.15 = (f32[1,1024]{1,0:T(1,128)S(1)}, f32[1,1024]{1,0:T(1,128)S(1)}, u32[]{:S(2)}, u32[]{:S(2)}) collective-permute-start(f32[1,1024]{1,0:T(1,128)S(1)} %get-tuple-element.70), channel_id=1, source_target_pairs={{2,0},{4,2},{6,4},{8,6},{10,8},{12,10},{14,12},{16,14},{18,16},{20... | collective-permute-start | bytes 12296 | tf_op jit(solution)/shard_map/ppermute | solution.py:39
  99.3 10.1 %collective-permute-start.14 = (f32[1,1024]{1,0:T(1,128)S(1)}, f32[1,1024]{1,0:T(1,128)S(1)}, u32[]{:S(2)}, u32[]{:S(2)}) collective-permute-start(f32[1,1024]{1,0:T(1,128)S(1)} %get-tuple-element.71), channel_id=1, source_target_pairs={{0,2},{2,4},{4,6},{6,8},{8,10},{10,12},{12,14},{14,16},{16,18},{18... | collective-permute-start | bytes 12296 | tf_op jit(solution)/shard_map/ppermute | solution.py:39
  104.0 5.5 %collective-permute-start.13 = (f32[1,384]{1,0:T(1,128)S(1)}, f32[1,384]{1,0:T(1,128)S(1)}, u32[]{:S(2)}, u32[]{:S(2)}) collective-permute-start(f32[1,384]{1,0:T(1,128)S(1)} %bitcast.70), channel_id=1, source_target_pairs={{0,32},{2,34},{4,36},{6,38},{8,40},{10,42},{12,44},{14,46},{16,48}... | collective-permute-start | bytes 4616 | tf_op jit(solution)/shard_map/ppermute | solution.py:39
  109.4 35.6 %collective-permute-start.17 = (f32[640,1024]{1,0:T(8,128)}, f32[640,1024]{1,0:T(8,128)S(1)}, u32[]{:S(2)}, u32[]{:S(2)}) collective-permute-start(f32[640,1024]{1,0:T(8,128)} %copy-done.2), channel_id=1, source_target_pairs={{0,64},{2,66},{4,68},{6,70},{8,72},{10,74},{12,76},{14,78},{16,80}... | collective-permute-start | bytes 7864328 | tf_op jit(solution)/shard_map/ppermute | solution.py:39
  115.9 11.1 %all-to-all-start = ((f32[16,1,384]{2,1,0:T(1,128)}), f32[16,1,384]{2,1,0:T(1,128)S(1)}, u32[]{:S(2)}, u32[]{:S(2)}) async-start(f32[16,1,384]{2,1,0:T(1,128)} %broadcast_in_dim.25), calls=%async_computation | async-start | bytes 49152 | tf_op jit(solution)/shard_map/all_to_all | solution.py:46
  119.4 31.3 %collective-permute-start.18 = (f32[128,1024]{1,0:T(8,128)}, f32[128,1024]{1,0:T(8,128)S(1)}, u32[]{:S(2)}, u32[]{:S(2)}) collective-permute-start(f32[128,1024]{1,0:T(8,128)} %copy-done.3), channel_id=1, source_target_pairs={{0,64},{2,66},{4,68},{6,70},{8,72},{10,74},{12,76},{14,78},{16,80}... | collective-permute-start | bytes 1572872 | tf_op jit(solution)/shard_map/ppermute | solution.py:39
  130.4 1.3 collective-permute-start.16
  132.4 1.2 copy-start.1
  (1 other events, 1.0 us)

commit v5 on v4

--- a/solution.py
+++ b/solution.py
@@ -62,7 +62,7 @@
 
 
 BLOCKS = [(0, 0), (0, 1), (0, 2), (0, 3), (1, 1), (1, 2), (1, 3), (1, 0)]
-SENT = (2, 5, 1)
+SENT = (1, 6, 1)
 
 
 def pack_kernel(held_ref, *refs):
@@ -365,10 +365,10 @@
     wc = jnp.where(on_diagonal, result[:2], result[1:3]).reshape(2, 1, 1024)
 
     got, ahead, wr, wc, dv = lax.optimization_barrier((got, ahead, wr, wc, dv))
-    out = balance("balance_ahead", 0, (0, 1), scalars, got, held_tiles, ahead, dv, wr, wc)
+    out = balance("balance_ahead", 0, (0,), scalars, got, held_tiles, ahead, dv, wr, wc)
     out, most = lax.optimization_barrier((out, most))
-    out = balance("balance_most", 0, (2, 3), scalars, got, held_tiles, most, dv, wr, wc, into=out)
-    out = balance("balance_rest", 1, (1, 2, 3), scalars, got, held_tiles, most, dv, wr, wc, into=out, base=2)
+    out = balance("balance_most", 0, (1, 2, 3), scalars, got, held_tiles, most, dv, wr, wc, into=out)
+    out = balance("balance_rest", 1, (1, 2, 3), scalars, got, held_tiles, most, dv, wr, wc, into=out, base=3)
     out, last = lax.optimization_barrier((out, last))
     out = balance("balance_last", 1, (0,), scalars, got, held_tiles, last, dv, wr, wc, into=out)
     return out, bias_out.reshape(2048)

time: 154 us -> 152 us (0.987)
  the two profiles are of different devices: /device:TPU:0 before, /device:TPU:122 now
where the time goes in v5:
time: 152 us; the launch traced here: 151 us
  starting transfers between devices  62.4 us (41%)
  waiting for transfers between devices  54.8 us (36%)
  Pallas kernels  20.6 us (14%)
  local copies, waits for them, and re-layouts  6.81 us (4%)
  between operations  4.59 us (3%)
  other arithmetic  2.1 us (1%)
    ppermute x14, starting transfers between devices, move(): return lambda value: lax.ppermute(value, AXES, pairs)  54.6 us
    ppermute x14, waiting for transfers between devices, move(): return lambda value: lax.ppermute(value, AXES, pairs)  50.5 us
    pallas_call x4, Pallas kernels, balance(): pl.pallas_call(functools.partial(balance_kernel, t, ks, base), in_specs=i...  10.6 us
    pallas_call x2, Pallas kernels, weighted_sums(): pl.pallas_call(sums_kernel, in_specs=[pl.BlockSpec(memory_space=pltpu.SME...  7.23 us
    all_to_all x1, starting transfers between devices, plane_sum(): lax.all_to_all(spread, 'bins', 0, 0, axis_index_groups=planes, tiled=True)  6.64 us
    ppermute x5, waiting for transfers between devices, moves(): lax.ppermute(value, AXES, both_ways)  4.35 us
    unnamed x15, local copies, waits for them, and re-layouts  4.11 us
  transfers between devices with their start and end apart: 20, of which 12 were waited for; matrix products, arithmetic and copies ran while one was open for 4% of the time, Pallas kernels for 12%

profile of v5, /device:TPU:122, one launch (start us, length us, event | category | flops | bytes accessed | tf_op | source)
XLA Modules:
  0.0 151.4 jit_solution(14632815971610938788)
XLA Ops:
  0.6 3.9 %collective-permute-start = (f32[2,1,1024,1024]{3,2,1,0:T(8,128)}, f32[2,1,1024,1024]{3,2,1,0:T(8,128)}, u32[]{:S(2)}, u32[]{:S(2)}) collective-permute-start(f32[2,1,1024,1024]{3,2,1,0:T(8,128)} %held_ref.13), channel_id=1, source_target_pairs={{1,65},{3,67},{5,69},{7,71},{9,73},{11,75},{13,77},{15,79},{17,81}... | collective-permute-start | bytes 25165832 | tf_op jit(solution)/shard_map/ppermute | solution.py:39
  5.3 2.3 %collective-permute-start.1 = (f32[1,1024]{1,0:T(1,128)S(1)}, f32[1,1024]{1,0:T(1,128)S(1)}, u32[]{:S(2)}, u32[]{:S(2)}) collective-permute-start(f32[1,1024]{1,0:T(1,128)S(1)} %bitcast.69), channel_id=1, source_target_pairs={{2,0},{4,2},{6,4},{8,6},{10,8},{12,10},{14,12},{16,14},{18,16},{20... | collective-permute-start | bytes 12296 | tf_op jit(solution)/shard_map/ppermute | solution.py:39
  7.6 7.8 %collective-permute-done.1 = f32[1,1024]{1,0:T(1,128)S(1)} collective-permute-done((f32[1,1024]{1,0:T(1,128)S(1)}, f32[1,1024]{1,0:T(1,128)S(1)}, u32[]{:S(2)}, u32[]{:S(2)}) %collective-permute-start.1) | collective-permute-done | bytes 4128 | tf_op jit(solution)/shard_map/ppermute | solution.py:39
  19.9 2.8 %pack_triangles.1 = (f32[128,1024]{1,0:T(8,128)S(1)}, f32[768,1024]{1,0:T(8,128)S(1)}, f32[128,1024]{1,0:T(8,128)S(1)}, f32[8,1,128]{2,1,0:T(1,128)S(1)}) custom-call(f32[2,1,1024,1024]{3,2,1,0:T(8,128)} %held_ref.13), custom_call_target="tpu_custom_call" | custom-call | flops 1048576 | bytes 8388608 | tf_op jit(solution)/shard_map/pack_triangles/pallas_call | solution.py:103
  24.6 5.4 %collective-permute-start.5 = (f32[128,1024]{1,0:T(8,128)S(1)}, f32[128,1024]{1,0:T(8,128)S(1)}, u32[]{:S(2)}, u32[]{:S(2)}) collective-permute-start(f32[128,1024]{1,0:T(8,128)S(1)} %get-tuple-element.36), channel_id=1, source_target_pairs={{0,64},{2,66},{4,68},{6,70},{8,72},{10,74},{12,76},{14,78},{16,80}... | collective-permute-start | bytes 1572872 | tf_op jit(solution)/shard_map/ppermute | solution.py:39
  30.1 3.6 %weighted_sums.2 = (f32[2,1,1024]{2,1,0:T(1,128)S(1)}, f32[2,1,1024]{2,1,0:T(1,128)S(1)}) custom-call(s32[3]{0:T(128)S(1)} %add_convert_fusion.sc_ref, f32[2,1,1024,1024]{3,2,1,0:T(8,128)} %held_ref.13, f32[2,1,1024]{2,1,0:T(1,128)S(1)} %copy.33.a_ref, f32[2,1,1024]{2,1,0:T(1,128)S(1)} %copy.34.b_ref), custom_call_target="tpu_custom_call" | custom-call | flops 8388608 | bytes 8388608 | tf_op jit(solution)/shard_map/weighted_sums/pallas_call | solution.py:161
  35.0 7.8 %collective-permute-done.5.pk_ref = f32[128,1024]{1,0:T(8,128)S(1)} collective-permute-done((f32[128,1024]{1,0:T(8,128)S(1)}, f32[128,1024]{1,0:T(8,128)S(1)}, u32[]{:S(2)}, u32[]{:S(2)}) %collective-permute-start.5) | collective-permute-done | bytes 524320 | tf_op jit(solution)/shard_map/ppermute | solution.py:39
  43.6 5.4 %collective-permute-start.6 = (f32[4,1024]{1,0:T(4,128)S(1)}, f32[4,1024]{1,0:T(4,128)S(1)}, u32[]{:S(2)}, u32[]{:S(2)}) collective-permute-start(f32[4,1024]{1,0:T(4,128)S(1)} %pad_maximum_fusion.5), channel_id=1, source_target_pairs={{0,64},{2,66},{4,68},{6,70},{8,72},{10,74},{12,76},{14,78},{16,80}... | collective-permute-start | bytes 49160 | tf_op jit(solution)/shard_map/ppermute | solution.py:39
  49.1 1.9 %collective-permute-done.6 = f32[4,1024]{1,0:T(4,128)S(1)} collective-permute-done((f32[4,1024]{1,0:T(4,128)S(1)}, f32[4,1024]{1,0:T(4,128)S(1)}, u32[]{:S(2)}, u32[]{:S(2)}) %collective-permute-start.6) | collective-permute-done | bytes 16416 | tf_op jit(solution)/shard_map/ppermute | solution.py:39
  53.0 2.7 %collective-permute-start.7 = (f32[2,1024]{1,0:T(2,128)S(1)}, f32[2,1024]{1,0:T(2,128)S(1)}, u32[]{:S(2)}, u32[]{:S(2)}) collective-permute-start(f32[2,1024]{1,0:T(2,128)S(1)} %get-tuple-element.102), channel_id=1, source_target_pairs={{62,0},{64,126}} | collective-permute-start | bytes 24584 | tf_op jit(solution)/shard_map/ppermute | solution.py:39
  55.7 8.8 %collective-permute-start.8 = (f32[2,1024]{1,0:T(2,128)S(1)}, f32[2,1024]{1,0:T(2,128)S(1)}, u32[]{:S(2)}, u32[]{:S(2)}) collective-permute-start(f32[2,1024]{1,0:T(2,128)S(1)} %get-tuple-element.103), channel_id=1, source_target_pairs={{0,2},{2,4},{4,6},{6,8},{8,10},{10,12},{12,14},{14,16},{16,18},{18... | collective-permute-start | bytes 24584 | tf_op jit(solution)/shard_map/ppermute | solution.py:39
  67.3 3.6 %weighted_sums.3 = (f32[2,1,1024]{2,1,0:T(1,128)S(1)}, f32[2,1,1024]{2,1,0:T(1,128)S(1)}) custom-call(s32[3]{0:T(128)S(1)} %add_convert_fusion.sc_ref, f32[2,1,1024,1024]{3,2,1,0:T(8,128)} %held_ref.13, f32[2,1,1024]{2,1,0:T(1,128)S(1)} %copy.35.a_ref, f32[2,1,1024]{2,1,0:T(1,128)S(1)} %copy.36.b_ref), custom_call_target="tpu_custom_call" | custom-call | flops 8388608 | bytes 8388608 | tf_op jit(solution)/shard_map/weighted_sums/pallas_call | solution.py:161
  74.7 5.8 %collective-permute-done.12 = f32[8,1024]{1,0:T(8,128)S(1)} collective-permute-done((f32[8,1024]{1,0:T(8,128)S(1)}, f32[8,1024]{1,0:T(8,128)S(1)}, u32[]{:S(2)}, u32[]{:S(2)}) %collective-permute-start.12) | collective-permute-done | bytes 32800 | tf_op jit(solution)/shard_map/ppermute | solution.py:39
  80.5 1.9 %collective-permute-start.15 = (f32[1,1024]{1,0:T(1,128)S(1)}, f32[1,1024]{1,0:T(1,128)S(1)}, u32[]{:S(2)}, u32[]{:S(2)}) collective-permute-start(f32[1,1024]{1,0:T(1,128)S(1)} %get-tuple-element.70), channel_id=1, source_target_pairs={{2,0},{4,2},{6,4},{8,6},{10,8},{12,10},{14,12},{16,14},{18,16},{20... | collective-permute-start | bytes 12296 | tf_op jit(solution)/shard_map/ppermute | solution.py:39
  82.4 8.6 %collective-permute-start.14 = (f32[1,1024]{1,0:T(1,128)S(1)}, f32[1,1024]{1,0:T(1,128)S(1)}, u32[]{:S(2)}, u32[]{:S(2)}) collective-permute-start(f32[1,1024]{1,0:T(1,128)S(1)} %get-tuple-element.71), channel_id=1, source_target_pairs={{0,2},{2,4},{4,6},{6,8},{8,10},{10,12},{12,14},{14,16},{16,18},{18... | collective-permute-start | bytes 12296 | tf_op jit(solution)/shard_map/ppermute | solution.py:39
  91.0 2.5 %collective-permute-start.13 = (f32[1,384]{1,0:T(1,128)S(1)}, f32[1,384]{1,0:T(1,128)S(1)}, u32[]{:S(2)}, u32[]{:S(2)}) collective-permute-start(f32[1,384]{1,0:T(1,128)S(1)} %bitcast.70), channel_id=1, source_target_pairs={{0,32},{2,34},{4,36},{6,38},{8,40},{10,42},{12,44},{14,46},{16,48}... | collective-permute-start | bytes 4616 | tf_op jit(solution)/shard_map/ppermute | solution.py:39
  93.5 3.1 %collective-permute-done.13 = f32[1,384]{1,0:T(1,128)S(1)} collective-permute-done((f32[1,384]{1,0:T(1,128)S(1)}, f32[1,384]{1,0:T(1,128)S(1)}, u32[]{:S(2)}, u32[]{:S(2)}) %collective-permute-start.13) | collective-permute-done | bytes 1568 | tf_op jit(solution)/shard_map/ppermute | solution.py:39
  96.6 4.8 %collective-permute-done.15 = f32[1,1024]{1,0:T(1,128)S(1)} collective-permute-done((f32[1,1024]{1,0:T(1,128)S(1)}, f32[1,1024]{1,0:T(1,128)S(1)}, u32[]{:S(2)}, u32[]{:S(2)}) %collective-permute-start.15) | collective-permute-done | bytes 4128 | tf_op jit(solution)/shard_map/ppermute | solution.py:39
  104.0 6.6 %all-to-all-start = ((f32[16,1,384]{2,1,0:T(1,128)}), f32[16,1,384]{2,1,0:T(1,128)S(1)}, u32[]{:S(2)}, u32[]{:S(2)}) async-start(f32[16,1,384]{2,1,0:T(1,128)} %broadcast_in_dim.25), calls=%async_computation | async-start | bytes 49152 | tf_op jit(solution)/shard_map/all_to_all | solution.py:46
  110.6 5.4 %collective-permute-start.18 = (f32[128,1024]{1,0:T(8,128)}, f32[128,1024]{1,0:T(8,128)}, u32[]{:S(2)}, u32[]{:S(2)}) collective-permute-start(f32[128,1024]{1,0:T(8,128)} %copy-done.3), channel_id=1, source_target_pairs={{0,64},{2,66},{4,68},{6,70},{8,72},{10,74},{12,76},{14,78},{16,80}... | collective-permute-start | bytes 1572872 | tf_op jit(solution)/shard_map/ppermute | solution.py:39
  124.3 17.9 %collective-permute-done.17.pk_ref = f32[768,1024]{1,0:T(8,128)S(1)} collective-permute-done((f32[768,1024]{1,0:T(8,128)}, f32[768,1024]{1,0:T(8,128)S(1)}, u32[]{:S(2)}, u32[]{:S(2)}) %collective-permute-start.17) | collective-permute-done | bytes 3145760 | tf_op jit(solution)/shard_map/ppermute | solution.py:39
  142.3 2.7 %balance_most.1.rest_0_ = f32[2,1,1024,1024]{3,2,1,0:T(8,128)} custom-call(s32[3]{0:T(128)S(1)} %add_convert_fusion.sc_ref, f32[2,1,1024,1024]{3,2,1,0:T(8,128)} %collective-permute-done.got_ref, f32[2,1,1024,1024]{3,2,1,0:T(8,128)} %held_ref.13, f32[768,1024]{1,0:T(8,128)S(1)} %collective-permute-done.17.pk_ref, ...), custom_call_target="tpu_custom_call", output_to_operand_aliasing={{}: (7, {})} | custom-call | flops 1572864 | bytes 6291456 | tf_op jit(solution)/shard_map/balance_most/pallas_call | solution.py:261
  145.0 3.5 %balance_rest.1.rest_0_ = f32[2,1,1024,1024]{3,2,1,0:T(8,128)} custom-call(s32[3]{0:T(128)S(1)} %add_convert_fusion.sc_ref, f32[2,1,1024,1024]{3,2,1,0:T(8,128)} %collective-permute-done.got_ref, f32[2,1,1024,1024]{3,2,1,0:T(8,128)} %held_ref.13, f32[768,1024]{1,0:T(8,128)S(1)} %collective-permute-done.17.pk_ref, ...), custom_call_target="tpu_custom_call", output_to_operand_aliasing={{}: (7, {})} | custom-call | flops 1572864 | bytes 6291456 | tf_op jit(solution)/shard_map/balance_rest/pallas_call | solution.py:261
  148.5 2.7 %balance_last.1 = f32[2,1,1024,1024]{3,2,1,0:T(8,128)} custom-call(s32[3]{0:T(128)S(1)} %add_convert_fusion.sc_ref, f32[2,1,1024,1024]{3,2,1,0:T(8,128)} %collective-permute-done.got_ref, f32[2,1,1024,1024]{3,2,1,0:T(8,128)} %held_ref.13, f32[128,1024]{1,0:T(8,128)} %collective-permute-done.18.pk_ref, ...), custom_call_target="tpu_custom_call", output_to_operand_aliasing={{}: (7, {})} | custom-call | flops 524288 | bytes 2097152 | tf_op jit(solution)/shard_map/balance_last/pallas_call | solution.py:261
  (86 shorter events, 25.1 us)
Async XLA Ops:
  0.6 120.9 %collective-permute-start = (f32[2,1,1024,1024]{3,2,1,0:T(8,128)}, f32[2,1,1024,1024]{3,2,1,0:T(8,128)}, u32[]{:S(2)}, u32[]{:S(2)}) collective-permute-start(f32[2,1,1024,1024]{3,2,1,0:T(8,128)} %held_ref.13), channel_id=1, source_target_pairs={{1,65},{3,67},{5,69},{7,71},{9,73},{11,75},{13,77},{15,79},{17,81}... | collective-permute-start | bytes 25165832 | tf_op jit(solution)/shard_map/ppermute | solution.py:39
  5.3 10.1 %collective-permute-start.1 = (f32[1,1024]{1,0:T(1,128)S(1)}, f32[1,1024]{1,0:T(1,128)S(1)}, u32[]{:S(2)}, u32[]{:S(2)}) collective-permute-start(f32[1,1024]{1,0:T(1,128)S(1)} %bitcast.69), channel_id=1, source_target_pairs={{2,0},{4,2},{6,4},{8,6},{10,8},{12,10},{14,12},{16,14},{18,16},{20... | collective-permute-start | bytes 12296 | tf_op jit(solution)/shard_map/ppermute | solution.py:39
  15.4 8.9 %collective-permute-start.2 = (f32[3,1024]{1,0:T(4,128)S(1)}, f32[3,1024]{1,0:T(4,128)S(1)}, u32[]{:S(2)}, u32[]{:S(2)}) collective-permute-start(f32[3,1024]{1,0:T(4,128)S(1)} %pad_maximum_fusion.2), channel_id=1, source_target_pairs={{0,64},{2,66},{4,68},{6,70},{8,72},{10,74},{12,76},{14,78},{16,80}... | collective-permute-start | bytes 36872 | tf_op jit(solution)/shard_map/ppermute | solution.py:39
  22.7 1.6 %copy-start.2 = (f32[768,1024]{1,0:T(8,128)}, f32[768,1024]{1,0:T(8,128)S(1)}, u32[]{:S(2)}) copy-start(f32[768,1024]{1,0:T(8,128)S(1)} %get-tuple-element.56) | copy-start | bytes 9437188
  24.3 18.5 %copy-start.3 = (f32[128,1024]{1,0:T(8,128)}, f32[128,1024]{1,0:T(8,128)S(1)}, u32[]{:S(2)}) copy-start(f32[128,1024]{1,0:T(8,128)S(1)} %get-tuple-element.59) | copy-start | bytes 1572868
  24.4 5.6 %collective-permute-start.3 = (f32[4,1024]{1,0:T(4,128)S(1)}, f32[4,1024]{1,0:T(4,128)S(1)}, u32[]{:S(2)}, u32[]{:S(2)}) collective-permute-start(f32[4,1024]{1,0:T(4,128)S(1)} %pad_maximum_fusion.3), channel_id=1, source_target_pairs={{0,1},{2,3},{4,5},{6,7},{8,9},{10,11},{12,13},{14,15},{16,17},{18,... | collective-permute-start | bytes 49160 | tf_op jit(solution)/shard_map/ppermute | solution.py:53
  24.6 18.2 %collective-permute-start.5 = (f32[128,1024]{1,0:T(8,128)S(1)}, f32[128,1024]{1,0:T(8,128)S(1)}, u32[]{:S(2)}, u32[]{:S(2)}) collective-permute-start(f32[128,1024]{1,0:T(8,128)S(1)} %get-tuple-element.36), channel_id=1, source_target_pairs={{0,64},{2,66},{4,68},{6,70},{8,72},{10,74},{12,76},{14,78},{16,80}... | collective-permute-start | bytes 1572872 | tf_op jit(solution)/shard_map/ppermute | solution.py:39
  30.1 89.6 %copy-start.4 = (f32[2048]{0:T(1024)S(1)}, f32[2048]{0:T(1024)}, u32[]{:S(2)}) copy-start(f32[2048]{0:T(1024)} %param.7) | copy-start | bytes 24580
  33.7 1.3 collective-permute-start.4
  43.6 7.4 %collective-permute-start.6 = (f32[4,1024]{1,0:T(4,128)S(1)}, f32[4,1024]{1,0:T(4,128)S(1)}, u32[]{:S(2)}, u32[]{:S(2)}) collective-permute-start(f32[4,1024]{1,0:T(4,128)S(1)} %pad_maximum_fusion.5), channel_id=1, source_target_pairs={{0,64},{2,66},{4,68},{6,70},{8,72},{10,74},{12,76},{14,78},{16,80}... | collective-permute-start | bytes 49160 | tf_op jit(solution)/shard_map/ppermute | solution.py:39
  51.1 13.4 %collective-permute-start.9 = (f32[2,1024]{1,0:T(2,128)S(1)}, f32[2,1024]{1,0:T(2,128)S(1)}, u32[]{:S(2)}, u32[]{:S(2)}) collective-permute-start(f32[2,1024]{1,0:T(2,128)S(1)} %get-tuple-element.101), channel_id=1, source_target_pairs={{2,0},{4,2},{6,4},{8,6},{10,8},{12,10},{14,12},{16,14},{18,16},{20... | collective-permute-start | bytes 24584 | tf_op jit(solution)/shard_map/ppermute | solution.py:39
  53.0 11.5 %collective-permute-start.7 = (f32[2,1024]{1,0:T(2,128)S(1)}, f32[2,1024]{1,0:T(2,128)S(1)}, u32[]{:S(2)}, u32[]{:S(2)}) collective-permute-start(f32[2,1024]{1,0:T(2,128)S(1)} %get-tuple-element.102), channel_id=1, source_target_pairs={{62,0},{64,126}} | collective-permute-start | bytes 24584 | tf_op jit(solution)/shard_map/ppermute | solution.py:39
  55.7 10.2 %collective-permute-start.8 = (f32[2,1024]{1,0:T(2,128)S(1)}, f32[2,1024]{1,0:T(2,128)S(1)}, u32[]{:S(2)}, u32[]{:S(2)}) collective-permute-start(f32[2,1024]{1,0:T(2,128)S(1)} %get-tuple-element.103), channel_id=1, source_target_pairs={{0,2},{2,4},{4,6},{6,8},{8,10},{10,12},{12,14},{14,16},{16,18},{18... | collective-permute-start | bytes 24584 | tf_op jit(solution)/shard_map/ppermute | solution.py:39
  66.0 1.3 collective-permute-start.10
  71.0 1.7 %collective-permute-start.11 = (f32[4,1024]{1,0:T(4,128)S(1)}, f32[4,1024]{1,0:T(4,128)S(1)}, u32[]{:S(2)}, u32[]{:S(2)}) collective-permute-start(f32[4,1024]{1,0:T(4,128)S(1)} %pad_maximum_fusion.7), channel_id=1, source_target_pairs={{0,1},{2,3},{4,5},{6,7},{8,9},{10,11},{12,13},{14,15},{16,17},{18,... | collective-permute-start | bytes 49160 | tf_op jit(solution)/shard_map/ppermute | solution.py:53
  72.7 7.7 %collective-permute-start.12 = (f32[8,1024]{1,0:T(8,128)S(1)}, f32[8,1024]{1,0:T(8,128)S(1)}, u32[]{:S(2)}, u32[]{:S(2)}) collective-permute-start(f32[8,1024]{1,0:T(8,128)S(1)} %concatenate.79), channel_id=1, source_target_pairs={{0,64},{2,66},{4,68},{6,70},{8,72},{10,74},{12,76},{14,78},{16,80}... | collective-permute-start | bytes 98312 | tf_op jit(solution)/shard_map/ppermute | solution.py:39
  80.5 20.9 %collective-permute-start.15 = (f32[1,1024]{1,0:T(1,128)S(1)}, f32[1,1024]{1,0:T(1,128)S(1)}, u32[]{:S(2)}, u32[]{:S(2)}) collective-permute-start(f32[1,1024]{1,0:T(1,128)S(1)} %get-tuple-element.70), channel_id=1, source_target_pairs={{2,0},{4,2},{6,4},{8,6},{10,8},{12,10},{14,12},{16,14},{18,16},{20... | collective-permute-start | bytes 12296 | tf_op jit(solution)/shard_map/ppermute | solution.py:39
  82.4 19.0 %collective-permute-start.14 = (f32[1,1024]{1,0:T(1,128)S(1)}, f32[1,1024]{1,0:T(1,128)S(1)}, u32[]{:S(2)}, u32[]{:S(2)}) collective-permute-start(f32[1,1024]{1,0:T(1,128)S(1)} %get-tuple-element.71), channel_id=1, source_target_pairs={{0,2},{2,4},{4,6},{6,8},{8,10},{10,12},{12,14},{14,16},{16,18},{18... | collective-permute-start | bytes 12296 | tf_op jit(solution)/shard_map/ppermute | solution.py:39
  91.0 5.6 %collective-permute-start.13 = (f32[1,384]{1,0:T(1,128)S(1)}, f32[1,384]{1,0:T(1,128)S(1)}, u32[]{:S(2)}, u32[]{:S(2)}) collective-permute-start(f32[1,384]{1,0:T(1,128)S(1)} %bitcast.70), channel_id=1, source_target_pairs={{0,32},{2,34},{4,36},{6,38},{8,40},{10,42},{12,44},{14,46},{16,48}... | collective-permute-start | bytes 4616 | tf_op jit(solution)/shard_map/ppermute | solution.py:39
  101.4 40.9 %collective-permute-start.17 = (f32[768,1024]{1,0:T(8,128)}, f32[768,1024]{1,0:T(8,128)S(1)}, u32[]{:S(2)}, u32[]{:S(2)}) collective-permute-start(f32[768,1024]{1,0:T(8,128)} %copy-done.2), channel_id=1, source_target_pairs={{0,64},{2,66},{4,68},{6,70},{8,72},{10,74},{12,76},{14,78},{16,80}... | collective-permute-start | bytes 9437192 | tf_op jit(solution)/shard_map/ppermute | solution.py:39
  104.0 12.1 %all-to-all-start = ((f32[16,1,384]{2,1,0:T(1,128)}), f32[16,1,384]{2,1,0:T(1,128)S(1)}, u32[]{:S(2)}, u32[]{:S(2)}) async-start(f32[16,1,384]{2,1,0:T(1,128)} %broadcast_in_dim.25), calls=%async_computation | async-start | bytes 49152 | tf_op jit(solution)/shard_map/all_to_all | solution.py:46
  110.6 37.9 %collective-permute-start.18 = (f32[128,1024]{1,0:T(8,128)}, f32[128,1024]{1,0:T(8,128)}, u32[]{:S(2)}, u32[]{:S(2)}) collective-permute-start(f32[128,1024]{1,0:T(8,128)} %copy-done.3), channel_id=1, source_target_pairs={{0,64},{2,66},{4,68},{6,70},{8,72},{10,74},{12,76},{14,78},{16,80}... | collective-permute-start | bytes 1572872 | tf_op jit(solution)/shard_map/ppermute | solution.py:39
  119.6 1.3 collective-permute-start.16
  121.6 1.0 copy-start.1
  (1 other events, 0.8 us)
